TPU v7x, 32 devices: a whole 2x2x4 slice. The times are simulated.
32 devices in a mesh: parts: 2 (over y), ctx: 4 (over z), head: 2 (over x), sub: 2 (over core).
Axes of the slice: x: 2, y: 2, z: 4, core: 2. Of those that a mesh axis runs over, the one named last changes fastest.
Arguments:
- queries: bfloat16 [1024, 12288], P(('parts', 'ctx'), ('head', 'sub')), parts along dimension 0, may hold values from -250 to 250
- latent: bfloat16 [1024, 512], P(('parts', 'ctx')), parts along dimension 0, may hold values from -6 to 6
- rope_keys: bfloat16 [1024, 64], P(('parts', 'ctx')), parts along dimension 0, may hold values from -4 to 4
- latent_gain: float32 [512], replicated, may hold values from 0.1 to 1.9
- up_weight: bfloat16 [512, 16384], P(None, ('head', 'sub')), may hold values from -0.25 to 0.25
- prompt_length: int32 [2], P('parts'), parts along dimension 0, may hold values from 256 to 512
Outputs:
- attended: bfloat16 [1024, 8192], P(('parts', 'ctx'), ('head', 'sub')), parts along dimension 0
There are 2 independent parts, one for each index of `parts`. A program takes and returns all parts, laid end to end along the dimension named above; an argument that names none is the same for every part. Nothing has to cross between parts.
All inputs are finite; a program needn't handle non-finite values.
Results may differ from a plain program's by a relative error of at most 0.012.
Values may be sent and summed in bfloat16 or wider, within the bound.
No kernel may reach another device: no remote copies, remote signals or barrier semaphores. Data moves between devices by JAX's collectives and lax.ppermute only.
A program may use at most 128 MiB of HBM per device.

v0:
```python
import math

import jax
import jax.numpy as jnp
from jax import lax
from jax.sharding import PartitionSpec as P

ROPE = 64
NOPE = 128
VDIM = 128


def rotate(values, positions):
    half_width = values.shape[-1] // 2
    frequency = 10000.0 ** (-jnp.arange(half_width, dtype=jnp.float32) / half_width)
    angles = positions.astype(jnp.float32)[..., None] * frequency
    cosines = jnp.cos(angles)
    sines = jnp.sin(angles)
    lower_half = values[..., :half_width]
    upper_half = values[..., half_width:]
    return jnp.concatenate(
        [lower_half * cosines - upper_half * sines, lower_half * sines + upper_half * cosines], -1
    )


def attend(carried, keys_values, rope_piece, query_nope, query_rope, query_pos, length):
    running_max, running_sum, weighted = carried
    key_count = keys_values.shape[0]
    heads_dev = query_nope.shape[1]
    grouped = keys_values.reshape(key_count, heads_dev, NOPE + VDIM)
    scores = jnp.einsum(
        "qhd,khd->hqk", query_nope, grouped[:, :, :NOPE], preferred_element_type=jnp.float32
    )
    scores = scores + jnp.einsum(
        "qhr,kr->hqk", query_rope, rope_piece, preferred_element_type=jnp.float32
    )
    scores = scores * (1.0 / math.sqrt(NOPE + ROPE))
    key_pos = jnp.arange(key_count, dtype=jnp.int32)
    allowed = (key_pos[None, :] <= query_pos[:, None]) & (key_pos[None, :] < length)
    scores = jnp.where(allowed[None], scores, -1e30)
    new_max = jnp.maximum(running_max, jnp.max(scores, -1))
    weights = jnp.where(allowed[None], jnp.exp(scores - new_max[:, :, None]), 0.0)
    running_sum = jnp.sum(weights, -1)
    weighted = jnp.einsum(
        "hqk,khv->hqv",
        weights.astype(jnp.bfloat16),
        grouped[:, :, NOPE:],
        preferred_element_type=jnp.float32,
    )
    return (new_max, running_sum, weighted)


def per_device(queries, latent, rope_keys, latent_gain, up_weight, prompt_length):
    length = prompt_length[0]
    latent_rows = latent.shape[0]
    latent_start = lax.axis_index("ctx") * latent_rows
    latent_pos = latent_start + jnp.arange(latent_rows, dtype=jnp.int32)
    widened = latent.astype(jnp.float32)
    shard_latent = (
        widened * lax.rsqrt(jnp.mean(widened * widened, -1, keepdims=True) + 1e-06) * latent_gain
    ).astype(jnp.bfloat16)
    shard_rope = rotate(rope_keys.astype(jnp.float32), latent_pos).astype(jnp.bfloat16)
    token_rows = queries.shape[0]
    heads_dev = up_weight.shape[1] // (NOPE + VDIM)
    query_start = lax.axis_index("ctx") * token_rows
    query_pos = query_start + jnp.arange(token_rows, dtype=jnp.int32)
    grouped = queries.reshape(token_rows, heads_dev, NOPE + ROPE)
    query_nope = grouped[:, :, :NOPE]
    query_rope = rotate(grouped[:, :, NOPE:].astype(jnp.float32), query_pos[:, None]).astype(
        jnp.bfloat16
    )
    start_state = (
        jnp.full((heads_dev, token_rows), -1e30, jnp.float32),
        jnp.zeros((heads_dev, token_rows), jnp.float32),
        jnp.zeros((heads_dev, token_rows, VDIM), jnp.float32),
    )
    keys_values = jnp.dot(
        lax.all_gather(shard_latent, "ctx", axis=0, tiled=True),
        up_weight,
        preferred_element_type=jnp.float32,
    ).astype(jnp.bfloat16)
    rope_piece = lax.all_gather(shard_rope, "ctx", axis=0, tiled=True)
    running_max, running_sum, weighted = attend(
        start_state, keys_values, rope_piece, query_nope, query_rope, query_pos, length
    )
    result = weighted / running_sum[:, :, None]
    result = jnp.where(query_pos[None, :, None] < length, result, 0.0)
    return result.astype(jnp.bfloat16).transpose(1, 0, 2).reshape(token_rows, heads_dev * VDIM)


def solution(mesh):
    placed = (
        P(("parts", "ctx"), ("head", "sub")),
        P(("parts", "ctx"), None),
        P(("parts", "ctx"), None),
        P(),
        P(None, ("head", "sub")),
        P("parts"),
    )
    return jax.shard_map(
        per_device,
        mesh=mesh,
        in_specs=placed,
        out_specs=P(("parts", "ctx"), ("head", "sub")),
        check_vma=False,
    )
```

profile of v0, /device:TPU:0, one launch (start us, length us, event | category | flops | bytes accessed | tf_op | source)
XLA Modules:
  0.0 46.7 jit_solution(16228726584107372220)
XLA Ops:
  0.0 1.5 %copy.15 = bf16[128,3072]{0,1:T(8,128)(2,1)S(1)} copy(bf16[128,3072]{1,0:T(8,128)(2,1)} %param.6) | data formatting | bytes 1572864 | tf_op args[0]
  1.6 0.7 %convert_element_type.41 = f32[128,64]{0,1:T(8,128)S(1)} convert(bf16[128,64]{0,1:T(8,128)(2,1)} %param.8) | non-fusion elementwise | flops 8192 | bytes 49152 | tf_op jit(solution)/shard_map/convert_element_type | solution.py:62
  2.3 0.1 subtract_convert_fusion.1
  2.5 0.1 subtract_convert_fusion
  2.6 13.7 %all_gather.7 = bf16[512,64]{0,1:T(8,128)(2,1)S(1)} all-gather(bf16[128,64]{0,1:T(8,128)(2,1)S(1)} %pad_maximum_fusion), channel_id=1, replica_groups=mesh['parts'=2,'ctx'=4,'head'=2,'sub'=2] {'ctx'}, dimensions={0}, use_global_device_ids=true | all-gather | bytes 81920 | tf_op jit(solution)/shard_map/all_gather | solution.py:82
  16.3 1.0 %fusion.22 = f32[128]{0:T(128)S(1)} fusion(bf16[128,512]{1,0:T(8,128)(2,1)} %param.7), kind=kLoop, calls=%fused_computation.19 | loop fusion | flops 196480 | bytes 131584 | tf_op jit(solution)/shard_map/reduce_sum | solution.py:60
  17.3 1.0 %fusion.24 = bf16[128,512]{1,0:T(8,128)(2,1)S(1)} fusion(bf16[128,512]{1,0:T(8,128)(2,1)} %param.7, f32[512]{0:T(512)} %param.9, f32[128]{0:T(128)S(1)} %add_rsqrt_fusion), kind=kLoop, calls=%fused_computation.21 | loop fusion | flops 262144 | bytes 264704 | tf_op jit(solution)/shard_map/convert_element_type | solution.py:61
  18.3 15.9 %all_gather.6 = bf16[512,512]{1,0:T(8,128)(2,1)S(1)} all-gather(bf16[128,512]{1,0:T(8,128)(2,1)S(1)} %fusion.24), channel_id=1, replica_groups=mesh['parts'=2,'ctx'=4,'head'=2,'sub'=2] {'ctx'}, dimensions={0}, use_global_device_ids=true | all-gather | bytes 655360 | tf_op jit(solution)/shard_map/all_gather | solution.py:78
  34.2 4.5 %convolution_convert_fusion = bf16[512,4096]{1,0:T(8,128)(2,1)S(1)} fusion(bf16[512,512]{1,0:T(8,128)(2,1)S(1)} %all_gather.6, bf16[512,4096]{1,0:T(8,128)(2,1)} %param.10), kind=kOutput, calls=%fused_computation | convolution fusion | flops 2149580800 | bytes 8912896 | tf_op jit(solution)/shard_map/dot_general | solution.py:77
  38.7 1.4 %copy.24 = bf16[64,8,16,256]{3,2,1,0:T(8,128)(2,1)S(1)} copy(bf16[64,8,16,256]{3,1,2,0:T(8,128)(2,1)S(1)} %bitcast.28) | data formatting | bytes 8388608
  40.2 0.7 %fusion.33 = (bf16[512,16,128]{2,1,0:T(8,128)(2,1)S(1)}, bf16[512,16,128]{2,1,0:T(8,128)(2,1)S(1)}) fusion(bf16[512,16,256]{2,1,0:T(8,128)(2,1)S(1)} %bitcast.27), kind=kLoop, calls=%fused_computation.45 | loop fusion | bytes 8388608 | tf_op jit(solution)/shard_map/slice | solution.py:47
  40.9 0.7 %fusion.6 = f32[16,512,128]{2,1,0:T(8,128)S(1)} fusion(bf16[512,16,128]{2,1,0:T(8,128)(2,1)S(1)} %get-tuple-element.6, bf16[128,16,192]{0,2,1:T(8,128)(2,1)S(1)} %bitcast.30), kind=kOutput, calls=%fused_computation.8 | convolution fusion | flops 268435456 | bytes 6815744 | tf_op jit(solution)/shard_map/qhd,khd->hqk/dot_general | solution.py:31
  42.3 0.1 fusion.28
  42.4 0.9 %fusion.34 = (f32[16,128]{1,0:T(8,128)S(1)}, f32[16,128,512]{1,2,0:T(8,128)S(1)}) fusion(bf16[128,16,32]{0,2,1:T(8,128)(2,1)S(1)} %get-tuple-element.8, bf16[128,16,32]{0,2,1:T(8,128)(2,1)S(1)} %get-tuple-element.7, bf16[512,64]{0,1:T(8,128)(2,1)S(1)} %all_gather.7, f32[16,512,128]{2,1,0:T(8,128)S(1)} %fusion.6, pred[128,512]{0,1:T(8,128)(4,1)S(1)} %fusion.28), kind=kOutput, calls=%fused_computation.46 | convolution fusion | flops 138934272 | bytes 8790016 | tf_op jit(solution)/shard_map/qhr,kr->hqk/dot_general | solution.py:34
  43.4 0.7 %fusion.2 = f32[16,128]{1,0:T(8,128)S(1)} fusion(f32[16,128,512]{1,2,0:T(8,128)S(1)} %get-tuple-element.14, f32[16,128]{1,0:T(8,128)S(1)} %broadcast_maximum_fusion, pred[128,512]{0,1:T(8,128)(4,1)S(1)} %fusion.28), kind=kLoop, calls=%fused_computation.5 | loop fusion | flops 3143680 | bytes 4276224 | tf_op jit(solution)/shard_map/reduce_sum | solution.py:43
  44.1 1.6 %select_convert_fusion = bf16[128,16,128]{0,2,1:T(8,128)(2,1)S(1)} fusion(f32[16,128,512]{1,2,0:T(8,128)S(1)} %get-tuple-element.14, f32[16,128]{1,0:T(8,128)S(1)} %broadcast_maximum_fusion, pred[128,512]{0,1:T(8,128)(4,1)S(1)} %fusion.28, bf16[512,16,128]{2,1,0:T(8,128)(2,1)S(1)} %get-tuple-element.5, f32[128,16]{0,1:T(8,128)S(1)} %bitcast.32, ...), kind=kOutput, calls=%fused_computation.15 | convolution fusion | flops 272367616 | bytes 6897792 | tf_op jit(solution)/shard_map/hqk,khv->hqv/dot_general | solution.py:44
  45.7 1.0 %copy.19 = bf16[128,2048]{1,0:T(8,128)(2,1)} copy(bf16[128,2048]{0,1:T(8,128)(2,1)S(1)} %bitcast.31) | data formatting | bytes 1048576 | tf_op jit(solution)/shard_map/reshape | solution.py:88
  (9 shorter events, 0.1 us)
where the time goes:
time: 47 us; the launch traced here: 46.7 us
  blocking collectives  29.6 us (63%)
  matrix products  7.8 us (17%)
  local copies, waits for them, and re-layouts  4.64 us (10%)
  other arithmetic  3.91 us (8%)
  between operations  0.79 us (2%)
    all_gather x1, blocking collectives, per_device(): lax.all_gather(shard_latent, 'ctx', axis=0, tiled=True)  15.9 us
    all_gather x1, blocking collectives, per_device(): rope_piece = lax.all_gather(shard_rope, 'ctx', axis=0, tiled=True)  13.7 us
    dot_general x1, matrix products, per_device(): jnp.dot(lax.all_gather(shard_latent, 'ctx', axis=0, tiled=True), up_weigh...  4.53 us
    unnamed x2, local copies, waits for them, and re-layouts  2.91 us
    dot_general x1, matrix products, attend(): jnp.einsum('hqk,khv->hqv', weights.astype(jnp.bfloat16), grouped[:, :, NO...  1.62 us
    reduce_sum x1, other arithmetic, per_device(): jnp.mean(widened * widened, -1, keepdims=True) + 1e-06  1.01 us
    convert_element_type x1, other arithmetic, per_device(): shard_latent = (widened * lax.rsqrt(jnp.mean(widened * widened, -1, keepd...  1.01 us
    reshape x1, local copies, waits for them, and re-layouts, per_device(): result.astype(jnp.bfloat16).transpose(1, 0, 2)  1.01 us

commit v1 on v0

v1 whole, which is shorter than its diff:
```python
import functools
import math

import jax
import jax.numpy as jnp
import numpy as np
from jax import lax
from jax.experimental import pallas as pl
from jax.experimental.pallas import tpu as pltpu
from jax.sharding import PartitionSpec as P

ROPE = 64
NOPE = 128
VDIM = 128
WIDE = 128
FULL = 256
MASKED = -1e30
EXPONENT = math.log2(math.e) / math.sqrt(NOPE + ROPE)

VMEM = pl.BlockSpec(memory_space=pltpu.VMEM)
SMEM = pl.BlockSpec(memory_space=pltpu.SMEM)


def tables(positions):
    half = ROPE // 2
    frequency = np.float32(10000.0) ** (-np.arange(half, dtype=np.float32) / np.float32(half))
    angles = np.arange(positions, dtype=np.float32)[:, None] * frequency.astype(np.float32)
    cosines, sines = np.cos(angles), np.sin(angles)
    rows = np.concatenate([cosines, cosines, -sines, sines], 1).astype(np.float32)
    columns = np.concatenate([cosines, sines], 1).T.astype(np.float32)
    return rows, np.ascontiguousarray(columns)


def pack_kernel(latent, rope, gain, table, length, place, payload, piece):
    rows, width = latent.shape
    half = ROPE // 2
    wide = latent[...].astype(jnp.float32)
    mean = jnp.mean(wide * wide, -1, keepdims=True)
    normed = (wide * lax.rsqrt(mean + 1e-06) * gain[...]).astype(jnp.bfloat16)
    keys = rope[...].astype(jnp.float32)
    low, high = keys[:half], keys[half:]
    cosines, sines = table[:half], table[half:]
    rotated = jnp.concatenate([low * cosines - high * sines, low * sines + high * cosines], 0)
    position = place[0] * rows + lax.broadcasted_iota(jnp.int32, (WIDE - ROPE, rows), 1)
    first = lax.broadcasted_iota(jnp.int32, (WIDE - ROPE, rows), 0) == 0
    bias = jnp.where(first & (position >= length[0]), MASKED, 0.0)
    extra = jnp.concatenate([rotated, bias], 0).T.astype(jnp.bfloat16)
    payload[:, :width] = normed
    payload[:, width:] = extra
    size = piece.shape[0]
    for k in range(rows // size):

        @pl.when(place[1] == k)
        def _():
            piece[:, :width] = normed[k * size : (k + 1) * size]
            piece[:, width:] = extra[k * size : (k + 1) * size]


def own_kernel(heads, queries, payload, weight, table, expanded, full):
    rows = queries.shape[0]
    width = weight.shape[0]
    cosines = jnp.concatenate([table[:, :ROPE]] * 2, 1)
    sines = jnp.concatenate([table[:, ROPE:]] * 2, 1)
    lane = lax.broadcasted_iota(jnp.int32, (rows, 2 * ROPE), 1)
    lower = lane % ROPE < ROPE // 2
    tail = (lax.broadcasted_iota(jnp.int32, (rows, FULL - NOPE - ROPE), 1) == 0).astype(
        jnp.float32
    ).astype(jnp.bfloat16)
    each = NOPE + ROPE
    for i in range(heads // 2):
        pair = queries[:, 2 * each * i : 2 * each * (i + 1)]
        ropes = jnp.concatenate([pair[:, NOPE:each], pair[:, each + NOPE :]], 1).astype(jnp.float32)
        turned = jnp.where(
            lower, pltpu.roll(ropes, 2 * ROPE - ROPE // 2, 1), pltpu.roll(ropes, ROPE // 2, 1)
        )
        ropes = (ropes * cosines + turned * sines).astype(jnp.bfloat16)
        for e in range(2):
            at = FULL * (2 * i + e)
            full[:, at : at + NOPE] = pair[:, each * e : each * e + NOPE]
            full[:, at + NOPE : at + FULL] = jnp.concatenate(
                [ropes[:, ROPE * e : ROPE * (e + 1)], tail], 1
            )
    columns = NOPE + VDIM
    for i in range(heads // 2):
        at = slice(2 * columns * i, 2 * columns * (i + 1))
        expanded[:, at] = jnp.dot(
            payload[:, :width], weight[:, at], preferred_element_type=jnp.float32
        ).astype(jnp.bfloat16)


def attend_kernel(heads, distances, full, own, expanded, weight, *rest):
    count = len(distances)
    pieces, (length, place, out, keys, grown, scores, weights) = rest[:count], rest[count:]
    rows = full.shape[0]
    width = weight.shape[0]
    columns = NOPE + VDIM
    ctx, sub = place[0], place[1]
    keys[:rows, width:] = own[:, width:]
    spare = (lax.broadcasted_iota(jnp.int32, (1, WIDE), 1) == ROPE).astype(jnp.float32)
    spare = (spare * MASKED).astype(jnp.bfloat16)
    at = rows
    for ref, (even, odd) in zip(pieces, distances, strict=True):
        size = ref.shape[0]
        keys[at : at + size, :width] = ref[:, :width]
        there = ctx >= jnp.where(sub == 0, even, odd)
        last = ref[:, width:]
        keys[at : at + size, width:] = jnp.where(there, last, jnp.broadcast_to(spare, last.shape))
        at += size
    total = at
    row = lax.broadcasted_iota(jnp.int32, (rows, rows), 0)
    causal = lax.broadcasted_iota(jnp.int32, (rows, rows), 1) <= row
    live = ctx * rows + lax.broadcasted_iota(jnp.int32, (rows, 1), 0) < length[0]

    def grow(i):
        at = slice(2 * columns * i, 2 * columns * (i + 1))
        grown[i % 3, :rows] = expanded[:, at]
        grown[i % 3, rows:] = jnp.dot(
            keys[rows:, :width], weight[:, at], preferred_element_type=jnp.float32
        ).astype(jnp.bfloat16)

    def score(h):
        i, e = divmod(h, 2)
        nope = grown[i % 3, :, columns * e : columns * e + NOPE]
        whole = jnp.concatenate([nope, keys[:, width:]], 1)
        found = lax.dot_general(
            full[:, FULL * h : FULL * (h + 1)],
            whole,
            (((1,), (1,)), ((), ())),
            preferred_element_type=jnp.float32,
        )
        scores[h % 2, :, :rows] = jnp.where(causal, found[:, :rows], MASKED)
        scores[h % 2, :, rows:] = found[:, rows:]

    def soften(h):
        found = scores[h % 2]
        top = jnp.max(found, 1, keepdims=True)
        raw = jnp.exp2(found * EXPONENT - top * EXPONENT)
        weights[h % 2] = raw.astype(jnp.bfloat16)
        return jnp.sum(raw, 1, keepdims=True)

    def mix(h, total_h):
        i, e = divmod(h, 2)
        values = grown[i % 3, :, columns * e + NOPE : columns * (e + 1)]
        mixed = jnp.dot(weights[h % 2], values, preferred_element_type=jnp.float32)
        out[:, VDIM * h : VDIM * (h + 1)] = jnp.where(live, mixed / total_h, 0.0).astype(
            jnp.bfloat16
        )

    totals = {}
    grow(0)
    for t in range(heads + 2):
        if t % 2 == 0 and t // 2 + 1 < heads // 2:
            grow(t // 2 + 1)
        if t < heads:
            score(t)
        if 0 <= t - 1 < heads:
            totals[t - 1] = soften(t - 1)
        if 0 <= t - 2 < heads:
            mix(t - 2, totals.pop(t - 2))


def in_vmem(x):
    return pltpu.with_memory_space_constraint(x, pltpu.VMEM)


def per_device(
    ctx_size, sub_size, queries, latent, rope_keys, latent_gain, up_weight, prompt_length
):
    rows, width = latent.shape
    heads = up_weight.shape[1] // (NOPE + VDIM)
    ctx = lax.axis_index("ctx")
    sub = lax.axis_index("sub")
    place = jnp.stack([ctx, sub]).astype(jnp.int32)
    by_row, by_column = tables(ctx_size * rows)
    row_table = lax.dynamic_slice_in_dim(jnp.asarray(by_row), ctx * rows, rows, 0)
    column_table = lax.dynamic_slice_in_dim(jnp.asarray(by_column), ctx * rows, rows, 1)

    bf16 = jnp.bfloat16
    wide = width + WIDE
    payload, piece = pl.pallas_call(
        pack_kernel,
        in_specs=[VMEM] * 4 + [SMEM] * 2,
        out_specs=[VMEM] * 2,
        out_shape=[
            jax.ShapeDtypeStruct((rows, wide), bf16),
            jax.ShapeDtypeStruct((rows // sub_size, wide), bf16),
        ],
        name="pack",
    )(latent, rope_keys.T, latent_gain.reshape(1, width), column_table, prompt_length, place)

    cores = ("ctx", "sub")
    whole_sets = (ctx_size - 1) // sub_size
    direct, distances = [], []
    for d in range(whole_sets * sub_size + 1, ctx_size):
        pairs = [
            (c * sub_size + s, (c + d) * sub_size + s)
            for c in range(ctx_size - d)
            for s in range(sub_size)
        ]
        direct.append(lax.ppermute(piece, cores, pairs))
        distances.append([d] * sub_size)
    for k in range(whole_sets):
        pairs = [
            (c * sub_size + s, (c + k * sub_size + 1 + s) * sub_size + s)
            for s in range(sub_size)
            for c in range(ctx_size - (k * sub_size + 1 + s))
        ]
        direct.append(lax.ppermute(payload, cores, pairs))
        distances.append([k * sub_size + 1 + s for s in range(sub_size)])

    expanded, full = pl.pallas_call(
        functools.partial(own_kernel, heads),
        in_specs=[VMEM] * 4,
        out_specs=[VMEM] * 2,
        out_shape=[
            jax.ShapeDtypeStruct((rows, up_weight.shape[1]), bf16),
            jax.ShapeDtypeStruct((rows, heads * FULL), bf16),
        ],
        name="own",
        cost_estimate=pl.CostEstimate(
            flops=2 * rows * width * up_weight.shape[1],
            bytes_accessed=2 * (queries.size + up_weight.size + 2 * rows * up_weight.shape[1]),
            transcendentals=0,
        ),
    )(queries, payload, up_weight, row_table)

    together = jnp.concatenate(direct, 0)
    pieces, both = [together], [distances]
    arrivals = list(zip(direct, distances, strict=True))
    for r in range(1, sub_size):
        swapped = lax.ppermute(together, "sub", [(s, (s + r) % sub_size) for s in range(sub_size)])
        at = 0
        for part, dist in zip(direct, distances, strict=True):
            arrivals.append(
                (
                    swapped[at : at + part.shape[0]],
                    [dist[(s - r) % sub_size] for s in range(sub_size)],
                )
            )
            at += part.shape[0]
    parts = [a for a, _ in arrivals]
    total = rows + sum(p.shape[0] for p in parts)

    return pl.pallas_call(
        functools.partial(attend_kernel, heads, [(d[0], d[-1]) for _, d in arrivals]),
        in_specs=[VMEM] * (4 + len(parts)) + [SMEM] * 2,
        out_specs=VMEM,
        out_shape=jax.ShapeDtypeStruct((rows, heads * VDIM), bf16),
        scratch_shapes=[
            pltpu.VMEM((total, wide), bf16),
            pltpu.VMEM((3, total, 2 * (NOPE + VDIM)), bf16),
            pltpu.VMEM((2, rows, total), jnp.float32),
            pltpu.VMEM((2, rows, total), bf16),
        ],
        name="attend",
        cost_estimate=pl.CostEstimate(
            flops=2 * total * (width + 2 * rows) * up_weight.shape[1],
            bytes_accessed=2 * (up_weight.size + 3 * rows * up_weight.shape[1]),
            transcendentals=heads * rows * total,
        ),
    )(full, payload, expanded, up_weight, *parts, prompt_length, place)


def solution(mesh):
    placed = (
        P(("parts", "ctx"), ("head", "sub")),
        P(("parts", "ctx"), None),
        P(("parts", "ctx"), None),
        P(),
        P(None, ("head", "sub")),
        P("parts"),
    )
    return jax.shard_map(
        functools.partial(per_device, mesh.shape["ctx"], mesh.shape["sub"]),
        mesh=mesh,
        in_specs=placed,
        out_specs=P(("parts", "ctx"), ("head", "sub")),
        check_vma=False,
    )
```

time: 47 us -> 32.9 us (0.70)
  the two profiles are of different devices: /device:TPU:0 before, /device:TPU:17 now
where the time goes in v1:
time: 32.9 us; the launch traced here: 32.6 us
  Pallas kernels  14 us (43%)
  waiting for transfers between devices  6.82 us (21%)
  starting transfers between devices  6.33 us (19%)
  local copies, waits for them, and re-layouts  4.17 us (13%)
  between operations  0.69 us (2%)
  other arithmetic  0.62 us (2%)
    pallas_call x1, Pallas kernels, per_device(): pl.pallas_call(functools.partial(attend_kernel, heads, [(d[0], d[-1]) for...  7.45 us
    ppermute x1, waiting for transfers between devices, per_device(): direct.append(lax.ppermute(payload, cores, pairs))  6.81 us
    pallas_call x1, Pallas kernels, per_device(): pl.pallas_call(functools.partial(own_kernel, heads), in_specs=[VMEM] * 4,...  4.76 us
    ppermute x1, starting transfers between devices, per_device(): lax.ppermute(together, 'sub', [(s, (s + r) % sub_size) for s in range(sub...  4.39 us
    pallas_call x1, Pallas kernels, per_device(): pl.pallas_call(pack_kernel, in_specs=[VMEM] * 4 + [SMEM] * 2, out_specs=[...  1.78 us
    dynamic_slice x1, local copies, waits for them, and re-layouts, per_device(): lax.dynamic_slice_in_dim(jnp.asarray(by_row), ctx * rows, rows, 0)  1.47 us
    dynamic_slice x1, local copies, waits for them, and re-layouts, per_device(): lax.dynamic_slice_in_dim(jnp.asarray(by_column), ctx * rows, rows, 1)  1.37 us
    slice x2, local copies, waits for them, and re-layouts, per_device(): swapped[at:at + part.shape[0]]  1.32 us
  transfers between devices with their start and end apart: 3, of which 1 were waited for; matrix products, arithmetic and copies ran while one was open for 5% of the time, Pallas kernels for 15%

profile of v1, /device:TPU:17, one launch (start us, length us, event | category | flops | bytes accessed | tf_op | source)
XLA Modules:
  0.0 32.6 jit_solution(11045487749514838599)
XLA Ops:
  0.7 0.6 %pad_add_fusion.place.rest_5_ = s32[2]{0:T(128)} fusion(s32[1]{0:T(128)} %bitcast.3, s32[1]{0:T(128)} %bitcast.2), kind=kLoop, calls=%fused_computation.1 | loop fusion | flops 2 | bytes 16 | tf_op jit(solution)/shard_map/stack | solution.py:173
  1.2 1.4 %constant_dynamic-slice_fusion.1.table = f32[64,128]{1,0:T(8,128)} fusion(f32[64,512]{1,0:T(8,128)} %constant.20.clone, s32[]{:T(128)S(6)} %select_n.4), kind=kLoop, calls=%fused_computation.3 | loop fusion | bytes 65540 | tf_op jit(solution)/shard_map/dynamic_slice | solution.py:176
  2.6 1.8 %pack.1 = (bf16[128,640]{1,0:T(8,128)(2,1)}, bf16[64,640]{1,0:T(8,128)(2,1)}) custom-call(bf16[128,512]{1,0:T(8,128)(2,1)} %latent.1, bf16[64,128]{1,0:T(8,128)(2,1)} %bitcast.4, f32[1,512]{1,0:T(1,128)} %bitcast.5, f32[64,128]{1,0:T(8,128)} %constant_dynamic-slice_fusion.1.table, s32[1]{0:T(128)S(6)} %copy.9.length.rest_4_, s32[2]{0:T(128)} %pad_add_fusion.place.rest_5_), custom_call_target="tpu_custom_call" | custom-call | tf_op jit(solution)/shard_map/pack/pallas_call | solution.py:180
  4.4 1.3 %collective-permute-start.1 = (bf16[128,640]{1,0:T(8,128)(2,1)}, bf16[128,640]{1,0:T(8,128)(2,1)S(1)}, u32[]{:S(2)}, u32[]{:S(2)}) collective-permute-start(bf16[128,640]{1,0:T(8,128)(2,1)} %get-tuple-element.9.payload.own), channel_id=1, source_target_pairs={{0,4},{4,8},{8,12},{1,9},{5,13},{2,6},{6,10},{10,14},{3,11},{7,15}... | collective-permute-start | bytes 491528 | tf_op jit(solution)/shard_map/ppermute | solution.py:208
  5.7 0.7 %collective-permute-start = (bf16[64,640]{1,0:T(8,128)(2,1)}, bf16[64,640]{1,0:T(8,128)(2,1)S(1)}, u32[]{:S(2)}, u32[]{:S(2)}) collective-permute-start(bf16[64,640]{1,0:T(8,128)(2,1)} %get-tuple-element.12), channel_id=1, source_target_pairs={{0,12},{1,13},{2,14},{3,15},{16,28},{17,29},{18,30},{19,31}} | collective-permute-start | bytes 245768 | tf_op jit(solution)/shard_map/ppermute | solution.py:200
  6.4 0.0 collective-permute-done.rest_0_
  6.4 0.0 copy-start.1
  6.4 6.8 %collective-permute-done.1.rest_1_ = bf16[128,640]{1,0:T(8,128)(2,1)S(1)} collective-permute-done((bf16[128,640]{1,0:T(8,128)(2,1)}, bf16[128,640]{1,0:T(8,128)(2,1)S(1)}, u32[]{:S(2)}, u32[]{:S(2)}) %collective-permute-start.1) | collective-permute-done | bytes 163872 | tf_op jit(solution)/shard_map/ppermute | solution.py:208
  13.2 0.0 copy-start
  13.2 4.4 %collective-permute-start.2 = (bf16[192,640]{1,0:T(8,128)(2,1)S(1)}, bf16[192,640]{1,0:T(8,128)(2,1)S(1)}, u32[]{:S(2)}, u32[]{:S(2)}) collective-permute-start(bf16[192,640]{1,0:T(8,128)(2,1)S(1)} %pad_maximum_fusion), channel_id=1, source_target_pairs={{0,1},{1,0},{2,3},{3,2},{4,5},{5,4},{6,7},{7,6},{8,9},{9,8},{10,11... | collective-permute-start | bytes 737288 | tf_op jit(solution)/shard_map/ppermute | solution.py:231
  17.6 1.5 %constant_dynamic-slice_fusion.table = f32[128,128]{1,0:T(8,128)} fusion(f32[512,128]{1,0:T(8,128)} %constant.19.clone, s32[]{:T(128)S(6)} %select_n.4), kind=kLoop, calls=%fused_computation.2 | loop fusion | bytes 131076 | tf_op jit(solution)/shard_map/dynamic_slice | solution.py:175
  19.1 4.8 %own.1 = (bf16[128,4096]{1,0:T(8,128)(2,1)}, bf16[128,4096]{1,0:T(8,128)(2,1)}) custom-call(bf16[128,3072]{1,0:T(8,128)(2,1)} %queries.1, bf16[128,640]{1,0:T(8,128)(2,1)} %get-tuple-element.9.payload.own, bf16[512,4096]{1,0:T(8,128)(2,1)} %weight.3, f32[128,128]{1,0:T(8,128)} %constant_dynamic-slice_fusion.table), custom_call_target="tpu_custom_call" | custom-call | flops 536870912 | bytes 7077888 | tf_op jit(solution)/shard_map/own/pallas_call | solution.py:211
  23.8 0.0 collective-permute-done.2
  23.8 0.7 %slice.8.rest_2_ = bf16[64,640]{1,0:T(8,128)(2,1)} slice(bf16[192,640]{1,0:T(8,128)(2,1)S(1)} %collective-permute-done.2), slice={[0:64], [0:640]} | slice | bytes 163840 | tf_op jit(solution)/shard_map/slice | solution.py:236
  24.5 0.7 %slice.9.rest_3_ = bf16[128,640]{1,0:T(8,128)(2,1)} slice(bf16[192,640]{1,0:T(8,128)(2,1)S(1)} %collective-permute-done.2), slice={[64:192], [0:640]} | slice | bytes 327680 | tf_op jit(solution)/shard_map/slice | solution.py:236
  25.2 0.0 copy-done.1
  25.2 0.0 copy-done
  25.2 7.4 %attend.1 = bf16[128,2048]{1,0:T(8,128)(2,1)} custom-call(bf16[128,4096]{1,0:T(8,128)(2,1)} %get-tuple-element.10.full, bf16[128,640]{1,0:T(8,128)(2,1)} %get-tuple-element.9.payload.own, bf16[128,4096]{1,0:T(8,128)(2,1)} %get-tuple-element.11.expanded, bf16[512,4096]{1,0:T(8,128)(2,1)} %weight.3, bf16[64,640]{1,0:T(8,128)(2,1)} %copy-done.1, ...), custom_call_target="tpu_custom_call" | custom-call | flops 3221225472 | bytes 7340032 | tf_op jit(solution)/shard_map/attend/pallas_call | solution.py:244
  (1 shorter events, 0.0 us)
Async XLA Ops:
  4.4 8.8 %collective-permute-start.1 = (bf16[128,640]{1,0:T(8,128)(2,1)}, bf16[128,640]{1,0:T(8,128)(2,1)S(1)}, u32[]{:S(2)}, u32[]{:S(2)}) collective-permute-start(bf16[128,640]{1,0:T(8,128)(2,1)} %get-tuple-element.9.payload.own), channel_id=1, source_target_pairs={{0,4},{4,8},{8,12},{1,9},{5,13},{2,6},{6,10},{10,14},{3,11},{7,15}... | collective-permute-start | bytes 491528 | tf_op jit(solution)/shard_map/ppermute | solution.py:208
  5.7 0.7 %collective-permute-start = (bf16[64,640]{1,0:T(8,128)(2,1)}, bf16[64,640]{1,0:T(8,128)(2,1)S(1)}, u32[]{:S(2)}, u32[]{:S(2)}) collective-permute-start(bf16[64,640]{1,0:T(8,128)(2,1)} %get-tuple-element.12), channel_id=1, source_target_pairs={{0,12},{1,13},{2,14},{3,15},{16,28},{17,29},{18,30},{19,31}} | collective-permute-start | bytes 245768 | tf_op jit(solution)/shard_map/ppermute | solution.py:200
  6.4 18.8 %copy-start.1 = (bf16[64,640]{1,0:T(8,128)(2,1)}, bf16[64,640]{1,0:T(8,128)(2,1)S(1)}, u32[]{:S(2)}) copy-start(bf16[64,640]{1,0:T(8,128)(2,1)S(1)} %collective-permute-done.rest_0_) | copy-start | bytes 245764
  13.2 12.0 %copy-start = (bf16[128,640]{1,0:T(8,128)(2,1)}, bf16[128,640]{1,0:T(8,128)(2,1)S(1)}, u32[]{:S(2)}) copy-start(bf16[128,640]{1,0:T(8,128)(2,1)S(1)} %collective-permute-done.1.rest_1_) | copy-start | bytes 491524
  13.2 10.6 %collective-permute-start.2 = (bf16[192,640]{1,0:T(8,128)(2,1)S(1)}, bf16[192,640]{1,0:T(8,128)(2,1)S(1)}, u32[]{:S(2)}, u32[]{:S(2)}) collective-permute-start(bf16[192,640]{1,0:T(8,128)(2,1)S(1)} %pad_maximum_fusion), channel_id=1, source_target_pairs={{0,1},{1,0},{2,3},{3,2},{4,5},{5,4},{6,7},{7,6},{8,9},{9,8},{10,11... | collective-permute-start | bytes 737288 | tf_op jit(solution)/shard_map/ppermute | solution.py:231

commit v2 on v1

--- a/solution.py
+++ b/solution.py
@@ -15,10 +15,12 @@
 WIDE = 128
 FULL = 256
 MASKED = -1e30
+MIB = 1024 * 1024
 EXPONENT = math.log2(math.e) / math.sqrt(NOPE + ROPE)
 
 VMEM = pl.BlockSpec(memory_space=pltpu.VMEM)
 SMEM = pl.BlockSpec(memory_space=pltpu.SMEM)
+ANY = pl.BlockSpec(memory_space=pl.ANY)
 
 
 def tables(positions):
@@ -31,17 +33,21 @@
     return rows, np.ascontiguousarray(columns)
 
 
-def pack_kernel(latent, rope, gain, table, length, place, payload, piece):
+def pack_kernel(latent, rope, gain, tables_hbm, length, payload, piece, table, arrived):
     rows, width = latent.shape
     half = ROPE // 2
+    ctx, sub = lax.axis_index("ctx"), lax.axis_index("sub")
+    copy = pltpu.make_async_copy(tables_hbm.at[ctx], table, arrived)
+    copy.start()
     wide = latent[...].astype(jnp.float32)
     mean = jnp.mean(wide * wide, -1, keepdims=True)
     normed = (wide * lax.rsqrt(mean + 1e-06) * gain[...]).astype(jnp.bfloat16)
     keys = rope[...].astype(jnp.float32)
     low, high = keys[:half], keys[half:]
+    copy.wait()
     cosines, sines = table[:half], table[half:]
     rotated = jnp.concatenate([low * cosines - high * sines, low * sines + high * cosines], 0)
-    position = place[0] * rows + lax.broadcasted_iota(jnp.int32, (WIDE - ROPE, rows), 1)
+    position = ctx * rows + lax.broadcasted_iota(jnp.int32, (WIDE - ROPE, rows), 1)
     first = lax.broadcasted_iota(jnp.int32, (WIDE - ROPE, rows), 0) == 0
     bias = jnp.where(first & (position >= length[0]), MASKED, 0.0)
     extra = jnp.concatenate([rotated, bias], 0).T.astype(jnp.bfloat16)
@@ -50,13 +56,16 @@
     size = piece.shape[0]
     for k in range(rows // size):
 
-        @pl.when(place[1] == k)
+        @pl.when(sub == k)
         def _():
             piece[:, :width] = normed[k * size : (k + 1) * size]
             piece[:, width:] = extra[k * size : (k + 1) * size]
 
 
-def own_kernel(heads, queries, payload, weight, table, expanded, full):
+def own_kernel(heads, queries, payload, weight, tables_hbm, expanded, full, table, arrived):
+    copy = pltpu.make_async_copy(tables_hbm.at[lax.axis_index("ctx")], table, arrived)
+    copy.start()
+    copy.wait()
     rows = queries.shape[0]
     width = weight.shape[0]
     cosines = jnp.concatenate([table[:, :ROPE]] * 2, 1)
@@ -90,23 +99,27 @@
 
 def attend_kernel(heads, distances, full, own, expanded, weight, *rest):
     count = len(distances)
-    pieces, (length, place, out, keys, grown, scores, weights) = rest[:count], rest[count:]
+    pieces, (length, out, keys, grown, scores, weights) = rest[:count], rest[count:]
     rows = full.shape[0]
     width = weight.shape[0]
     columns = NOPE + VDIM
-    ctx, sub = place[0], place[1]
+    ctx, sub = lax.axis_index("ctx"), lax.axis_index("sub")
     keys[:rows, width:] = own[:, width:]
     spare = (lax.broadcasted_iota(jnp.int32, (1, WIDE), 1) == ROPE).astype(jnp.float32)
     spare = (spare * MASKED).astype(jnp.bfloat16)
     at = rows
-    for ref, (even, odd) in zip(pieces, distances, strict=True):
-        size = ref.shape[0]
-        keys[at : at + size, :width] = ref[:, :width]
-        there = ctx >= jnp.where(sub == 0, even, odd)
-        last = ref[:, width:]
-        keys[at : at + size, width:] = jnp.where(there, last, jnp.broadcast_to(spare, last.shape))
-        at += size
-    total = at
+    for ref, inside in zip(pieces, distances, strict=True):
+        begin = 0
+        for size, by_core in inside:
+            piece = slice(begin, begin + size)
+            keys[at : at + size, :width] = ref[piece, :width]
+            distance = sum(jnp.where(sub == s, d, 0) for s, d in enumerate(by_core))
+            last = ref[piece, width:]
+            keys[at : at + size, width:] = jnp.where(
+                ctx >= distance, last, jnp.broadcast_to(spare, last.shape)
+            )
+            at += size
+            begin += size
     row = lax.broadcasted_iota(jnp.int32, (rows, rows), 0)
     causal = lax.broadcasted_iota(jnp.int32, (rows, rows), 1) <= row
     live = ctx * rows + lax.broadcasted_iota(jnp.int32, (rows, 1), 0) < length[0]
@@ -159,34 +172,29 @@
             mix(t - 2, totals.pop(t - 2))
 
 
-def in_vmem(x):
-    return pltpu.with_memory_space_constraint(x, pltpu.VMEM)
-
-
 def per_device(
     ctx_size, sub_size, queries, latent, rope_keys, latent_gain, up_weight, prompt_length
 ):
     rows, width = latent.shape
     heads = up_weight.shape[1] // (NOPE + VDIM)
-    ctx = lax.axis_index("ctx")
-    sub = lax.axis_index("sub")
-    place = jnp.stack([ctx, sub]).astype(jnp.int32)
     by_row, by_column = tables(ctx_size * rows)
-    row_table = lax.dynamic_slice_in_dim(jnp.asarray(by_row), ctx * rows, rows, 0)
-    column_table = lax.dynamic_slice_in_dim(jnp.asarray(by_column), ctx * rows, rows, 1)
+    by_row = by_row.reshape(ctx_size, rows, 2 * ROPE)
+    by_column = by_column.reshape(ROPE, ctx_size, rows).transpose(1, 0, 2)
 
     bf16 = jnp.bfloat16
     wide = width + WIDE
     payload, piece = pl.pallas_call(
         pack_kernel,
-        in_specs=[VMEM] * 4 + [SMEM] * 2,
+        in_specs=[VMEM] * 3 + [ANY, SMEM],
         out_specs=[VMEM] * 2,
         out_shape=[
             jax.ShapeDtypeStruct((rows, wide), bf16),
             jax.ShapeDtypeStruct((rows // sub_size, wide), bf16),
         ],
+        scratch_shapes=[pltpu.VMEM((ROPE, rows), jnp.float32), pltpu.SemaphoreType.DMA],
+        compiler_params=pltpu.CompilerParams(vmem_limit_bytes=4 * MIB),
         name="pack",
-    )(latent, rope_keys.T, latent_gain.reshape(1, width), column_table, prompt_length, place)
+    )(latent, rope_keys.T, latent_gain.reshape(1, width), jnp.asarray(by_column), prompt_length)
 
     cores = ("ctx", "sub")
     whole_sets = (ctx_size - 1) // sub_size
@@ -198,7 +206,7 @@
             for s in range(sub_size)
         ]
         direct.append(lax.ppermute(piece, cores, pairs))
-        distances.append([d] * sub_size)
+        distances.append((piece.shape[0], [d] * sub_size))
     for k in range(whole_sets):
         pairs = [
             (c * sub_size + s, (c + k * sub_size + 1 + s) * sub_size + s)
@@ -206,44 +214,45 @@
             for c in range(ctx_size - (k * sub_size + 1 + s))
         ]
         direct.append(lax.ppermute(payload, cores, pairs))
-        distances.append([k * sub_size + 1 + s for s in range(sub_size)])
+        distances.append((rows, [k * sub_size + 1 + s for s in range(sub_size)]))
 
     expanded, full = pl.pallas_call(
         functools.partial(own_kernel, heads),
-        in_specs=[VMEM] * 4,
+        in_specs=[VMEM] * 3 + [ANY],
         out_specs=[VMEM] * 2,
         out_shape=[
             jax.ShapeDtypeStruct((rows, up_weight.shape[1]), bf16),
             jax.ShapeDtypeStruct((rows, heads * FULL), bf16),
         ],
+        scratch_shapes=[pltpu.VMEM((rows, 2 * ROPE), jnp.float32), pltpu.SemaphoreType.DMA],
+        compiler_params=pltpu.CompilerParams(
+            vmem_limit_bytes=4 * MIB
+            + 2 * (queries.size + up_weight.size + 2 * rows * up_weight.shape[1])
+        ),
         name="own",
         cost_estimate=pl.CostEstimate(
             flops=2 * rows * width * up_weight.shape[1],
             bytes_accessed=2 * (queries.size + up_weight.size + 2 * rows * up_weight.shape[1]),
             transcendentals=0,
         ),
-    )(queries, payload, up_weight, row_table)
-
+    )(queries, payload, up_weight, jnp.asarray(by_row))
+
+    *direct, expanded, full = lax.optimization_barrier((*direct, expanded, full))
     together = jnp.concatenate(direct, 0)
-    pieces, both = [together], [distances]
-    arrivals = list(zip(direct, distances, strict=True))
+    pieces, inside = [together], [distances]
     for r in range(1, sub_size):
-        swapped = lax.ppermute(together, "sub", [(s, (s + r) % sub_size) for s in range(sub_size)])
-        at = 0
-        for part, dist in zip(direct, distances, strict=True):
-            arrivals.append(
-                (
-                    swapped[at : at + part.shape[0]],
-                    [dist[(s - r) % sub_size] for s in range(sub_size)],
-                )
-            )
-            at += part.shape[0]
-    parts = [a for a, _ in arrivals]
-    total = rows + sum(p.shape[0] for p in parts)
+        pairs = [(s, (s + r) % sub_size) for s in range(sub_size)]
+        pieces.append(lax.ppermute(together, "sub", pairs))
+        inside.append(
+            [(size, [d[(s - r) % sub_size] for s in range(sub_size)]) for size, d in distances]
+        )
+    total = rows + sum(p.shape[0] for p in pieces)
+    held = (full, expanded, up_weight, *pieces)
+    scratch = 2 * total * (wide + 6 * (NOPE + VDIM) + 6 * rows)
 
     return pl.pallas_call(
-        functools.partial(attend_kernel, heads, [(d[0], d[-1]) for _, d in arrivals]),
-        in_specs=[VMEM] * (4 + len(parts)) + [SMEM] * 2,
+        functools.partial(attend_kernel, heads, inside),
+        in_specs=[VMEM] * (4 + len(pieces)) + [SMEM],
         out_specs=VMEM,
         out_shape=jax.ShapeDtypeStruct((rows, heads * VDIM), bf16),
         scratch_shapes=[
@@ -252,13 +261,16 @@
             pltpu.VMEM((2, rows, total), jnp.float32),
             pltpu.VMEM((2, rows, total), bf16),
         ],
+        compiler_params=pltpu.CompilerParams(
+            vmem_limit_bytes=6 * MIB + 2 * sum(x.size for x in held) + scratch
+        ),
         name="attend",
         cost_estimate=pl.CostEstimate(
             flops=2 * total * (width + 2 * rows) * up_weight.shape[1],
             bytes_accessed=2 * (up_weight.size + 3 * rows * up_weight.shape[1]),
             transcendentals=heads * rows * total,
         ),
-    )(full, payload, expanded, up_weight, *parts, prompt_length, place)
+    )(full, payload, expanded, up_weight, *pieces, prompt_length)
 
 
 def solution(mesh):

time: 32.9 us -> 24.2 us (0.74)
  the two profiles are of different devices: /device:TPU:17 before, /device:TPU:0 now
where the time goes in v2:
time: 24.2 us; the launch traced here: 23.9 us
  starting transfers between devices  8.35 us (35%)
  local copies, waits for them, and re-layouts  7.5 us (31%)
  Pallas kernels  5.77 us (24%)
  waiting for transfers between devices  1.5 us (6%)
  between operations  0.75 us (3%)
    unnamed x17, local copies, waits for them, and re-layouts  7.48 us
    ppermute x1, starting transfers between devices, per_device(): direct.append(lax.ppermute(payload, cores, pairs))  4.97 us
    pallas_call x1, Pallas kernels, per_device(): pl.pallas_call(functools.partial(attend_kernel, heads, inside), in_specs=...  4.47 us
    ppermute x1, starting transfers between devices, per_device(): direct.append(lax.ppermute(piece, cores, pairs))  3.31 us
    ppermute x1, waiting for transfers between devices, per_device(): pieces.append(lax.ppermute(together, 'sub', pairs))  1.5 us
    pallas_call x1, Pallas kernels, per_device(): pl.pallas_call(functools.partial(own_kernel, heads), in_specs=[VMEM] * 3...  1.06 us
  transfers between devices with their start and end apart: 3, of which 1 were waited for; matrix products, arithmetic and copies ran while one was open for 0% of the time, Pallas kernels for 4%

profile of v2, /device:TPU:0, one launch (start us, length us, event | category | flops | bytes accessed | tf_op | source)
XLA Modules:
  0.0 23.9 jit_solution(8647595275079337076)
XLA Ops:
  0.7 0.0 copy-start.4
  0.7 0.9 %copy-done.4 = bf16[128,512]{1,0:T(8,128)(2,1)S(1)} copy-done((bf16[128,512]{1,0:T(8,128)(2,1)S(1)}, bf16[128,512]{1,0:T(8,128)(2,1)}, u32[]{:S(2)}) %copy-start.4) | copy-done | bytes 131096
  1.6 0.0 copy-start.5
  1.6 0.9 %copy-done.5 = f32[4,64,128]{2,1,0:T(8,128)S(1)} copy-done((f32[4,64,128]{2,1,0:T(8,128)S(1)}, f32[4,64,128]{2,1,0:T(8,128)}, u32[]{:S(2)}) %copy-start.5) | copy-done | bytes 131096
  2.5 0.0 copy-start.6
  2.5 0.7 %copy-done.6 = bf16[128,64]{0,1:T(8,128)(2,1)S(1)} copy-done((bf16[128,64]{0,1:T(8,128)(2,1)S(1)}, bf16[128,64]{0,1:T(8,128)(2,1)}, u32[]{:S(2)}) %copy-start.6) | copy-done | bytes 16408
  3.2 0.0 copy-start.7
  3.2 0.7 %copy-done.7 = f32[512]{0:T(512)S(1)} copy-done((f32[512]{0:T(512)S(1)}, f32[512]{0:T(512)}, u32[]{:S(2)}) %copy-start.7) | copy-done | bytes 2072
  3.9 0.2 %pack.1 = (bf16[128,640]{1,0:T(8,128)(2,1)S(1)}, bf16[64,640]{1,0:T(8,128)(2,1)S(1)}) custom-call(bf16[128,512]{1,0:T(8,128)(2,1)S(1)} %copy-done.4, bf16[64,128]{1,0:T(8,128)(2,1)S(1)} %bitcast.2, f32[1,512]{1,0:T(1,128)S(1)} %bitcast.3, f32[4,64,128]{2,1,0:T(8,128)S(1)} %copy-done.5, s32[1]{0:T(128)S(6)} %copy.10.length.rest_2_), custom_call_target="tpu_custom_call" | custom-call | tf_op jit(solution)/shard_map/pack/pallas_call | solution.py:186
  4.1 5.0 %collective-permute-start.1 = (bf16[128,640]{1,0:T(8,128)(2,1)S(1)}, bf16[128,640]{1,0:T(8,128)(2,1)S(1)}, u32[]{:S(2)}, u32[]{:S(2)}) collective-permute-start(bf16[128,640]{1,0:T(8,128)(2,1)S(1)} %get-tuple-element.14.payload.own), channel_id=1, source_target_pairs={{0,4},{4,8},{8,12},{1,9},{5,13},{2,6},{6,10},{10,14},{3,11},{7,15}... | collective-permute-start | bytes 491528 | tf_op jit(solution)/shard_map/ppermute | solution.py:216
  9.1 3.3 %collective-permute-start = (bf16[64,640]{1,0:T(8,128)(2,1)S(1)}, bf16[64,640]{1,0:T(8,128)(2,1)S(1)}, u32[]{:S(2)}, u32[]{:S(2)}) collective-permute-start(bf16[64,640]{1,0:T(8,128)(2,1)S(1)} %get-tuple-element.13), channel_id=1, source_target_pairs={{0,12},{1,13},{2,14},{3,15},{16,28},{17,29},{18,30},{19,31}} | collective-permute-start | bytes 245768 | tf_op jit(solution)/shard_map/ppermute | solution.py:208
  12.4 0.0 copy-start
  12.4 2.2 %copy-done = bf16[512,4096]{1,0:T(8,128)(2,1)S(1)} copy-done((bf16[512,4096]{1,0:T(8,128)(2,1)S(1)}, bf16[512,4096]{1,0:T(8,128)(2,1)}, u32[]{:S(2)}) %copy-start) | copy-done | bytes 4194328
  14.6 0.0 copy-start.2
  14.6 1.1 %copy-done.2 = bf16[128,3072]{1,0:T(8,128)(2,1)S(1)} copy-done((bf16[128,3072]{1,0:T(8,128)(2,1)S(1)}, bf16[128,3072]{1,0:T(8,128)(2,1)}, u32[]{:S(2)}) %copy-start.2) | copy-done | bytes 786456
  15.7 0.0 copy-start.3
  15.7 0.9 %copy-done.3 = f32[4,128,128]{2,1,0:T(8,128)S(1)} copy-done((f32[4,128,128]{2,1,0:T(8,128)S(1)}, f32[4,128,128]{2,1,0:T(8,128)}, u32[]{:S(2)}) %copy-start.3) | copy-done | bytes 262168
  16.7 0.0 copy-start.1
  16.7 1.1 %own.1 = (bf16[128,4096]{1,0:T(8,128)(2,1)S(1)}, bf16[128,4096]{1,0:T(8,128)(2,1)S(1)}) custom-call(bf16[128,3072]{1,0:T(8,128)(2,1)S(1)} %copy-done.2, bf16[128,640]{1,0:T(8,128)(2,1)S(1)} %get-tuple-element.14.payload.own, bf16[512,4096]{1,0:T(8,128)(2,1)S(1)} %copy-done, f32[4,128,128]{2,1,0:T(8,128)S(1)} %copy-done.3), custom_call_target="tpu_custom_call" | custom-call | flops 536870912 | bytes 7077888 | tf_op jit(solution)/shard_map/own/pallas_call | solution.py:219
  17.8 0.0 collective-permute-done
  17.8 0.0 collective-permute-done.1
  17.8 0.1 collective-permute-start.2
  17.9 1.5 %collective-permute-done.2.rest_1_ = bf16[192,640]{1,0:T(8,128)(2,1)S(1)} collective-permute-done((bf16[192,640]{1,0:T(8,128)(2,1)S(1)}, bf16[192,640]{1,0:T(8,128)(2,1)S(1)}, u32[]{:S(2)}, u32[]{:S(2)}) %collective-permute-start.2) | collective-permute-done | bytes 245792 | tf_op jit(solution)/shard_map/ppermute | solution.py:245
  19.4 0.0 copy-done.1
  19.4 4.5 %attend.1 = bf16[128,2048]{1,0:T(8,128)(2,1)} custom-call(bf16[128,4096]{1,0:T(8,128)(2,1)S(1)} %get-tuple-element.17.full, bf16[128,640]{1,0:T(8,128)(2,1)S(1)} %get-tuple-element.14.payload.own, bf16[128,4096]{1,0:T(8,128)(2,1)S(1)} %get-tuple-element.18.expanded, bf16[512,4096]{1,0:T(8,128)(2,1)S(1)} %copy-done.1, ...), custom_call_target="tpu_custom_call" | custom-call | flops 3221225472 | bytes 7340032 | tf_op jit(solution)/shard_map/attend/pallas_call | solution.py:253
  (2 shorter events, 0.0 us)
Async XLA Ops:
  0.7 0.9 %copy-start.4 = (bf16[128,512]{1,0:T(8,128)(2,1)S(1)}, bf16[128,512]{1,0:T(8,128)(2,1)}, u32[]{:S(2)}) copy-start(bf16[128,512]{1,0:T(8,128)(2,1)} %latent.1) | copy-start | bytes 393220
  1.6 0.9 %copy-start.5 = (f32[4,64,128]{2,1,0:T(8,128)S(1)}, f32[4,64,128]{2,1,0:T(8,128)}, u32[]{:S(2)}) copy-start(f32[4,64,128]{2,1,0:T(8,128)} %constant.4.clone.tables_hbm) | copy-start | bytes 393220
  2.5 0.7 %copy-start.6 = (bf16[128,64]{0,1:T(8,128)(2,1)S(1)}, bf16[128,64]{0,1:T(8,128)(2,1)}, u32[]{:S(2)}) copy-start(bf16[128,64]{0,1:T(8,128)(2,1)} %param.10) | copy-start | bytes 49156
  3.2 0.7 %copy-start.7 = (f32[512]{0:T(512)S(1)}, f32[512]{0:T(512)}, u32[]{:S(2)}) copy-start(f32[512]{0:T(512)} %param.11) | copy-start | bytes 6148
  4.1 13.7 %collective-permute-start.1 = (bf16[128,640]{1,0:T(8,128)(2,1)S(1)}, bf16[128,640]{1,0:T(8,128)(2,1)S(1)}, u32[]{:S(2)}, u32[]{:S(2)}) collective-permute-start(bf16[128,640]{1,0:T(8,128)(2,1)S(1)} %get-tuple-element.14.payload.own), channel_id=1, source_target_pairs={{0,4},{4,8},{8,12},{1,9},{5,13},{2,6},{6,10},{10,14},{3,11},{7,15}... | collective-permute-start | bytes 491528 | tf_op jit(solution)/shard_map/ppermute | solution.py:216
  9.1 8.7 %collective-permute-start = (bf16[64,640]{1,0:T(8,128)(2,1)S(1)}, bf16[64,640]{1,0:T(8,128)(2,1)S(1)}, u32[]{:S(2)}, u32[]{:S(2)}) collective-permute-start(bf16[64,640]{1,0:T(8,128)(2,1)S(1)} %get-tuple-element.13), channel_id=1, source_target_pairs={{0,12},{1,13},{2,14},{3,15},{16,28},{17,29},{18,30},{19,31}} | collective-permute-start | bytes 245768 | tf_op jit(solution)/shard_map/ppermute | solution.py:208
  12.4 2.2 %copy-start = (bf16[512,4096]{1,0:T(8,128)(2,1)S(1)}, bf16[512,4096]{1,0:T(8,128)(2,1)}, u32[]{:S(2)}) copy-start(bf16[512,4096]{1,0:T(8,128)(2,1)} %weight.3) | copy-start | bytes 12582916
  14.6 1.1 %copy-start.2 = (bf16[128,3072]{1,0:T(8,128)(2,1)S(1)}, bf16[128,3072]{1,0:T(8,128)(2,1)}, u32[]{:S(2)}) copy-start(bf16[128,3072]{1,0:T(8,128)(2,1)} %queries.1) | copy-start | bytes 2359300
  15.7 0.9 %copy-start.3 = (f32[4,128,128]{2,1,0:T(8,128)S(1)}, f32[4,128,128]{2,1,0:T(8,128)}, u32[]{:S(2)}) copy-start(f32[4,128,128]{2,1,0:T(8,128)} %constant.5.clone.tables_hbm) | copy-start | bytes 786436
  16.7 2.7 %copy-start.1 = (bf16[512,4096]{1,0:T(8,128)(2,1)S(1)}, bf16[512,4096]{1,0:T(8,128)(2,1)}, u32[]{:S(2)}) copy-start(bf16[512,4096]{1,0:T(8,128)(2,1)} %weight.3) | copy-start | bytes 12582916
  17.8 1.6 %collective-permute-start.2 = (bf16[192,640]{1,0:T(8,128)(2,1)S(1)}, bf16[192,640]{1,0:T(8,128)(2,1)S(1)}, u32[]{:S(2)}, u32[]{:S(2)}) collective-permute-start(bf16[192,640]{1,0:T(8,128)(2,1)S(1)} %constant_dynamic-update-slice_fusion.rest_0_), channel_id=1, source_target_pairs={{0,1},{1,0},{2,3},{3,2},{4,5},{5,4},{6,7},{7,6},{8,9},{9,8},{10,11... | collective-permute-start | bytes 737288 | tf_op jit(solution)/shard_map/ppermute | solution.py:245

commit v3 on v2

--- a/solution.py
+++ b/solution.py
@@ -16,10 +16,12 @@
 FULL = 256
 MASKED = -1e30
 MIB = 1024 * 1024
+PACK_FLOPS = 4 * 10**9
 EXPONENT = math.log2(math.e) / math.sqrt(NOPE + ROPE)
 
 VMEM = pl.BlockSpec(memory_space=pltpu.VMEM)
 SMEM = pl.BlockSpec(memory_space=pltpu.SMEM)
+HBM = pl.BlockSpec(memory_space=pltpu.HBM)
 ANY = pl.BlockSpec(memory_space=pl.ANY)
 
 
@@ -33,18 +35,27 @@
     return rows, np.ascontiguousarray(columns)
 
 
-def pack_kernel(latent, rope, gain, tables_hbm, length, payload, piece, table, arrived):
+def pack_kernel(
+    latent_hbm, rope_hbm, gain_hbm, tables_hbm, length, payload, piece, latent, rope, gain, table, arrived
+):
     rows, width = latent.shape
     half = ROPE // 2
     ctx, sub = lax.axis_index("ctx"), lax.axis_index("sub")
-    copy = pltpu.make_async_copy(tables_hbm.at[ctx], table, arrived)
-    copy.start()
+    copies = [
+        pltpu.make_async_copy(source, target, arrived.at[k])
+        for k, (source, target) in enumerate(
+            [(latent_hbm, latent), (gain_hbm, gain), (rope_hbm, rope), (tables_hbm.at[ctx], table)]
+        )
+    ]
+    for copy in copies:
+        copy.start()
+    for copy in copies:
+        copy.wait()
     wide = latent[...].astype(jnp.float32)
     mean = jnp.mean(wide * wide, -1, keepdims=True)
     normed = (wide * lax.rsqrt(mean + 1e-06) * gain[...]).astype(jnp.bfloat16)
     keys = rope[...].astype(jnp.float32)
     low, high = keys[:half], keys[half:]
-    copy.wait()
     cosines, sines = table[:half], table[half:]
     rotated = jnp.concatenate([low * cosines - high * sines, low * sines + high * cosines], 0)
     position = ctx * rows + lax.broadcasted_iota(jnp.int32, (WIDE - ROPE, rows), 1)
@@ -97,21 +108,26 @@
         ).astype(jnp.bfloat16)
 
 
-def attend_kernel(heads, distances, full, own, expanded, weight, *rest):
-    count = len(distances)
+def attend_kernel(heads, layout, levels, full, own, expanded, weight, *rest):
+    count = len(rest) - 6
     pieces, (length, out, keys, grown, scores, weights) = rest[:count], rest[count:]
     rows = full.shape[0]
     width = weight.shape[0]
     columns = NOPE + VDIM
     ctx, sub = lax.axis_index("ctx"), lax.axis_index("sub")
-    keys[:rows, width:] = own[:, width:]
-    spare = (lax.broadcasted_iota(jnp.int32, (1, WIDE), 1) == ROPE).astype(jnp.float32)
-    spare = (spare * MASKED).astype(jnp.bfloat16)
-    at = rows
-    for ref, inside in zip(pieces, distances, strict=True):
-        begin = 0
-        for size, by_core in inside:
-            piece = slice(begin, begin + size)
+    row = lax.broadcasted_iota(jnp.int32, (rows, rows), 0)
+    causal = lax.broadcasted_iota(jnp.int32, (rows, rows), 1) <= row
+    live = ctx * rows + lax.broadcasted_iota(jnp.int32, (rows, 1), 0) < length[0]
+
+    def run(total):
+        keys[:rows, width:] = own[:, width:]
+        spare = (lax.broadcasted_iota(jnp.int32, (1, WIDE), 1) == ROPE).astype(jnp.float32)
+        spare = (spare * MASKED).astype(jnp.bfloat16)
+        at = rows
+        for which, begin, size, by_core in layout:
+            if at >= total:
+                break
+            ref, piece = pieces[which], slice(begin, begin + size)
             keys[at : at + size, :width] = ref[piece, :width]
             distance = sum(jnp.where(sub == s, d, 0) for s, d in enumerate(by_core))
             last = ref[piece, width:]
@@ -119,57 +135,68 @@
                 ctx >= distance, last, jnp.broadcast_to(spare, last.shape)
             )
             at += size
-            begin += size
-    row = lax.broadcasted_iota(jnp.int32, (rows, rows), 0)
-    causal = lax.broadcasted_iota(jnp.int32, (rows, rows), 1) <= row
-    live = ctx * rows + lax.broadcasted_iota(jnp.int32, (rows, 1), 0) < length[0]
-
-    def grow(i):
-        at = slice(2 * columns * i, 2 * columns * (i + 1))
-        grown[i % 3, :rows] = expanded[:, at]
-        grown[i % 3, rows:] = jnp.dot(
-            keys[rows:, :width], weight[:, at], preferred_element_type=jnp.float32
-        ).astype(jnp.bfloat16)
-
-    def score(h):
-        i, e = divmod(h, 2)
-        nope = grown[i % 3, :, columns * e : columns * e + NOPE]
-        whole = jnp.concatenate([nope, keys[:, width:]], 1)
-        found = lax.dot_general(
-            full[:, FULL * h : FULL * (h + 1)],
-            whole,
-            (((1,), (1,)), ((), ())),
-            preferred_element_type=jnp.float32,
-        )
-        scores[h % 2, :, :rows] = jnp.where(causal, found[:, :rows], MASKED)
-        scores[h % 2, :, rows:] = found[:, rows:]
-
-    def soften(h):
-        found = scores[h % 2]
-        top = jnp.max(found, 1, keepdims=True)
-        raw = jnp.exp2(found * EXPONENT - top * EXPONENT)
-        weights[h % 2] = raw.astype(jnp.bfloat16)
-        return jnp.sum(raw, 1, keepdims=True)
-
-    def mix(h, total_h):
-        i, e = divmod(h, 2)
-        values = grown[i % 3, :, columns * e + NOPE : columns * (e + 1)]
-        mixed = jnp.dot(weights[h % 2], values, preferred_element_type=jnp.float32)
-        out[:, VDIM * h : VDIM * (h + 1)] = jnp.where(live, mixed / total_h, 0.0).astype(
-            jnp.bfloat16
-        )
-
-    totals = {}
-    grow(0)
-    for t in range(heads + 2):
-        if t % 2 == 0 and t // 2 + 1 < heads // 2:
-            grow(t // 2 + 1)
-        if t < heads:
-            score(t)
-        if 0 <= t - 1 < heads:
-            totals[t - 1] = soften(t - 1)
-        if 0 <= t - 2 < heads:
-            mix(t - 2, totals.pop(t - 2))
+
+        def grow(i):
+            at = slice(2 * columns * i, 2 * columns * (i + 1))
+            grown[i % 3, :rows] = expanded[:, at]
+            if total > rows:
+                grown[i % 3, rows:total] = jnp.dot(
+                    keys[rows:total, :width], weight[:, at], preferred_element_type=jnp.float32
+                ).astype(jnp.bfloat16)
+
+        def score(h):
+            i, e = divmod(h, 2)
+            nope = grown[i % 3, :total, columns * e : columns * e + NOPE]
+            whole = jnp.concatenate([nope, keys[:total, width:]], 1)
+            found = lax.dot_general(
+                full[:, FULL * h : FULL * (h + 1)],
+                whole,
+                (((1,), (1,)), ((), ())),
+                preferred_element_type=jnp.float32,
+            )
+            scores[h % 2, :, :rows] = jnp.where(causal, found[:, :rows], MASKED)
+            if total > rows:
+                scores[h % 2, :, rows:total] = found[:, rows:]
+
+        def soften(h):
+            found = scores[h % 2, :, :total]
+            top = jnp.max(found, 1, keepdims=True)
+            raw = jnp.exp2(found * EXPONENT - top * EXPONENT)
+            weights[h % 2, :, :total] = raw.astype(jnp.bfloat16)
+            return jnp.sum(raw, 1, keepdims=True)
+
+        def mix(h, total_h):
+            i, e = divmod(h, 2)
+            values = grown[i % 3, :total, columns * e + NOPE : columns * (e + 1)]
+            mixed = jnp.dot(weights[h % 2, :, :total], values, preferred_element_type=jnp.float32)
+            out[:, VDIM * h : VDIM * (h + 1)] = jnp.where(live, mixed / total_h, 0.0).astype(
+                jnp.bfloat16
+            )
+
+        totals = {}
+        grow(0)
+        for t in range(heads + 2):
+            if t % 2 == 0 and t // 2 + 1 < heads // 2:
+                grow(t // 2 + 1)
+            if t < heads:
+                score(t)
+            if 0 <= t - 1 < heads:
+                totals[t - 1] = soften(t - 1)
+            if 0 <= t - 2 < heads:
+                mix(t - 2, totals.pop(t - 2))
+
+    above = -1
+    for last, total in levels:
+
+        @pl.when((ctx > above) & (ctx <= last))
+        def _():
+            run(total)
+
+        above = last
+
+
+def in_hbm(x):
+    return pltpu.with_memory_space_constraint(x, pltpu.HBM)
 
 
 def per_device(
@@ -185,20 +212,43 @@
     wide = width + WIDE
     payload, piece = pl.pallas_call(
         pack_kernel,
-        in_specs=[VMEM] * 3 + [ANY, SMEM],
+        in_specs=[HBM] * 4 + [SMEM],
         out_specs=[VMEM] * 2,
         out_shape=[
             jax.ShapeDtypeStruct((rows, wide), bf16),
             jax.ShapeDtypeStruct((rows // sub_size, wide), bf16),
         ],
-        scratch_shapes=[pltpu.VMEM((ROPE, rows), jnp.float32), pltpu.SemaphoreType.DMA],
+        scratch_shapes=[
+            pltpu.VMEM((rows, width), bf16),
+            pltpu.VMEM((ROPE, rows), bf16),
+            pltpu.VMEM((1, width), jnp.float32),
+            pltpu.VMEM((ROPE, rows), jnp.float32),
+            pltpu.SemaphoreType.DMA((4,)),
+        ],
+        cost_estimate=pl.CostEstimate(
+            flops=PACK_FLOPS, bytes_accessed=8 * rows * width, transcendentals=0
+        ),
         compiler_params=pltpu.CompilerParams(vmem_limit_bytes=4 * MIB),
         name="pack",
-    )(latent, rope_keys.T, latent_gain.reshape(1, width), jnp.asarray(by_column), prompt_length)
+    )(
+        in_hbm(latent),
+        in_hbm(rope_keys.T),
+        in_hbm(latent_gain.reshape(1, width)),
+        in_hbm(jnp.asarray(by_column)),
+        prompt_length,
+    )
 
     cores = ("ctx", "sub")
     whole_sets = (ctx_size - 1) // sub_size
     direct, distances = [], []
+    for k in range(whole_sets):
+        pairs = [
+            (c * sub_size + s, (c + k * sub_size + 1 + s) * sub_size + s)
+            for s in range(sub_size)
+            for c in range(ctx_size - (k * sub_size + 1 + s))
+        ]
+        direct.append(lax.ppermute(payload, cores, pairs))
+        distances.append([k * sub_size + 1 + s for s in range(sub_size)])
     for d in range(whole_sets * sub_size + 1, ctx_size):
         pairs = [
             (c * sub_size + s, (c + d) * sub_size + s)
@@ -206,15 +256,7 @@
             for s in range(sub_size)
         ]
         direct.append(lax.ppermute(piece, cores, pairs))
-        distances.append((piece.shape[0], [d] * sub_size))
-    for k in range(whole_sets):
-        pairs = [
-            (c * sub_size + s, (c + k * sub_size + 1 + s) * sub_size + s)
-            for s in range(sub_size)
-            for c in range(ctx_size - (k * sub_size + 1 + s))
-        ]
-        direct.append(lax.ppermute(payload, cores, pairs))
-        distances.append((rows, [k * sub_size + 1 + s for s in range(sub_size)]))
+        distances.append([d] * sub_size)
 
     expanded, full = pl.pallas_call(
         functools.partial(own_kernel, heads),
@@ -239,19 +281,27 @@
 
     *direct, expanded, full = lax.optimization_barrier((*direct, expanded, full))
     together = jnp.concatenate(direct, 0)
-    pieces, inside = [together], [distances]
+    pieces = [together]
     for r in range(1, sub_size):
         pairs = [(s, (s + r) % sub_size) for s in range(sub_size)]
         pieces.append(lax.ppermute(together, "sub", pairs))
-        inside.append(
-            [(size, [d[(s - r) % sub_size] for s in range(sub_size)]) for size, d in distances]
-        )
+    layout, begin = [], 0
+    for part, by_core in zip(direct, distances, strict=True):
+        for r in range(sub_size):
+            turned = [by_core[(s - r) % sub_size] for s in range(sub_size)]
+            layout.append((r, begin, part.shape[0], turned))
+        begin += part.shape[0]
     total = rows + sum(p.shape[0] for p in pieces)
+    levels = [(0, rows)]
+    if whole_sets:
+        levels.append((sub_size, rows * (1 + sub_size)))
+    if levels[-1][0] < ctx_size - 1:
+        levels.append((ctx_size - 1, total))
     held = (full, expanded, up_weight, *pieces)
     scratch = 2 * total * (wide + 6 * (NOPE + VDIM) + 6 * rows)
 
     return pl.pallas_call(
-        functools.partial(attend_kernel, heads, inside),
+        functools.partial(attend_kernel, heads, layout, levels),
         in_specs=[VMEM] * (4 + len(pieces)) + [SMEM],
         out_specs=VMEM,
         out_shape=jax.ShapeDtypeStruct((rows, heads * VDIM), bf16),

time: 24.2 us -> 20.5 us (0.85)
  the two profiles are of different devices: /device:TPU:0 before, /device:TPU:25 now
where the time goes in v3:
time: 20.5 us; the launch traced here: 20.3 us
  waiting for transfers between devices  9.81 us (48%)
  Pallas kernels  6.91 us (34%)
  starting transfers between devices  2.79 us (14%)
  between operations  0.75 us (4%)
    ppermute x1, waiting for transfers between devices, per_device(): direct.append(lax.ppermute(piece, cores, pairs))  6.83 us
    pallas_call x1, Pallas kernels, per_device(): pl.pallas_call(functools.partial(attend_kernel, heads, layout, levels), i...  4.54 us
    ppermute x1, waiting for transfers between devices, per_device(): pieces.append(lax.ppermute(together, 'sub', pairs))  1.5 us
    ppermute x1, waiting for transfers between devices, per_device(): direct.append(lax.ppermute(payload, cores, pairs))  1.48 us
    ppermute x1, starting transfers between devices, per_device(): direct.append(lax.ppermute(payload, cores, pairs))  1.42 us
    ppermute x1, starting transfers between devices, per_device(): direct.append(lax.ppermute(piece, cores, pairs))  1.29 us
    pallas_call x1, Pallas kernels, per_device(): pl.pallas_call(pack_kernel, in_specs=[HBM] * 4 + [SMEM], out_specs=[VMEM]...  1.25 us
    pallas_call x1, Pallas kernels, per_device(): pl.pallas_call(functools.partial(own_kernel, heads), in_specs=[VMEM] * 3...  1.11 us
  transfers between devices with their start and end apart: 3, of which 3 were waited for; matrix products, arithmetic and copies ran while one was open for 0% of the time, Pallas kernels for 5%

profile of v3, /device:TPU:25, one launch (start us, length us, event | category | flops | bytes accessed | tf_op | source)
XLA Modules:
  0.0 20.3 jit_solution(1715009443229296393)
XLA Ops:
  0.7 0.0 copy-start
  0.7 0.0 copy-start.1
  0.7 0.0 copy-start.2
  0.7 1.2 %pack.1 = (bf16[128,640]{1,0:T(8,128)(2,1)S(1)}, bf16[64,640]{1,0:T(8,128)(2,1)S(1)}) custom-call(bf16[128,512]{1,0:T(8,128)(2,1)} %latent_hbm.1, bf16[64,128]{1,0:T(8,128)(2,1)} %bitcast.2, f32[1,512]{1,0:T(1,128)} %bitcast.3, f32[4,64,128]{2,1,0:T(8,128)} %constant.4.clone.tables_hbm, s32[1]{0:T(128)S(6)} %copy.10.length.rest_2_), custom_call_target="tpu_custom_call" | custom-call | flops 4000000000 | bytes 524288 | tf_op jit(solution)/shard_map/pack/pallas_call | solution.py:213
  1.9 1.4 %collective-permute-start = (bf16[128,640]{1,0:T(8,128)(2,1)S(1)}, bf16[128,640]{1,0:T(8,128)(2,1)S(1)}, u32[]{:S(2)}, u32[]{:S(2)}) collective-permute-start(bf16[128,640]{1,0:T(8,128)(2,1)S(1)} %get-tuple-element.13.payload.own), channel_id=1, source_target_pairs={{0,4},{4,8},{8,12},{1,9},{5,13},{2,6},{6,10},{10,14},{3,11},{7,15}... | collective-permute-start | bytes 491528 | tf_op jit(solution)/shard_map/ppermute | solution.py:250
  3.4 1.3 %collective-permute-start.1 = (bf16[64,640]{1,0:T(8,128)(2,1)S(1)}, bf16[64,640]{1,0:T(8,128)(2,1)S(1)}, u32[]{:S(2)}, u32[]{:S(2)}) collective-permute-start(bf16[64,640]{1,0:T(8,128)(2,1)S(1)} %get-tuple-element.14), channel_id=1, source_target_pairs={{0,12},{1,13},{2,14},{3,15},{16,28},{17,29},{18,30},{19,31}} | collective-permute-start | bytes 245768 | tf_op jit(solution)/shard_map/ppermute | solution.py:258
  4.7 0.0 copy-done
  4.7 0.0 copy-done.1
  4.7 0.0 copy-done.2
  4.7 1.1 %own.1 = (bf16[128,4096]{1,0:T(8,128)(2,1)S(1)}, bf16[128,4096]{1,0:T(8,128)(2,1)S(1)}) custom-call(bf16[128,3072]{1,0:T(8,128)(2,1)S(1)} %copy-done.1, bf16[128,640]{1,0:T(8,128)(2,1)S(1)} %get-tuple-element.13.payload.own, bf16[512,4096]{1,0:T(8,128)(2,1)S(1)} %copy-done, f32[4,128,128]{2,1,0:T(8,128)S(1)} %copy-done.2), custom_call_target="tpu_custom_call" | custom-call | flops 536870912 | bytes 7077888 | tf_op jit(solution)/shard_map/own/pallas_call | solution.py:261
  5.8 6.8 %collective-permute-done.1 = bf16[64,640]{1,0:T(8,128)(2,1)S(1)} collective-permute-done((bf16[64,640]{1,0:T(8,128)(2,1)S(1)}, bf16[64,640]{1,0:T(8,128)(2,1)S(1)}, u32[]{:S(2)}, u32[]{:S(2)}) %collective-permute-start.1) | collective-permute-done | bytes 81952 | tf_op jit(solution)/shard_map/ppermute | solution.py:258
  12.7 1.5 %collective-permute-done = bf16[128,640]{1,0:T(8,128)(2,1)S(1)} collective-permute-done((bf16[128,640]{1,0:T(8,128)(2,1)S(1)}, bf16[128,640]{1,0:T(8,128)(2,1)S(1)}, u32[]{:S(2)}, u32[]{:S(2)}) %collective-permute-start) | collective-permute-done | bytes 163872 | tf_op jit(solution)/shard_map/ppermute | solution.py:250
  14.2 0.1 collective-permute-start.2
  14.3 1.5 %collective-permute-done.2.rest_1_ = bf16[192,640]{1,0:T(8,128)(2,1)S(1)} collective-permute-done((bf16[192,640]{1,0:T(8,128)(2,1)S(1)}, bf16[192,640]{1,0:T(8,128)(2,1)S(1)}, u32[]{:S(2)}, u32[]{:S(2)}) %collective-permute-start.2) | collective-permute-done | bytes 245792 | tf_op jit(solution)/shard_map/ppermute | solution.py:287
  15.8 4.5 %attend.1 = bf16[128,2048]{1,0:T(8,128)(2,1)} custom-call(bf16[128,4096]{1,0:T(8,128)(2,1)S(1)} %get-tuple-element.17.full, bf16[128,640]{1,0:T(8,128)(2,1)S(1)} %get-tuple-element.13.payload.own, bf16[128,4096]{1,0:T(8,128)(2,1)S(1)} %get-tuple-element.18.expanded, bf16[512,4096]{1,0:T(8,128)(2,1)S(1)} %copy-done, ...), custom_call_target="tpu_custom_call" | custom-call | flops 3221225472 | bytes 7340032 | tf_op jit(solution)/shard_map/attend/pallas_call | solution.py:303
  (2 shorter events, 0.0 us)
Async XLA Ops:
  0.7 4.0 %copy-start = (bf16[512,4096]{1,0:T(8,128)(2,1)S(1)}, bf16[512,4096]{1,0:T(8,128)(2,1)}, u32[]{:S(2)}) copy-start(bf16[512,4096]{1,0:T(8,128)(2,1)} %weight.3) | copy-start | bytes 12582916
  0.7 4.0 %copy-start.1 = (bf16[128,3072]{1,0:T(8,128)(2,1)S(1)}, bf16[128,3072]{1,0:T(8,128)(2,1)}, u32[]{:S(2)}) copy-start(bf16[128,3072]{1,0:T(8,128)(2,1)} %queries.1) | copy-start | bytes 2359300
  0.7 4.0 %copy-start.2 = (f32[4,128,128]{2,1,0:T(8,128)S(1)}, f32[4,128,128]{2,1,0:T(8,128)}, u32[]{:S(2)}) copy-start(f32[4,128,128]{2,1,0:T(8,128)} %constant.5.clone.tables_hbm) | copy-start | bytes 786436
  1.9 12.2 %collective-permute-start = (bf16[128,640]{1,0:T(8,128)(2,1)S(1)}, bf16[128,640]{1,0:T(8,128)(2,1)S(1)}, u32[]{:S(2)}, u32[]{:S(2)}) collective-permute-start(bf16[128,640]{1,0:T(8,128)(2,1)S(1)} %get-tuple-element.13.payload.own), channel_id=1, source_target_pairs={{0,4},{4,8},{8,12},{1,9},{5,13},{2,6},{6,10},{10,14},{3,11},{7,15}... | collective-permute-start | bytes 491528 | tf_op jit(solution)/shard_map/ppermute | solution.py:250
  3.4 9.3 %collective-permute-start.1 = (bf16[64,640]{1,0:T(8,128)(2,1)S(1)}, bf16[64,640]{1,0:T(8,128)(2,1)S(1)}, u32[]{:S(2)}, u32[]{:S(2)}) collective-permute-start(bf16[64,640]{1,0:T(8,128)(2,1)S(1)} %get-tuple-element.14), channel_id=1, source_target_pairs={{0,12},{1,13},{2,14},{3,15},{16,28},{17,29},{18,30},{19,31}} | collective-permute-start | bytes 245768 | tf_op jit(solution)/shard_map/ppermute | solution.py:258
  14.2 1.6 %collective-permute-start.2 = (bf16[192,640]{1,0:T(8,128)(2,1)S(1)}, bf16[192,640]{1,0:T(8,128)(2,1)S(1)}, u32[]{:S(2)}, u32[]{:S(2)}) collective-permute-start(bf16[192,640]{1,0:T(8,128)(2,1)S(1)} %constant_dynamic-update-slice_fusion.rest_0_), channel_id=1, source_target_pairs={{0,1},{1,0},{2,3},{3,2},{4,5},{5,4},{6,7},{7,6},{8,9},{9,8},{10,11... | collective-permute-start | bytes 737288 | tf_op jit(solution)/shard_map/ppermute | solution.py:287

commit v4 on v3

--- a/solution.py
+++ b/solution.py
@@ -17,6 +17,7 @@
 MASKED = -1e30
 MIB = 1024 * 1024
 PACK_FLOPS = 4 * 10**9
+OUT_COPIES = 4
 EXPONENT = math.log2(math.e) / math.sqrt(NOPE + ROPE)
 
 VMEM = pl.BlockSpec(memory_space=pltpu.VMEM)
@@ -109,8 +110,8 @@
 
 
 def attend_kernel(heads, layout, levels, full, own, expanded, weight, *rest):
-    count = len(rest) - 6
-    pieces, (length, out, keys, grown, scores, weights) = rest[:count], rest[count:]
+    count = len(rest) - 8
+    pieces, (length, out_hbm, keys, grown, scores, weights, out, sent) = rest[:count], rest[count:]
     rows = full.shape[0]
     width = weight.shape[0]
     columns = NOPE + VDIM
@@ -118,35 +119,43 @@
     row = lax.broadcasted_iota(jnp.int32, (rows, rows), 0)
     causal = lax.broadcasted_iota(jnp.int32, (rows, rows), 1) <= row
     live = ctx * rows + lax.broadcasted_iota(jnp.int32, (rows, 1), 0) < length[0]
+    stage, buffers = 2, 4
+    block = VDIM * heads // OUT_COPIES
+
+    def leave(k):
+        at = pl.ds(k * block, block)
+        return pltpu.make_async_copy(out.at[:, at], out_hbm.at[:, at], sent.at[k])
 
     def run(total):
         keys[:rows, width:] = own[:, width:]
         spare = (lax.broadcasted_iota(jnp.int32, (1, WIDE), 1) == ROPE).astype(jnp.float32)
         spare = (spare * MASKED).astype(jnp.bfloat16)
         at = rows
-        for which, begin, size, by_core in layout:
+        for which, begin, size, masks in layout:
             if at >= total:
                 break
             ref, piece = pieces[which], slice(begin, begin + size)
             keys[at : at + size, :width] = ref[piece, :width]
-            distance = sum(jnp.where(sub == s, d, 0) for s, d in enumerate(by_core))
+            holders = sum(jnp.where(sub == s, mask, 0) for s, mask in enumerate(masks))
             last = ref[piece, width:]
             keys[at : at + size, width:] = jnp.where(
-                ctx >= distance, last, jnp.broadcast_to(spare, last.shape)
+                lax.shift_right_logical(holders, ctx) & 1 == 1,
+                last,
+                jnp.broadcast_to(spare, last.shape),
             )
             at += size
 
         def grow(i):
             at = slice(2 * columns * i, 2 * columns * (i + 1))
-            grown[i % 3, :rows] = expanded[:, at]
+            grown[i % 4, :rows] = expanded[:, at]
             if total > rows:
-                grown[i % 3, rows:total] = jnp.dot(
+                grown[i % 4, rows:total] = jnp.dot(
                     keys[rows:total, :width], weight[:, at], preferred_element_type=jnp.float32
                 ).astype(jnp.bfloat16)
 
         def score(h):
             i, e = divmod(h, 2)
-            nope = grown[i % 3, :total, columns * e : columns * e + NOPE]
+            nope = grown[i % 4, :total, columns * e : columns * e + NOPE]
             whole = jnp.concatenate([nope, keys[:total, width:]], 1)
             found = lax.dot_general(
                 full[:, FULL * h : FULL * (h + 1)],
@@ -154,45 +163,73 @@
                 (((1,), (1,)), ((), ())),
                 preferred_element_type=jnp.float32,
             )
-            scores[h % 2, :, :rows] = jnp.where(causal, found[:, :rows], MASKED)
+            scores[h % buffers, :, :rows] = jnp.where(causal, found[:, :rows], MASKED)
             if total > rows:
-                scores[h % 2, :, rows:total] = found[:, rows:]
+                scores[h % buffers, :, rows:total] = found[:, rows:]
 
         def soften(h):
-            found = scores[h % 2, :, :total]
+            found = scores[h % buffers, :, :total]
             top = jnp.max(found, 1, keepdims=True)
             raw = jnp.exp2(found * EXPONENT - top * EXPONENT)
-            weights[h % 2, :, :total] = raw.astype(jnp.bfloat16)
+            weights[h % buffers, :, :total] = raw.astype(jnp.bfloat16)
             return jnp.sum(raw, 1, keepdims=True)
 
         def mix(h, total_h):
             i, e = divmod(h, 2)
-            values = grown[i % 3, :total, columns * e + NOPE : columns * (e + 1)]
-            mixed = jnp.dot(weights[h % 2, :, :total], values, preferred_element_type=jnp.float32)
+            values = grown[i % 4, :total, columns * e + NOPE : columns * (e + 1)]
+            mixed = jnp.dot(
+                weights[h % buffers, :, :total], values, preferred_element_type=jnp.float32
+            )
             out[:, VDIM * h : VDIM * (h + 1)] = jnp.where(live, mixed / total_h, 0.0).astype(
                 jnp.bfloat16
             )
+            if (h + 1) % (heads // OUT_COPIES) == 0:
+                leave(h // (heads // OUT_COPIES)).start()
 
         totals = {}
+        steps = heads // stage
         grow(0)
-        for t in range(heads + 2):
-            if t % 2 == 0 and t // 2 + 1 < heads // 2:
-                grow(t // 2 + 1)
-            if t < heads:
-                score(t)
-            if 0 <= t - 1 < heads:
-                totals[t - 1] = soften(t - 1)
-            if 0 <= t - 2 < heads:
-                mix(t - 2, totals.pop(t - 2))
-
-    above = -1
-    for last, total in levels:
-
-        @pl.when((ctx > above) & (ctx <= last))
+        for t in range(steps + 2):
+            if t + 1 < heads // 2:
+                grow(t + 1)
+            for h in range(stage * t, stage * (t + 1)):
+                if t < steps:
+                    score(h)
+            for h in range(stage * (t - 1), stage * t):
+                if 0 <= t - 1 < steps:
+                    totals[h] = soften(h)
+            for h in range(stage * (t - 2), stage * (t - 1)):
+                if 0 <= t - 2 < steps:
+                    mix(h, totals.pop(h))
+
+    for total, places in levels:
+
+        @pl.when(functools.reduce(jnp.logical_or, [ctx == c for c in places]))
         def _():
             run(total)
 
-        above = last
+    for k in range(OUT_COPIES):
+        leave(k).wait()
+
+
+def plan(shards, cores):
+    colours = []
+    for distance in range(shards - 1, 0, -1):
+        for source in range(shards - distance):
+            target = source + distance
+            for colour in colours:
+                if all(source != i and target != j for i, j in colour):
+                    colour.append((source, target))
+                    break
+            else:
+                colours.append([(source, target)])
+    whole = len(colours) // cores * cores
+    sets = [colours[k : k + cores] for k in range(0, whole, cores)]
+    return sets, colours[whole:]
+
+
+def signed(mask):
+    return mask - (1 << 32) if mask >= 1 << 31 else mask
 
 
 def in_hbm(x):
@@ -239,24 +276,16 @@
     )
 
     cores = ("ctx", "sub")
-    whole_sets = (ctx_size - 1) // sub_size
-    direct, distances = [], []
-    for k in range(whole_sets):
+    sets, rest = plan(ctx_size, sub_size)
+    sends = [(payload, by_core) for by_core in sets]
+    sends += [(piece, [edges] * sub_size) for edges in rest]
+    direct, holders = [], []
+    for data, by_core in sends:
         pairs = [
-            (c * sub_size + s, (c + k * sub_size + 1 + s) * sub_size + s)
-            for s in range(sub_size)
-            for c in range(ctx_size - (k * sub_size + 1 + s))
+            (i * sub_size + s, j * sub_size + s) for s, edges in enumerate(by_core) for i, j in edges
         ]
-        direct.append(lax.ppermute(payload, cores, pairs))
-        distances.append([k * sub_size + 1 + s for s in range(sub_size)])
-    for d in range(whole_sets * sub_size + 1, ctx_size):
-        pairs = [
-            (c * sub_size + s, (c + d) * sub_size + s)
-            for c in range(ctx_size - d)
-            for s in range(sub_size)
-        ]
-        direct.append(lax.ppermute(piece, cores, pairs))
-        distances.append([d] * sub_size)
+        direct.append(lax.ppermute(data, cores, pairs))
+        holders.append([sum(1 << j for _, j in edges) for edges in by_core])
 
     expanded, full = pl.pallas_call(
         functools.partial(own_kernel, heads),
@@ -286,30 +315,33 @@
         pairs = [(s, (s + r) % sub_size) for s in range(sub_size)]
         pieces.append(lax.ppermute(together, "sub", pairs))
     layout, begin = [], 0
-    for part, by_core in zip(direct, distances, strict=True):
+    total, need = rows, [rows] * ctx_size
+    for part, masks in zip(direct, holders, strict=True):
+        size = part.shape[0]
         for r in range(sub_size):
-            turned = [by_core[(s - r) % sub_size] for s in range(sub_size)]
-            layout.append((r, begin, part.shape[0], turned))
-        begin += part.shape[0]
-    total = rows + sum(p.shape[0] for p in pieces)
-    levels = [(0, rows)]
-    if whole_sets:
-        levels.append((sub_size, rows * (1 + sub_size)))
-    if levels[-1][0] < ctx_size - 1:
-        levels.append((ctx_size - 1, total))
+            turned = [signed(masks[(s - r) % sub_size]) for s in range(sub_size)]
+            layout.append((r, begin, size, turned))
+        total += size * sub_size
+        begin += size
+        need = [total if any(m >> c & 1 for m in masks) else n for c, n in enumerate(need)]
+    if len(set(need)) > 3:
+        need = [rows] + [total] * (ctx_size - 1)
+    levels = [(t, [c for c in range(ctx_size) if need[c] == t]) for t in sorted(set(need))]
     held = (full, expanded, up_weight, *pieces)
-    scratch = 2 * total * (wide + 6 * (NOPE + VDIM) + 6 * rows)
+    scratch = 2 * total * (wide + 8 * (NOPE + VDIM) + 12 * rows)
 
     return pl.pallas_call(
         functools.partial(attend_kernel, heads, layout, levels),
         in_specs=[VMEM] * (4 + len(pieces)) + [SMEM],
-        out_specs=VMEM,
+        out_specs=ANY,
         out_shape=jax.ShapeDtypeStruct((rows, heads * VDIM), bf16),
         scratch_shapes=[
             pltpu.VMEM((total, wide), bf16),
-            pltpu.VMEM((3, total, 2 * (NOPE + VDIM)), bf16),
-            pltpu.VMEM((2, rows, total), jnp.float32),
-            pltpu.VMEM((2, rows, total), bf16),
+            pltpu.VMEM((4, total, 2 * (NOPE + VDIM)), bf16),
+            pltpu.VMEM((4, rows, total), jnp.float32),
+            pltpu.VMEM((4, rows, total), bf16),
+            pltpu.VMEM((rows, heads * VDIM), bf16),
+            pltpu.SemaphoreType.DMA((OUT_COPIES,)),
         ],
         compiler_params=pltpu.CompilerParams(
             vmem_limit_bytes=6 * MIB + 2 * sum(x.size for x in held) + scratch

time: 20.5 us -> 20.4 us (level)
  Pallas kernels: 6.91 us -> 6.69 us
    pallas_call x1, Pallas kernels: 4.54 us -> 4.33 us  [per_device(): pl.pallas_call(functools.partial(attend_kernel, heads, layout, levels), i...]
  transfers between devices with their start and end apart: 3 -> 3, of which waited for: 3 -> 3; matrix products, arithmetic and copies ran while one was open for 0% -> 0% of each run, Pallas kernels for 5% -> 6%
where the time goes in v4:
time: 20.4 us; the launch traced here: 20.2 us
  waiting for transfers between devices  9.9 us (49%)
  Pallas kernels  6.69 us (33%)
  starting transfers between devices  2.79 us (14%)
  between operations  0.75 us (4%)
    ppermute x2, waiting for transfers between devices, per_device(): direct.append(lax.ppermute(data, cores, pairs))  8.4 us
    pallas_call x1, Pallas kernels, per_device(): pl.pallas_call(functools.partial(attend_kernel, heads, layout, levels), i...  4.33 us
    ppermute x2, starting transfers between devices, per_device(): direct.append(lax.ppermute(data, cores, pairs))  2.72 us
    ppermute x1, waiting for transfers between devices, per_device(): pieces.append(lax.ppermute(together, 'sub', pairs))  1.5 us
    pallas_call x1, Pallas kernels, per_device(): pl.pallas_call(pack_kernel, in_specs=[HBM] * 4 + [SMEM], out_specs=[VMEM]...  1.25 us
    pallas_call x1, Pallas kernels, per_device(): pl.pallas_call(functools.partial(own_kernel, heads), in_specs=[VMEM] * 3...  1.11 us
  transfers between devices with their start and end apart: 3, of which 3 were waited for; matrix products, arithmetic and copies ran while one was open for 0% of the time, Pallas kernels for 6%

profile of v4, /device:TPU:25, one launch (start us, length us, event | category | flops | bytes accessed | tf_op | source)
XLA Modules:
  0.0 20.2 jit_solution(1366624252829940477)
XLA Ops:
  0.7 0.0 copy-start
  0.7 0.0 copy-start.1
  0.7 0.0 copy-start.2
  0.7 1.2 %pack.1 = (bf16[128,640]{1,0:T(8,128)(2,1)S(1)}, bf16[64,640]{1,0:T(8,128)(2,1)S(1)}) custom-call(bf16[128,512]{1,0:T(8,128)(2,1)} %latent_hbm.1, bf16[64,128]{1,0:T(8,128)(2,1)} %bitcast.2, f32[1,512]{1,0:T(1,128)} %bitcast.3, f32[4,64,128]{2,1,0:T(8,128)} %constant.4.clone.tables_hbm, s32[1]{0:T(128)S(6)} %copy.10.length.rest_2_), custom_call_target="tpu_custom_call" | custom-call | flops 4000000000 | bytes 524288 | tf_op jit(solution)/shard_map/pack/pallas_call | solution.py:250
  1.9 1.4 %collective-permute-start = (bf16[128,640]{1,0:T(8,128)(2,1)S(1)}, bf16[128,640]{1,0:T(8,128)(2,1)S(1)}, u32[]{:S(2)}, u32[]{:S(2)}) collective-permute-start(bf16[128,640]{1,0:T(8,128)(2,1)S(1)} %get-tuple-element.13.payload.own), channel_id=1, source_target_pairs={{0,12},{4,8},{1,9},{5,13},{2,14},{6,10},{3,11},{7,15},{16,28},{20,... | collective-permute-start | bytes 491528 | tf_op jit(solution)/shard_map/ppermute | solution.py:287
  3.4 1.3 %collective-permute-start.1 = (bf16[64,640]{1,0:T(8,128)(2,1)S(1)}, bf16[64,640]{1,0:T(8,128)(2,1)S(1)}, u32[]{:S(2)}, u32[]{:S(2)}) collective-permute-start(bf16[64,640]{1,0:T(8,128)(2,1)S(1)} %get-tuple-element.14), channel_id=1, source_target_pairs={{0,4},{8,12},{1,5},{9,13},{2,6},{10,14},{3,7},{11,15},{16,20},{24,... | collective-permute-start | bytes 245768 | tf_op jit(solution)/shard_map/ppermute | solution.py:287
  4.7 0.0 copy-done
  4.7 0.0 copy-done.1
  4.7 0.0 copy-done.2
  4.7 1.1 %own.1 = (bf16[128,4096]{1,0:T(8,128)(2,1)S(1)}, bf16[128,4096]{1,0:T(8,128)(2,1)S(1)}) custom-call(bf16[128,3072]{1,0:T(8,128)(2,1)S(1)} %copy-done.1, bf16[128,640]{1,0:T(8,128)(2,1)S(1)} %get-tuple-element.13.payload.own, bf16[512,4096]{1,0:T(8,128)(2,1)S(1)} %copy-done, f32[4,128,128]{2,1,0:T(8,128)S(1)} %copy-done.2), custom_call_target="tpu_custom_call" | custom-call | flops 536870912 | bytes 7077888 | tf_op jit(solution)/shard_map/own/pallas_call | solution.py:290
  5.8 2.8 %collective-permute-done.1 = bf16[64,640]{1,0:T(8,128)(2,1)S(1)} collective-permute-done((bf16[64,640]{1,0:T(8,128)(2,1)S(1)}, bf16[64,640]{1,0:T(8,128)(2,1)S(1)}, u32[]{:S(2)}, u32[]{:S(2)}) %collective-permute-start.1) | collective-permute-done | bytes 81952 | tf_op jit(solution)/shard_map/ppermute | solution.py:287
  8.6 5.6 %collective-permute-done = bf16[128,640]{1,0:T(8,128)(2,1)S(1)} collective-permute-done((bf16[128,640]{1,0:T(8,128)(2,1)S(1)}, bf16[128,640]{1,0:T(8,128)(2,1)S(1)}, u32[]{:S(2)}, u32[]{:S(2)}) %collective-permute-start) | collective-permute-done | bytes 163872 | tf_op jit(solution)/shard_map/ppermute | solution.py:287
  14.3 0.1 collective-permute-start.2
  14.3 1.5 %collective-permute-done.2.rest_1_ = bf16[192,640]{1,0:T(8,128)(2,1)S(1)} collective-permute-done((bf16[192,640]{1,0:T(8,128)(2,1)S(1)}, bf16[192,640]{1,0:T(8,128)(2,1)S(1)}, u32[]{:S(2)}, u32[]{:S(2)}) %collective-permute-start.2) | collective-permute-done | bytes 245792 | tf_op jit(solution)/shard_map/ppermute | solution.py:316
  15.8 4.3 %attend.1 = bf16[128,2048]{1,0:T(8,128)(2,1)} custom-call(bf16[128,4096]{1,0:T(8,128)(2,1)S(1)} %get-tuple-element.17.full, bf16[128,640]{1,0:T(8,128)(2,1)S(1)} %get-tuple-element.13.payload.own, bf16[128,4096]{1,0:T(8,128)(2,1)S(1)} %get-tuple-element.18.expanded, bf16[512,4096]{1,0:T(8,128)(2,1)S(1)} %copy-done, ...), custom_call_target="tpu_custom_call" | custom-call | flops 3221225472 | bytes 7340032 | tf_op jit(solution)/shard_map/attend/pallas_call | solution.py:333
  (2 shorter events, 0.0 us)
Async XLA Ops:
  0.7 4.0 %copy-start = (bf16[512,4096]{1,0:T(8,128)(2,1)S(1)}, bf16[512,4096]{1,0:T(8,128)(2,1)}, u32[]{:S(2)}) copy-start(bf16[512,4096]{1,0:T(8,128)(2,1)} %weight.3) | copy-start | bytes 12582916
  0.7 4.0 %copy-start.1 = (bf16[128,3072]{1,0:T(8,128)(2,1)S(1)}, bf16[128,3072]{1,0:T(8,128)(2,1)}, u32[]{:S(2)}) copy-start(bf16[128,3072]{1,0:T(8,128)(2,1)} %queries.1) | copy-start | bytes 2359300
  0.7 4.0 %copy-start.2 = (f32[4,128,128]{2,1,0:T(8,128)S(1)}, f32[4,128,128]{2,1,0:T(8,128)}, u32[]{:S(2)}) copy-start(f32[4,128,128]{2,1,0:T(8,128)} %constant.5.clone.tables_hbm) | copy-start | bytes 786436
  1.9 12.3 %collective-permute-start = (bf16[128,640]{1,0:T(8,128)(2,1)S(1)}, bf16[128,640]{1,0:T(8,128)(2,1)S(1)}, u32[]{:S(2)}, u32[]{:S(2)}) collective-permute-start(bf16[128,640]{1,0:T(8,128)(2,1)S(1)} %get-tuple-element.13.payload.own), channel_id=1, source_target_pairs={{0,12},{4,8},{1,9},{5,13},{2,14},{6,10},{3,11},{7,15},{16,28},{20,... | collective-permute-start | bytes 491528 | tf_op jit(solution)/shard_map/ppermute | solution.py:287
  3.4 5.2 %collective-permute-start.1 = (bf16[64,640]{1,0:T(8,128)(2,1)S(1)}, bf16[64,640]{1,0:T(8,128)(2,1)S(1)}, u32[]{:S(2)}, u32[]{:S(2)}) collective-permute-start(bf16[64,640]{1,0:T(8,128)(2,1)S(1)} %get-tuple-element.14), channel_id=1, source_target_pairs={{0,4},{8,12},{1,5},{9,13},{2,6},{10,14},{3,7},{11,15},{16,20},{24,... | collective-permute-start | bytes 245768 | tf_op jit(solution)/shard_map/ppermute | solution.py:287
  14.3 1.6 %collective-permute-start.2 = (bf16[192,640]{1,0:T(8,128)(2,1)S(1)}, bf16[192,640]{1,0:T(8,128)(2,1)S(1)}, u32[]{:S(2)}, u32[]{:S(2)}) collective-permute-start(bf16[192,640]{1,0:T(8,128)(2,1)S(1)} %constant_dynamic-update-slice_fusion.rest_0_), channel_id=1, source_target_pairs={{0,1},{1,0},{2,3},{3,2},{4,5},{5,4},{6,7},{7,6},{8,9},{9,8},{10,11... | collective-permute-start | bytes 737288 | tf_op jit(solution)/shard_map/ppermute | solution.py:316

commit v5 on v4

v5 whole, which is shorter than its diff:
```python
import functools
import math

import jax
import jax.numpy as jnp
import numpy as np
from jax import lax
from jax.experimental import pallas as pl
from jax.experimental.pallas import tpu as pltpu
from jax.sharding import PartitionSpec as P

ROPE = 64
NOPE = 128
VDIM = 128
WIDE = 128
FULL = 256
MASKED = -1e30
MIB = 1024 * 1024
PACK_FLOPS = 4 * 10**9
OUT_COPIES = 4
EXPONENT = math.log2(math.e) / math.sqrt(NOPE + ROPE)

VMEM = pl.BlockSpec(memory_space=pltpu.VMEM)
SMEM = pl.BlockSpec(memory_space=pltpu.SMEM)
HBM = pl.BlockSpec(memory_space=pltpu.HBM)
ANY = pl.BlockSpec(memory_space=pl.ANY)


def tables(positions):
    half = ROPE // 2
    frequency = np.float32(10000.0) ** (-np.arange(half, dtype=np.float32) / np.float32(half))
    angles = np.arange(positions, dtype=np.float32)[:, None] * frequency.astype(np.float32)
    cosines, sines = np.cos(angles), np.sin(angles)
    rows = np.concatenate([cosines, cosines, -sines, sines], 1).astype(np.float32)
    columns = np.concatenate([cosines, sines], 1).T.astype(np.float32)
    return rows, np.ascontiguousarray(columns)


def normalise(latent, gain):
    wide = latent.astype(jnp.float32)
    mean = jnp.mean(wide * wide, -1, keepdims=True)
    return (wide * lax.rsqrt(mean + 1e-06) * gain).astype(jnp.bfloat16)


def last_tile(rope, table, start, live):
    half = ROPE // 2
    keys = rope.astype(jnp.float32)
    low, high = keys[:half], keys[half:]
    cosines, sines = table[:half], table[half:]
    rotated = jnp.concatenate([low * cosines - high * sines, low * sines + high * cosines], 0)
    shape = (WIDE - ROPE, rope.shape[1])
    position = start + lax.broadcasted_iota(jnp.int32, shape, 1)
    first = lax.broadcasted_iota(jnp.int32, shape, 0) == 0
    bias = jnp.where(first & (position >= live), MASKED, 0.0)
    return jnp.concatenate([rotated, bias], 0).T.astype(jnp.bfloat16)


def spare_tile(rows):
    lane = lax.broadcasted_iota(jnp.int32, (rows, WIDE), 1)
    return jnp.where(lane == ROPE, MASKED, 0.0).astype(jnp.bfloat16)


def pack_kernel(
    latent_hbm, rope_hbm, gain_hbm, tables_hbm, length, payload, piece, latent, rope, gain, table, arrived
):
    rows, width = latent.shape
    ctx, sub = lax.axis_index("ctx"), lax.axis_index("sub")
    copies = [
        pltpu.make_async_copy(source, target, arrived.at[k])
        for k, (source, target) in enumerate(
            [(latent_hbm, latent), (gain_hbm, gain), (rope_hbm, rope), (tables_hbm.at[ctx], table)]
        )
    ]
    for copy in copies:
        copy.start()
    for copy in copies:
        copy.wait()
    normed = normalise(latent[...], gain[...])
    extra = last_tile(rope[...], table[...], ctx * rows, length[0])
    payload[:, :width] = normed
    payload[:, width:] = extra
    size = piece.shape[0]
    for k in range(rows // size):

        @pl.when(sub == k)
        def _():
            piece[:, :width] = normed[k * size : (k + 1) * size]
            piece[:, width:] = extra[k * size : (k + 1) * size]


def pick(sub, values):
    return sum(jnp.where(sub == s, value, 0) for s, value in enumerate(values))


def holds(sub, ctx, masks):
    return lax.shift_right_logical(pick(sub, masks), ctx) & 1 == 1


def mid_kernel(sources, masks, piece_masks, gain, tables, length, *rest):
    count = len(sources)
    latents, ropes, pieces = rest[:count], rest[count : 2 * count], rest[2 * count : -1]
    together = rest[-1]
    ctx, sub = lax.axis_index("ctx"), lax.axis_index("sub")
    at = 0
    for latent, rope, source, mask in zip(latents, ropes, sources, masks, strict=True):
        rows, width = latent.shape
        origin = sum(
            jnp.where((sub == s) & (ctx == j), i, 0)
            for s, edges in enumerate(source)
            for i, j in edges
        )
        together[at : at + rows, :width] = normalise(latent[...], gain[...])
        tile = last_tile(rope[...], tables[origin], origin * rows, length[0])
        together[at : at + rows, width:] = jnp.where(holds(sub, ctx, mask), tile, spare_tile(rows))
        at += rows
    for piece, mask in zip(pieces, piece_masks, strict=True):
        size, width = piece.shape[0], piece.shape[1] - WIDE
        together[at : at + size, :width] = piece[:, :width]
        together[at : at + size, width:] = jnp.where(
            holds(sub, ctx, mask), piece[:, width:], spare_tile(size)
        )
        at += size


def grow_kernel(step, together, weight, grown):
    width = weight.shape[0]

    @pl.when(lax.axis_index("ctx") > 0)
    def _():
        for k in range(weight.shape[1] // step):
            at = slice(k * step, (k + 1) * step)
            grown[:, at] = jnp.dot(
                together[:, :width], weight[:, at], preferred_element_type=jnp.float32
            ).astype(jnp.bfloat16)


def own_kernel(heads, queries, payload, weight, tables_hbm, expanded, full, table, arrived):
    copy = pltpu.make_async_copy(tables_hbm.at[lax.axis_index("ctx")], table, arrived)
    copy.start()
    copy.wait()
    rows = queries.shape[0]
    width = weight.shape[0]
    cosines = jnp.concatenate([table[:, :ROPE]] * 2, 1)
    sines = jnp.concatenate([table[:, ROPE:]] * 2, 1)
    lane = lax.broadcasted_iota(jnp.int32, (rows, 2 * ROPE), 1)
    lower = lane % ROPE < ROPE // 2
    tail = (lax.broadcasted_iota(jnp.int32, (rows, FULL - NOPE - ROPE), 1) == 0).astype(
        jnp.float32
    ).astype(jnp.bfloat16)
    each = NOPE + ROPE
    for i in range(heads // 2):
        pair = queries[:, 2 * each * i : 2 * each * (i + 1)]
        ropes = jnp.concatenate([pair[:, NOPE:each], pair[:, each + NOPE :]], 1).astype(jnp.float32)
        turned = jnp.where(
            lower, pltpu.roll(ropes, 2 * ROPE - ROPE // 2, 1), pltpu.roll(ropes, ROPE // 2, 1)
        )
        ropes = (ropes * cosines + turned * sines).astype(jnp.bfloat16)
        for e in range(2):
            at = FULL * (2 * i + e)
            full[:, at : at + NOPE] = pair[:, each * e : each * e + NOPE]
            full[:, at + NOPE : at + FULL] = jnp.concatenate(
                [ropes[:, ROPE * e : ROPE * (e + 1)], tail], 1
            )
    columns = NOPE + VDIM
    for i in range(heads // 2):
        at = slice(2 * columns * i, 2 * columns * (i + 1))
        expanded[:, at] = jnp.dot(
            payload[:, :width], weight[:, at], preferred_element_type=jnp.float32
        ).astype(jnp.bfloat16)


def attend_kernel(heads, sets, levels, full, own, expanded, weight, together, fetched, *rest):
    swapped = rest[:-7]
    length, out_hbm, grown, scores, weights, out, sent = rest[-7:]
    rows = full.shape[0]
    width = weight.shape[0]
    columns = NOPE + VDIM
    ctx = lax.axis_index("ctx")
    row = lax.broadcasted_iota(jnp.int32, (rows, rows), 0)
    causal = lax.broadcasted_iota(jnp.int32, (rows, rows), 1) <= row
    live = ctx * rows + lax.broadcasted_iota(jnp.int32, (rows, 1), 0) < length[0]
    stage, buffers = 2, 4
    block = VDIM * heads // OUT_COPIES

    def leave(k):
        at = pl.ds(k * block, block)
        return pltpu.make_async_copy(out.at[:, at], out_hbm.at[:, at], sent.at[k])

    def run(level):
        every = together.shape[0]
        part = (0, sets, every)[level]
        total = rows + part * (1 + len(swapped))

        def rows_of(own_part, direct_part, swapped_part):
            found = [own_part()]
            for begin, end in ((0, sets), (sets, every)):
                if begin < end <= part:
                    found.append(direct_part(slice(begin, end)))
                    for r in range(len(swapped)):
                        found.append(swapped_part(r, slice(begin, end)))
            return found[0] if len(found) == 1 else jnp.concatenate(found, 0)

        def grow(i):
            at = slice(2 * columns * i, 2 * columns * (i + 1))
            for r, ref in enumerate(swapped):
                if part:
                    grown[i % 4, r, :part] = jnp.dot(
                        ref[:part, :width], weight[:, at], preferred_element_type=jnp.float32
                    ).astype(jnp.bfloat16)

        def column(h, begin, end):
            i, e = divmod(h, 2)
            return rows_of(
                lambda: expanded[:, columns * h + begin : columns * h + end],
                lambda piece: fetched[piece, columns * h + begin : columns * h + end],
                lambda r, piece: grown[i % 4, r, piece, columns * e + begin : columns * e + end],
            )

        def score(h):
            last = rows_of(
                lambda: own[:, width:],
                lambda piece: together[piece, width:],
                lambda r, piece: swapped[r][piece, width:],
            )
            found = lax.dot_general(
                full[:, FULL * h : FULL * (h + 1)],
                jnp.concatenate([column(h, 0, NOPE), last], 1),
                (((1,), (1,)), ((), ())),
                preferred_element_type=jnp.float32,
            )
            scores[h % buffers, :, :rows] = jnp.where(causal, found[:, :rows], MASKED)
            if total > rows:
                scores[h % buffers, :, rows:total] = found[:, rows:]

        def soften(h):
            found = scores[h % buffers, :, :total]
            top = jnp.max(found, 1, keepdims=True)
            raw = jnp.exp2(found * EXPONENT - top * EXPONENT)
            weights[h % buffers, :, :total] = raw.astype(jnp.bfloat16)
            return jnp.sum(raw, 1, keepdims=True)

        def mix(h, total_h):
            mixed = jnp.dot(
                weights[h % buffers, :, :total],
                column(h, NOPE, columns),
                preferred_element_type=jnp.float32,
            )
            out[:, VDIM * h : VDIM * (h + 1)] = jnp.where(live, mixed / total_h, 0.0).astype(
                jnp.bfloat16
            )
            if (h + 1) % (heads // OUT_COPIES) == 0:
                leave(h // (heads // OUT_COPIES)).start()

        totals = {}
        steps = heads // stage
        grow(0)
        for t in range(steps + 2):
            if t + 1 < heads // 2:
                grow(t + 1)
            for h in range(stage * t, stage * (t + 1)):
                if t < steps:
                    score(h)
            for h in range(stage * (t - 1), stage * t):
                if 0 <= t - 1 < steps:
                    totals[h] = soften(h)
            for h in range(stage * (t - 2), stage * (t - 1)):
                if 0 <= t - 2 < steps:
                    mix(h, totals.pop(h))

    for level, places in levels:

        @pl.when(functools.reduce(jnp.logical_or, [ctx == c for c in places]))
        def _():
            run(level)

    for k in range(OUT_COPIES):
        leave(k).wait()


def plan(shards, cores):
    colours = []
    for distance in range(shards - 1, 0, -1):
        for source in range(shards - distance):
            target = source + distance
            for colour in colours:
                if all(source != i and target != j for i, j in colour):
                    colour.append((source, target))
                    break
            else:
                colours.append([(source, target)])
    whole = len(colours) // cores * cores
    sets = [colours[k : k + cores] for k in range(0, whole, cores)]
    return sets, colours[whole:]


def signed(mask):
    return mask - (1 << 32) if mask >= 1 << 31 else mask


def in_hbm(x):
    return pltpu.with_memory_space_constraint(x, pltpu.HBM)


def grant(*arrays):
    return pltpu.CompilerParams(vmem_limit_bytes=4 * MIB + 2 * sum(x.size for x in arrays))


def per_device(
    ctx_size, sub_size, queries, latent, rope_keys, latent_gain, up_weight, prompt_length
):
    rows, width = latent.shape
    heads = up_weight.shape[1] // (NOPE + VDIM)
    by_row, by_column = tables(ctx_size * rows)
    by_row = jnp.asarray(by_row.reshape(ctx_size, rows, 2 * ROPE))
    by_column = jnp.asarray(by_column.reshape(ROPE, ctx_size, rows).transpose(1, 0, 2))
    gain = latent_gain.reshape(1, width)
    turned = rope_keys.T
    bf16 = jnp.bfloat16
    wide = width + WIDE

    cores = ("ctx", "sub")
    sets, rest = plan(ctx_size, sub_size)

    def send(data, by_core):
        pairs = [
            (i * sub_size + s, j * sub_size + s) for s, edges in enumerate(by_core) for i, j in edges
        ]
        return lax.ppermute(data, cores, pairs)

    def receivers(by_core):
        return [signed(sum(1 << j for _, j in edges)) for edges in by_core]

    latents = [send(latent, by_core) for by_core in sets]
    ropes = [send(turned, by_core) for by_core in sets]

    payload, piece = pl.pallas_call(
        pack_kernel,
        in_specs=[HBM] * 4 + [SMEM],
        out_specs=[VMEM] * 2,
        out_shape=[
            jax.ShapeDtypeStruct((rows, wide), bf16),
            jax.ShapeDtypeStruct((rows // sub_size, wide), bf16),
        ],
        scratch_shapes=[
            pltpu.VMEM((rows, width), bf16),
            pltpu.VMEM((ROPE, rows), bf16),
            pltpu.VMEM((1, width), jnp.float32),
            pltpu.VMEM((ROPE, rows), jnp.float32),
            pltpu.SemaphoreType.DMA((4,)),
        ],
        cost_estimate=pl.CostEstimate(
            flops=PACK_FLOPS, bytes_accessed=8 * rows * width, transcendentals=0
        ),
        compiler_params=grant(),
        name="pack",
    )(in_hbm(latent), in_hbm(turned), in_hbm(gain), in_hbm(by_column), prompt_length)

    pieces = [send(piece, [edges] * sub_size) for edges in rest]

    expanded, full = pl.pallas_call(
        functools.partial(own_kernel, heads),
        in_specs=[VMEM] * 3 + [ANY],
        out_specs=[VMEM] * 2,
        out_shape=[
            jax.ShapeDtypeStruct((rows, up_weight.shape[1]), bf16),
            jax.ShapeDtypeStruct((rows, heads * FULL), bf16),
        ],
        scratch_shapes=[pltpu.VMEM((rows, 2 * ROPE), jnp.float32), pltpu.SemaphoreType.DMA],
        compiler_params=grant(queries, up_weight, payload, up_weight[:rows], up_weight[:rows]),
        name="own",
        cost_estimate=pl.CostEstimate(
            flops=2 * rows * width * up_weight.shape[1],
            bytes_accessed=2 * (queries.size + up_weight.size + 2 * rows * up_weight.shape[1]),
            transcendentals=0,
        ),
    )(queries, payload, up_weight, by_row)

    latents, ropes, pieces, expanded, full = lax.optimization_barrier(
        (latents, ropes, pieces, expanded, full)
    )
    reach = sum(x.shape[0] for x in (*latents, *pieces))
    whole = sum(x.shape[0] for x in latents)
    together = pl.pallas_call(
        functools.partial(
            mid_kernel,
            sets,
            [receivers(by_core) for by_core in sets],
            [receivers([edges] * sub_size) for edges in rest],
        ),
        in_specs=[VMEM] * 2 + [SMEM] + [VMEM] * (2 * len(latents) + len(pieces)),
        out_specs=VMEM,
        out_shape=jax.ShapeDtypeStruct((reach, wide), bf16),
        compiler_params=grant(by_column, by_column, *latents, *ropes, *pieces, *pieces, *latents),
        name="mid",
    )(gain, by_column, prompt_length, *latents, *ropes, *pieces)

    swapped = []
    for r in range(1, sub_size):
        pairs = [(s, (s + r) % sub_size) for s in range(sub_size)]
        swapped.append(lax.ppermute(together, "sub", pairs))

    fetched = pl.pallas_call(
        functools.partial(grow_kernel, 4 * (NOPE + VDIM)),
        in_specs=[VMEM] * 2,
        out_specs=VMEM,
        out_shape=jax.ShapeDtypeStruct((reach, up_weight.shape[1]), bf16),
        compiler_params=pltpu.CompilerParams(
            vmem_limit_bytes=4 * MIB
            + 2 * (up_weight.size + reach * (wide + up_weight.shape[1]))
        ),
        name="grow",
        cost_estimate=pl.CostEstimate(
            flops=2 * reach * width * up_weight.shape[1],
            bytes_accessed=2 * (up_weight.size + reach * up_weight.shape[1]),
            transcendentals=0,
        ),
    )(together, up_weight)

    needs = [0] * ctx_size
    for level, groups in ((1, [e for by_core in sets for e in by_core]), (2, rest)):
        for edges in groups:
            for _, j in edges:
                needs[j] = level
    levels = [(k, [c for c in range(ctx_size) if needs[c] == k]) for k in sorted(set(needs))]
    total = rows + sub_size * reach
    held = 2 * (up_weight.size + (reach + 2 * rows) * up_weight.shape[1] + total * wide)
    scratch = 8 * total * (NOPE + VDIM) * 2 + 24 * rows * total + 2 * rows * heads * VDIM
    return pl.pallas_call(
        functools.partial(attend_kernel, heads, whole, levels),
        in_specs=[VMEM] * (6 + len(swapped)) + [SMEM],
        out_specs=ANY,
        out_shape=jax.ShapeDtypeStruct((rows, heads * VDIM), bf16),
        scratch_shapes=[
            pltpu.VMEM((4, len(swapped), reach, 2 * (NOPE + VDIM)), bf16),
            pltpu.VMEM((4, rows, total), jnp.float32),
            pltpu.VMEM((4, rows, total), bf16),
            pltpu.VMEM((rows, heads * VDIM), bf16),
            pltpu.SemaphoreType.DMA((OUT_COPIES,)),
        ],
        compiler_params=pltpu.CompilerParams(vmem_limit_bytes=6 * MIB + held + scratch),
        name="attend",
        cost_estimate=pl.CostEstimate(
            flops=2 * total * (width + 2 * rows) * up_weight.shape[1],
            bytes_accessed=2 * (up_weight.size + 3 * rows * up_weight.shape[1]),
            transcendentals=heads * rows * total,
        ),
    )(full, payload, expanded, up_weight, together, fetched, *swapped, prompt_length)


def solution(mesh):
    placed = (
        P(("parts", "ctx"), ("head", "sub")),
        P(("parts", "ctx"), None),
        P(("parts", "ctx"), None),
        P(),
        P(None, ("head", "sub")),
        P("parts"),
    )
    return jax.shard_map(
        functools.partial(per_device, mesh.shape["ctx"], mesh.shape["sub"]),
        mesh=mesh,
        in_specs=placed,
        out_specs=P(("parts", "ctx"), ("head", "sub")),
        check_vma=False,
    )
```

time: 20.4 us -> 18.4 us (0.902)
  waiting for transfers between devices: 9.9 us -> 5.05 us
  starting transfers between devices: 2.79 us -> 5.28 us
  Pallas kernels: 6.69 us -> 7.07 us
    ppermute x3 -> x4, waiting for transfers between devices: 9.9 us -> 5.05 us  [the longest x3 4.91 us: send(): return lax.ppermute(data, cores, pairs)]
    ppermute x3 -> x4, starting transfers between devices: 2.79 us -> 5.28 us  [the longest x3 4 us: send(): return lax.ppermute(data, cores, pairs)]
    pallas_call x1 -> x3, Pallas kernels: 4.33 us -> 4.72 us  [the longest x1 3.58 us: per_device(): pl.pallas_call(functools.partial(attend_kernel, heads, whole, levels), in...]
  transfers between devices with their start and end apart: 3 -> 4, of which waited for: 3 -> 3; matrix products, arithmetic and copies ran while one was open for 0% -> 0% of each run, Pallas kernels for 6% -> 18%
where the time goes in v5:
time: 18.4 us; the launch traced here: 18.2 us
  Pallas kernels  7.07 us (38%)
  starting transfers between devices  5.28 us (29%)
  waiting for transfers between devices  5.05 us (27%)
  between operations  0.78 us (4%)
    ppermute x3, waiting for transfers between devices, send(): return lax.ppermute(data, cores, pairs)  4.91 us
    ppermute x3, starting transfers between devices, send(): return lax.ppermute(data, cores, pairs)  4 us
    pallas_call x1, Pallas kernels, per_device(): pl.pallas_call(functools.partial(attend_kernel, heads, whole, levels), in...  3.58 us
    ppermute x1, starting transfers between devices, per_device(): swapped.append(lax.ppermute(together, 'sub', pairs))  1.28 us
    pallas_call x1, Pallas kernels, per_device(): pl.pallas_call(pack_kernel, in_specs=[HBM] * 4 + [SMEM], out_specs=[VMEM]...  1.25 us
    pallas_call x1, Pallas kernels, per_device(): pl.pallas_call(functools.partial(own_kernel, heads), in_specs=[VMEM] * 3...  1.1 us
    pallas_call x1, Pallas kernels, per_device(): pl.pallas_call(functools.partial(grow_kernel, 4 * (NOPE + VDIM)), in_spec...  0.99 us
  transfers between devices with their start and end apart: 4, of which 3 were waited for; matrix products, arithmetic and copies ran while one was open for 0% of the time, Pallas kernels for 18%

profile of v5, /device:TPU:25, one launch (start us, length us, event | category | flops | bytes accessed | tf_op | source)
XLA Modules:
  0.0 18.2 jit_solution(1664559153840847090)
XLA Ops:
  0.0 1.3 %collective-permute-start = (bf16[128,512]{1,0:T(8,128)(2,1)}, bf16[128,512]{1,0:T(8,128)(2,1)S(1)}, u32[]{:S(2)}, u32[]{:S(2)}) collective-permute-start(bf16[128,512]{1,0:T(8,128)(2,1)} %latent_hbm.1), channel_id=1, source_target_pairs={{0,12},{4,8},{1,9},{5,13},{2,14},{6,10},{3,11},{7,15},{16,28},{20,... | collective-permute-start | bytes 393224 | tf_op jit(solution)/shard_map/ppermute | solution.py:328
  1.9 0.0 copy-start.5
  1.9 0.0 copy-start
  2.0 0.0 copy-start.1
  2.0 0.0 copy-start.2
  2.0 1.2 %pack.1 = (bf16[128,640]{1,0:T(8,128)(2,1)S(1)}, bf16[64,640]{1,0:T(8,128)(2,1)S(1)}) custom-call(bf16[128,512]{1,0:T(8,128)(2,1)} %latent_hbm.1, bf16[64,128]{1,0:T(8,128)(2,1)} %bitcast.4, f32[1,512]{1,0:T(1,128)} %bitcast.2, f32[4,64,128]{2,1,0:T(8,128)} %constant.5.clone.tables_hbm.tables, s32[1]{0:T(128)S(6)} %copy.9.length.rest_1_), custom_call_target="tpu_custom_call" | custom-call | flops 4000000000 | bytes 524288 | tf_op jit(solution)/shard_map/pack/pallas_call | solution.py:336
  3.2 0.0 copy-start.3
  3.2 0.0 copy-start.4
  3.3 1.4 %collective-permute-start.2 = (bf16[64,640]{1,0:T(8,128)(2,1)S(1)}, bf16[64,640]{1,0:T(8,128)(2,1)S(1)}, u32[]{:S(2)}, u32[]{:S(2)}) collective-permute-start(bf16[64,640]{1,0:T(8,128)(2,1)S(1)} %get-tuple-element.14), channel_id=1, source_target_pairs={{0,4},{8,12},{1,5},{9,13},{2,6},{10,14},{3,7},{11,15},{16,20},{24,... | collective-permute-start | bytes 245768 | tf_op jit(solution)/shard_map/ppermute | solution.py:328
  4.7 0.0 copy-done.5
  4.7 1.3 %collective-permute-start.1 = (bf16[64,128]{1,0:T(8,128)(2,1)S(1)}, bf16[64,128]{1,0:T(8,128)(2,1)S(1)}, u32[]{:S(2)}, u32[]{:S(2)}) collective-permute-start(bf16[64,128]{1,0:T(8,128)(2,1)S(1)} %bitcast.5), channel_id=1, source_target_pairs={{0,12},{4,8},{1,9},{5,13},{2,14},{6,10},{3,11},{7,15},{16,28},{20,... | collective-permute-start | bytes 49160 | tf_op jit(solution)/shard_map/ppermute | solution.py:328
  6.0 0.0 copy-done
  6.0 0.0 copy-done.1
  6.0 0.0 copy-done.2
  6.0 1.1 %own.1 = (bf16[128,4096]{1,0:T(8,128)(2,1)S(1)}, bf16[128,4096]{1,0:T(8,128)(2,1)S(1)}) custom-call(bf16[128,3072]{1,0:T(8,128)(2,1)S(1)} %copy-done.1, bf16[128,640]{1,0:T(8,128)(2,1)S(1)} %get-tuple-element.15.payload.own, bf16[512,4096]{1,0:T(8,128)(2,1)S(1)} %copy-done, f32[4,128,128]{2,1,0:T(8,128)S(1)} %copy-done.2), custom_call_target="tpu_custom_call" | custom-call | flops 536870912 | bytes 7077888 | tf_op jit(solution)/shard_map/own/pallas_call | solution.py:360
  7.1 3.9 %collective-permute-done.1.rest_1_ = bf16[64,128]{1,0:T(8,128)(2,1)S(1)} collective-permute-done((bf16[64,128]{1,0:T(8,128)(2,1)S(1)}, bf16[64,128]{1,0:T(8,128)(2,1)S(1)}, u32[]{:S(2)}, u32[]{:S(2)}) %collective-permute-start.1) | collective-permute-done | bytes 16416 | tf_op jit(solution)/shard_map/ppermute | solution.py:328
  11.1 1.0 %collective-permute-done.2.rest_2_ = bf16[64,640]{1,0:T(8,128)(2,1)S(1)} collective-permute-done((bf16[64,640]{1,0:T(8,128)(2,1)S(1)}, bf16[64,640]{1,0:T(8,128)(2,1)S(1)}, u32[]{:S(2)}, u32[]{:S(2)}) %collective-permute-start.2) | collective-permute-done | bytes 81952 | tf_op jit(solution)/shard_map/ppermute | solution.py:328
  12.0 0.0 collective-permute-done.rest_0_
  12.1 0.0 copy-done.3
  12.1 0.0 copy-done.4
  12.1 0.1 mid.1.together
  12.2 1.3 %collective-permute-start.3 = (bf16[192,640]{1,0:T(8,128)(2,1)S(1)}, bf16[192,640]{1,0:T(8,128)(2,1)S(1)}, u32[]{:S(2)}, u32[]{:S(2)}) collective-permute-start(bf16[192,640]{1,0:T(8,128)(2,1)S(1)} %mid.1.together), channel_id=1, source_target_pairs={{0,1},{1,0},{2,3},{3,2},{4,5},{5,4},{6,7},{7,6},{8,9},{9,8},{10,11... | collective-permute-start | bytes 737288 | tf_op jit(solution)/shard_map/ppermute | solution.py:400
  13.5 1.0 %grow.1.fetched = bf16[192,4096]{1,0:T(8,128)(2,1)S(1)} custom-call(bf16[192,640]{1,0:T(8,128)(2,1)S(1)} %mid.1.together, bf16[512,4096]{1,0:T(8,128)(2,1)S(1)} %copy-done), custom_call_target="tpu_custom_call" | custom-call | flops 805306368 | bytes 5767168 | tf_op jit(solution)/shard_map/grow/pallas_call | solution.py:402
  14.5 0.1 collective-permute-done.3.rest_0_
  14.6 3.6 %attend.1 = bf16[128,2048]{1,0:T(8,128)(2,1)} custom-call(bf16[128,4096]{1,0:T(8,128)(2,1)S(1)} %get-tuple-element.18.full, bf16[128,640]{1,0:T(8,128)(2,1)S(1)} %get-tuple-element.15.payload.own, bf16[128,4096]{1,0:T(8,128)(2,1)S(1)} %get-tuple-element.19.expanded, bf16[512,4096]{1,0:T(8,128)(2,1)S(1)} %copy-done, bf16[192,640]{1,0:T(8,128)(2,1)S(1)} %mid.1.together, ...), custom_call_target="tpu_custom_call" | custom-call | flops 3221225472 | bytes 7340032 | tf_op jit(solution)/shard_map/attend/pallas_call | solution.py:428
Async XLA Ops:
  0.0 12.1 %collective-permute-start = (bf16[128,512]{1,0:T(8,128)(2,1)}, bf16[128,512]{1,0:T(8,128)(2,1)S(1)}, u32[]{:S(2)}, u32[]{:S(2)}) collective-permute-start(bf16[128,512]{1,0:T(8,128)(2,1)} %latent_hbm.1), channel_id=1, source_target_pairs={{0,12},{4,8},{1,9},{5,13},{2,14},{6,10},{3,11},{7,15},{16,28},{20,... | collective-permute-start | bytes 393224 | tf_op jit(solution)/shard_map/ppermute | solution.py:328
  1.9 2.8 %copy-start.5 = (bf16[128,64]{0,1:T(8,128)(2,1)S(1)}, bf16[128,64]{0,1:T(8,128)(2,1)}, u32[]{:S(2)}) copy-start(bf16[128,64]{0,1:T(8,128)(2,1)} %param.10) | copy-start | bytes 49156
  1.9 4.1 %copy-start = (bf16[512,4096]{1,0:T(8,128)(2,1)S(1)}, bf16[512,4096]{1,0:T(8,128)(2,1)}, u32[]{:S(2)}) copy-start(bf16[512,4096]{1,0:T(8,128)(2,1)} %weight.5) | copy-start | bytes 12582916
  2.0 4.1 %copy-start.1 = (bf16[128,3072]{1,0:T(8,128)(2,1)S(1)}, bf16[128,3072]{1,0:T(8,128)(2,1)}, u32[]{:S(2)}) copy-start(bf16[128,3072]{1,0:T(8,128)(2,1)} %queries.1) | copy-start | bytes 2359300
  2.0 4.1 %copy-start.2 = (f32[4,128,128]{2,1,0:T(8,128)S(1)}, f32[4,128,128]{2,1,0:T(8,128)}, u32[]{:S(2)}) copy-start(f32[4,128,128]{2,1,0:T(8,128)} %constant.4.clone.tables_hbm) | copy-start | bytes 786436
  3.2 8.8 %copy-start.3 = (f32[4,64,128]{2,1,0:T(8,128)S(1)}, f32[4,64,128]{2,1,0:T(8,128)}, u32[]{:S(2)}) copy-start(f32[4,64,128]{2,1,0:T(8,128)} %constant.5.clone.tables_hbm.tables) | copy-start | bytes 393220
  3.2 8.8 %copy-start.4 = (f32[512]{0:T(512)S(1)}, f32[512]{0:T(512)}, u32[]{:S(2)}) copy-start(f32[512]{0:T(512)} %param.11) | copy-start | bytes 6148
  3.3 8.8 %collective-permute-start.2 = (bf16[64,640]{1,0:T(8,128)(2,1)S(1)}, bf16[64,640]{1,0:T(8,128)(2,1)S(1)}, u32[]{:S(2)}, u32[]{:S(2)}) collective-permute-start(bf16[64,640]{1,0:T(8,128)(2,1)S(1)} %get-tuple-element.14), channel_id=1, source_target_pairs={{0,4},{8,12},{1,5},{9,13},{2,6},{10,14},{3,7},{11,15},{16,20},{24,... | collective-permute-start | bytes 245768 | tf_op jit(solution)/shard_map/ppermute | solution.py:328
  4.7 6.4 %collective-permute-start.1 = (bf16[64,128]{1,0:T(8,128)(2,1)S(1)}, bf16[64,128]{1,0:T(8,128)(2,1)S(1)}, u32[]{:S(2)}, u32[]{:S(2)}) collective-permute-start(bf16[64,128]{1,0:T(8,128)(2,1)S(1)} %bitcast.5), channel_id=1, source_target_pairs={{0,12},{4,8},{1,9},{5,13},{2,14},{6,10},{3,11},{7,15},{16,28},{20,... | collective-permute-start | bytes 49160 | tf_op jit(solution)/shard_map/ppermute | solution.py:328
  12.2 2.4 %collective-permute-start.3 = (bf16[192,640]{1,0:T(8,128)(2,1)S(1)}, bf16[192,640]{1,0:T(8,128)(2,1)S(1)}, u32[]{:S(2)}, u32[]{:S(2)}) collective-permute-start(bf16[192,640]{1,0:T(8,128)(2,1)S(1)} %mid.1.together), channel_id=1, source_target_pairs={{0,1},{1,0},{2,3},{3,2},{4,5},{5,4},{6,7},{7,6},{8,9},{9,8},{10,11... | collective-permute-start | bytes 737288 | tf_op jit(solution)/shard_map/ppermute | solution.py:400

commit v6 on v5

--- a/solution.py
+++ b/solution.py
@@ -42,33 +42,47 @@
     return (wide * lax.rsqrt(mean + 1e-06) * gain).astype(jnp.bfloat16)
 
 
-def last_tile(rope, table, start, live):
+def last_tile(rope, table):
     half = ROPE // 2
     keys = rope.astype(jnp.float32)
     low, high = keys[:half], keys[half:]
     cosines, sines = table[:half], table[half:]
-    rotated = jnp.concatenate([low * cosines - high * sines, low * sines + high * cosines], 0)
-    shape = (WIDE - ROPE, rope.shape[1])
-    position = start + lax.broadcasted_iota(jnp.int32, shape, 1)
-    first = lax.broadcasted_iota(jnp.int32, shape, 0) == 0
-    bias = jnp.where(first & (position >= live), MASKED, 0.0)
-    return jnp.concatenate([rotated, bias], 0).T.astype(jnp.bfloat16)
-
-
-def spare_tile(rows):
-    lane = lax.broadcasted_iota(jnp.int32, (rows, WIDE), 1)
-    return jnp.where(lane == ROPE, MASKED, 0.0).astype(jnp.bfloat16)
+    zeros = jnp.zeros((WIDE - ROPE, rope.shape[1]), jnp.float32)
+    rotated = [low * cosines - high * sines, low * sines + high * cosines, zeros]
+    return jnp.concatenate(rotated, 0).T.astype(jnp.bfloat16)
+
+
+def masked_tile(tile, allowed):
+    lane = lax.broadcasted_iota(jnp.int32, tile.shape, 1)
+    token = lax.broadcasted_iota(jnp.int32, tile.shape, 0)
+    bias = jnp.where((lane == ROPE) & ~allowed(token), MASKED, 0.0)
+    return tile + bias.astype(jnp.bfloat16)
 
 
 def pack_kernel(
-    latent_hbm, rope_hbm, gain_hbm, tables_hbm, length, payload, piece, latent, rope, gain, table, arrived
+    latent_hbm,
+    rope_hbm,
+    gain_hbm,
+    tables_hbm,
+    payload,
+    piece,
+    latent,
+    rope,
+    gain,
+    table,
+    arrived,
 ):
     rows, width = latent.shape
     ctx, sub = lax.axis_index("ctx"), lax.axis_index("sub")
     copies = [
         pltpu.make_async_copy(source, target, arrived.at[k])
         for k, (source, target) in enumerate(
-            [(latent_hbm, latent), (gain_hbm, gain), (rope_hbm, rope), (tables_hbm.at[ctx], table)]
+            [
+                (latent_hbm, latent),
+                (gain_hbm, gain),
+                (rope_hbm, rope),
+                (tables_hbm.at[ctx], table),
+            ]
         )
     ]
     for copy in copies:
@@ -76,7 +90,7 @@
     for copy in copies:
         copy.wait()
     normed = normalise(latent[...], gain[...])
-    extra = last_tile(rope[...], table[...], ctx * rows, length[0])
+    extra = last_tile(rope[...], table[...])
     payload[:, :width] = normed
     payload[:, width:] = extra
     size = piece.shape[0]
@@ -88,36 +102,40 @@
             piece[:, width:] = extra[k * size : (k + 1) * size]
 
 
-def pick(sub, values):
-    return sum(jnp.where(sub == s, value, 0) for s, value in enumerate(values))
-
-
-def holds(sub, ctx, masks):
-    return lax.shift_right_logical(pick(sub, masks), ctx) & 1 == 1
-
-
-def mid_kernel(sources, masks, piece_masks, gain, tables, length, *rest):
+def mid_kernel(sources, piece_sources, gain, tables, length, *rest):
     count = len(sources)
     latents, ropes, pieces = rest[:count], rest[count : 2 * count], rest[2 * count : -1]
     together = rest[-1]
     ctx, sub = lax.axis_index("ctx"), lax.axis_index("sub")
-    at = 0
-    for latent, rope, source, mask in zip(latents, ropes, sources, masks, strict=True):
-        rows, width = latent.shape
-        origin = sum(
-            jnp.where((sub == s) & (ctx == j), i, 0)
+
+    def origin(source):
+        picked = [
+            jnp.where((sub == s) & (ctx == j), i + 1, 0)
             for s, edges in enumerate(source)
             for i, j in edges
+        ]
+        return sum(picked) - 1
+
+    def allowed(start, there):
+        return lambda token: (start + token < length[0]) & there
+
+    at = 0
+    for latent, rope, source in zip(latents, ropes, sources, strict=True):
+        rows, width = latent.shape
+        shard = origin(source)
+        start = jnp.maximum(shard, 0)
+        together[at : at + rows, :width] = normalise(latent[...], gain[...])
+        together[at : at + rows, width:] = masked_tile(
+            last_tile(rope[...], tables[start]), allowed(start * rows, shard >= 0)
         )
-        together[at : at + rows, :width] = normalise(latent[...], gain[...])
-        tile = last_tile(rope[...], tables[origin], origin * rows, length[0])
-        together[at : at + rows, width:] = jnp.where(holds(sub, ctx, mask), tile, spare_tile(rows))
         at += rows
-    for piece, mask in zip(pieces, piece_masks, strict=True):
+    for piece, edges in zip(pieces, piece_sources, strict=True):
         size, width = piece.shape[0], piece.shape[1] - WIDE
+        cores = lax.axis_size("sub")
+        shard = origin([edges] * cores)
         together[at : at + size, :width] = piece[:, :width]
-        together[at : at + size, width:] = jnp.where(
-            holds(sub, ctx, mask), piece[:, width:], spare_tile(size)
+        together[at : at + size, width:] = masked_tile(
+            piece[:, width:], allowed((shard * cores + sub) * size, shard >= 0)
         )
         at += size
 
@@ -170,8 +188,8 @@
 
 
 def attend_kernel(heads, sets, levels, full, own, expanded, weight, together, fetched, *rest):
-    swapped = rest[:-7]
-    length, out_hbm, grown, scores, weights, out, sent = rest[-7:]
+    swapped = rest[:-8]
+    length, out_hbm, last_own, grown, scores, weights, out, sent = rest[-8:]
     rows = full.shape[0]
     width = weight.shape[0]
     columns = NOPE + VDIM
@@ -179,6 +197,7 @@
     row = lax.broadcasted_iota(jnp.int32, (rows, rows), 0)
     causal = lax.broadcasted_iota(jnp.int32, (rows, rows), 1) <= row
     live = ctx * rows + lax.broadcasted_iota(jnp.int32, (rows, 1), 0) < length[0]
+    last_own[...] = masked_tile(own[:, width:], lambda token: ctx * rows + token < length[0])
     stage, buffers = 2, 4
     block = VDIM * heads // OUT_COPIES
 
@@ -218,7 +237,7 @@
 
         def score(h):
             last = rows_of(
-                lambda: own[:, width:],
+                lambda: last_own[...],
                 lambda piece: together[piece, width:],
                 lambda r, piece: swapped[r][piece, width:],
             )
@@ -293,10 +312,6 @@
     return sets, colours[whole:]
 
 
-def signed(mask):
-    return mask - (1 << 32) if mask >= 1 << 31 else mask
-
-
 def in_hbm(x):
     return pltpu.with_memory_space_constraint(x, pltpu.HBM)
 
@@ -327,15 +342,12 @@
         ]
         return lax.ppermute(data, cores, pairs)
 
-    def receivers(by_core):
-        return [signed(sum(1 << j for _, j in edges)) for edges in by_core]
-
     latents = [send(latent, by_core) for by_core in sets]
     ropes = [send(turned, by_core) for by_core in sets]
 
     payload, piece = pl.pallas_call(
         pack_kernel,
-        in_specs=[HBM] * 4 + [SMEM],
+        in_specs=[HBM] * 4,
         out_specs=[VMEM] * 2,
         out_shape=[
             jax.ShapeDtypeStruct((rows, wide), bf16),
@@ -353,7 +365,7 @@
         ),
         compiler_params=grant(),
         name="pack",
-    )(in_hbm(latent), in_hbm(turned), in_hbm(gain), in_hbm(by_column), prompt_length)
+    )(in_hbm(latent), in_hbm(turned), in_hbm(gain), in_hbm(by_column))
 
     pieces = [send(piece, [edges] * sub_size) for edges in rest]
 
@@ -375,18 +387,14 @@
         ),
     )(queries, payload, up_weight, by_row)
 
+    expanded, prompt_length = lax.optimization_barrier((expanded, prompt_length))
     latents, ropes, pieces, expanded, full = lax.optimization_barrier(
         (latents, ropes, pieces, expanded, full)
     )
     reach = sum(x.shape[0] for x in (*latents, *pieces))
     whole = sum(x.shape[0] for x in latents)
     together = pl.pallas_call(
-        functools.partial(
-            mid_kernel,
-            sets,
-            [receivers(by_core) for by_core in sets],
-            [receivers([edges] * sub_size) for edges in rest],
-        ),
+        functools.partial(mid_kernel, sets, rest),
         in_specs=[VMEM] * 2 + [SMEM] + [VMEM] * (2 * len(latents) + len(pieces)),
         out_specs=VMEM,
         out_shape=jax.ShapeDtypeStruct((reach, wide), bf16),
@@ -431,6 +439,7 @@
         out_specs=ANY,
         out_shape=jax.ShapeDtypeStruct((rows, heads * VDIM), bf16),
         scratch_shapes=[
+            pltpu.VMEM((rows, WIDE), bf16),
             pltpu.VMEM((4, len(swapped), reach, 2 * (NOPE + VDIM)), bf16),
             pltpu.VMEM((4, rows, total), jnp.float32),
             pltpu.VMEM((4, rows, total), bf16),
@@ -456,10 +465,13 @@
         P(None, ("head", "sub")),
         P("parts"),
     )
-    return jax.shard_map(
+    step = jax.shard_map(
         functools.partial(per_device, mesh.shape["ctx"], mesh.shape["sub"]),
         mesh=mesh,
         in_specs=placed,
         out_specs=P(("parts", "ctx"), ("head", "sub")),
         check_vma=False,
     )
+    if len(plan(mesh.shape["ctx"], mesh.shape["sub"])[0]) > 1:
+        return step
+    return step

time: 18.4 us -> 17.8 us (0.967)
  waiting for transfers between devices: 5.05 us -> 4.61 us
  starting transfers between devices: 5.28 us -> 5.07 us
    ppermute x3, waiting for transfers between devices: 4.91 us -> 4.47 us  [send(): return lax.ppermute(data, cores, pairs)]
    ppermute x1, starting transfers between devices: 1.28 us -> 1.07 us  [per_device(): swapped.append(lax.ppermute(together, 'sub', pairs))]
  transfers between devices with their start and end apart: 4 -> 4, of which waited for: 3 -> 3; matrix products, arithmetic and copies ran while one was open for 0% -> 0% of each run, Pallas kernels for 18% -> 19%
where the time goes in v6:
time: 17.8 us; the launch traced here: 17.6 us
  Pallas kernels  7.08 us (40%)
  starting transfers between devices  5.07 us (28%)
  waiting for transfers between devices  4.61 us (26%)
  between operations  0.78 us (4%)
    ppermute x3, waiting for transfers between devices, send(): return lax.ppermute(data, cores, pairs)  4.47 us
    ppermute x3, starting transfers between devices, send(): return lax.ppermute(data, cores, pairs)  4 us
    pallas_call x1, Pallas kernels, per_device(): pl.pallas_call(functools.partial(attend_kernel, heads, whole, levels), in...  3.59 us
    pallas_call x1, Pallas kernels, per_device(): pl.pallas_call(pack_kernel, in_specs=[HBM] * 4, out_specs=[VMEM] * 2, out...  1.25 us
    pallas_call x1, Pallas kernels, per_device(): pl.pallas_call(functools.partial(own_kernel, heads), in_specs=[VMEM] * 3...  1.1 us
    ppermute x1, starting transfers between devices, per_device(): swapped.append(lax.ppermute(together, 'sub', pairs))  1.07 us
    pallas_call x1, Pallas kernels, per_device(): pl.pallas_call(functools.partial(grow_kernel, 4 * (NOPE + VDIM)), in_spec...  1 us
  transfers between devices with their start and end apart: 4, of which 3 were waited for; matrix products, arithmetic and copies ran while one was open for 0% of the time, Pallas kernels for 19%

profile of v6, /device:TPU:25, one launch (start us, length us, event | category | flops | bytes accessed | tf_op | source)
XLA Modules:
  0.0 17.6 jit_solution(16148725589269749015)
XLA Ops:
  0.0 1.3 %collective-permute-start = (bf16[128,512]{1,0:T(8,128)(2,1)}, bf16[128,512]{1,0:T(8,128)(2,1)S(1)}, u32[]{:S(2)}, u32[]{:S(2)}) collective-permute-start(bf16[128,512]{1,0:T(8,128)(2,1)} %latent_hbm.1), channel_id=1, source_target_pairs={{0,12},{4,8},{1,9},{5,13},{2,14},{6,10},{3,11},{7,15},{16,28},{20,... | collective-permute-start | bytes 393224 | tf_op jit(solution)/shard_map/ppermute | solution.py:343
  1.3 0.0 copy-start.5
  1.3 0.0 copy-start
  1.3 0.0 copy-start.1
  1.3 0.0 copy-start.2
  1.3 1.2 %pack.1 = (bf16[128,640]{1,0:T(8,128)(2,1)S(1)}, bf16[64,640]{1,0:T(8,128)(2,1)S(1)}) custom-call(bf16[128,512]{1,0:T(8,128)(2,1)} %latent_hbm.1, bf16[64,128]{1,0:T(8,128)(2,1)} %bitcast.4, f32[1,512]{1,0:T(1,128)} %bitcast.2, f32[4,64,128]{2,1,0:T(8,128)} %constant.5.clone.tables_hbm.tables), custom_call_target="tpu_custom_call" | custom-call | flops 4000000000 | bytes 524288 | tf_op jit(solution)/shard_map/pack/pallas_call | solution.py:348
  2.6 0.0 copy-start.3
  2.6 0.0 copy-start.4
  2.6 1.4 %collective-permute-start.2 = (bf16[64,640]{1,0:T(8,128)(2,1)S(1)}, bf16[64,640]{1,0:T(8,128)(2,1)S(1)}, u32[]{:S(2)}, u32[]{:S(2)}) collective-permute-start(bf16[64,640]{1,0:T(8,128)(2,1)S(1)} %get-tuple-element.16), channel_id=1, source_target_pairs={{0,4},{8,12},{1,5},{9,13},{2,6},{10,14},{3,7},{11,15},{16,20},{24,... | collective-permute-start | bytes 245768 | tf_op jit(solution)/shard_map/ppermute | solution.py:343
  4.0 0.0 copy-done.5
  4.1 1.3 %collective-permute-start.1 = (bf16[64,128]{1,0:T(8,128)(2,1)S(1)}, bf16[64,128]{1,0:T(8,128)(2,1)S(1)}, u32[]{:S(2)}, u32[]{:S(2)}) collective-permute-start(bf16[64,128]{1,0:T(8,128)(2,1)S(1)} %bitcast.5), channel_id=1, source_target_pairs={{0,12},{4,8},{1,9},{5,13},{2,14},{6,10},{3,11},{7,15},{16,28},{20,... | collective-permute-start | bytes 49160 | tf_op jit(solution)/shard_map/ppermute | solution.py:343
  5.4 0.0 copy-done
  5.4 0.0 copy-done.1
  5.4 0.0 copy-done.2
  5.4 1.1 %own.1 = (bf16[128,4096]{1,0:T(8,128)(2,1)S(1)}, bf16[128,4096]{1,0:T(8,128)(2,1)S(1)}) custom-call(bf16[128,3072]{1,0:T(8,128)(2,1)S(1)} %copy-done.1, bf16[128,640]{1,0:T(8,128)(2,1)S(1)} %get-tuple-element.17.payload.own, bf16[512,4096]{1,0:T(8,128)(2,1)S(1)} %copy-done, f32[4,128,128]{2,1,0:T(8,128)S(1)} %copy-done.2), custom_call_target="tpu_custom_call" | custom-call | flops 536870912 | bytes 7077888 | tf_op jit(solution)/shard_map/own/pallas_call | solution.py:372
  7.1 3.9 %collective-permute-done.1.rest_1_ = bf16[64,128]{1,0:T(8,128)(2,1)S(1)} collective-permute-done((bf16[64,128]{1,0:T(8,128)(2,1)S(1)}, bf16[64,128]{1,0:T(8,128)(2,1)S(1)}, u32[]{:S(2)}, u32[]{:S(2)}) %collective-permute-start.1) | collective-permute-done | bytes 16416 | tf_op jit(solution)/shard_map/ppermute | solution.py:343
  11.1 0.5 %collective-permute-done.2.rest_2_ = bf16[64,640]{1,0:T(8,128)(2,1)S(1)} collective-permute-done((bf16[64,640]{1,0:T(8,128)(2,1)S(1)}, bf16[64,640]{1,0:T(8,128)(2,1)S(1)}, u32[]{:S(2)}, u32[]{:S(2)}) %collective-permute-start.2) | collective-permute-done | bytes 81952 | tf_op jit(solution)/shard_map/ppermute | solution.py:343
  11.6 0.0 collective-permute-done.rest_0_
  11.6 0.0 copy-done.3
  11.6 0.0 copy-done.4
  11.6 0.1 mid.1.together
  11.8 1.1 %collective-permute-start.3 = (bf16[192,640]{1,0:T(8,128)(2,1)S(1)}, bf16[192,640]{1,0:T(8,128)(2,1)S(1)}, u32[]{:S(2)}, u32[]{:S(2)}) collective-permute-start(bf16[192,640]{1,0:T(8,128)(2,1)S(1)} %mid.1.together), channel_id=1, source_target_pairs={{0,1},{1,0},{2,3},{3,2},{4,5},{5,4},{6,7},{7,6},{8,9},{9,8},{10,11... | collective-permute-start | bytes 737288 | tf_op jit(solution)/shard_map/ppermute | solution.py:408
  12.8 1.0 %grow.1.fetched = bf16[192,4096]{1,0:T(8,128)(2,1)S(1)} custom-call(bf16[192,640]{1,0:T(8,128)(2,1)S(1)} %mid.1.together, bf16[512,4096]{1,0:T(8,128)(2,1)S(1)} %copy-done), custom_call_target="tpu_custom_call" | custom-call | flops 805306368 | bytes 5767168 | tf_op jit(solution)/shard_map/grow/pallas_call | solution.py:410
  13.9 0.1 collective-permute-done.3.rest_0_
  14.0 3.6 %attend.1 = bf16[128,2048]{1,0:T(8,128)(2,1)} custom-call(bf16[128,4096]{1,0:T(8,128)(2,1)S(1)} %get-tuple-element.21.full, bf16[128,640]{1,0:T(8,128)(2,1)S(1)} %get-tuple-element.17.payload.own, bf16[128,4096]{1,0:T(8,128)(2,1)S(1)} %get-tuple-element.22.expanded, bf16[512,4096]{1,0:T(8,128)(2,1)S(1)} %copy-done, bf16[192,640]{1,0:T(8,128)(2,1)S(1)} %mid.1.together, ...), custom_call_target="tpu_custom_call" | custom-call | flops 3221225472 | bytes 7340032 | tf_op jit(solution)/shard_map/attend/pallas_call | solution.py:436
Async XLA Ops:
  0.0 11.6 %collective-permute-start = (bf16[128,512]{1,0:T(8,128)(2,1)}, bf16[128,512]{1,0:T(8,128)(2,1)S(1)}, u32[]{:S(2)}, u32[]{:S(2)}) collective-permute-start(bf16[128,512]{1,0:T(8,128)(2,1)} %latent_hbm.1), channel_id=1, source_target_pairs={{0,12},{4,8},{1,9},{5,13},{2,14},{6,10},{3,11},{7,15},{16,28},{20,... | collective-permute-start | bytes 393224 | tf_op jit(solution)/shard_map/ppermute | solution.py:343
  1.3 2.8 %copy-start.5 = (bf16[128,64]{0,1:T(8,128)(2,1)S(1)}, bf16[128,64]{0,1:T(8,128)(2,1)}, u32[]{:S(2)}) copy-start(bf16[128,64]{0,1:T(8,128)(2,1)} %param.10) | copy-start | bytes 49156
  1.3 4.1 %copy-start = (bf16[512,4096]{1,0:T(8,128)(2,1)S(1)}, bf16[512,4096]{1,0:T(8,128)(2,1)}, u32[]{:S(2)}) copy-start(bf16[512,4096]{1,0:T(8,128)(2,1)} %weight.5) | copy-start | bytes 12582916
  1.3 4.1 %copy-start.1 = (bf16[128,3072]{1,0:T(8,128)(2,1)S(1)}, bf16[128,3072]{1,0:T(8,128)(2,1)}, u32[]{:S(2)}) copy-start(bf16[128,3072]{1,0:T(8,128)(2,1)} %queries.1) | copy-start | bytes 2359300
  1.3 4.1 %copy-start.2 = (f32[4,128,128]{2,1,0:T(8,128)S(1)}, f32[4,128,128]{2,1,0:T(8,128)}, u32[]{:S(2)}) copy-start(f32[4,128,128]{2,1,0:T(8,128)} %constant.4.clone.tables_hbm) | copy-start | bytes 786436
  2.6 9.0 %copy-start.3 = (f32[4,64,128]{2,1,0:T(8,128)S(1)}, f32[4,64,128]{2,1,0:T(8,128)}, u32[]{:S(2)}) copy-start(f32[4,64,128]{2,1,0:T(8,128)} %constant.5.clone.tables_hbm.tables) | copy-start | bytes 393220
  2.6 9.0 %copy-start.4 = (f32[512]{0:T(512)S(1)}, f32[512]{0:T(512)}, u32[]{:S(2)}) copy-start(f32[512]{0:T(512)} %param.11) | copy-start | bytes 6148
  2.6 9.0 %collective-permute-start.2 = (bf16[64,640]{1,0:T(8,128)(2,1)S(1)}, bf16[64,640]{1,0:T(8,128)(2,1)S(1)}, u32[]{:S(2)}, u32[]{:S(2)}) collective-permute-start(bf16[64,640]{1,0:T(8,128)(2,1)S(1)} %get-tuple-element.16), channel_id=1, source_target_pairs={{0,4},{8,12},{1,5},{9,13},{2,6},{10,14},{3,7},{11,15},{16,20},{24,... | collective-permute-start | bytes 245768 | tf_op jit(solution)/shard_map/ppermute | solution.py:343
  4.1 7.0 %collective-permute-start.1 = (bf16[64,128]{1,0:T(8,128)(2,1)S(1)}, bf16[64,128]{1,0:T(8,128)(2,1)S(1)}, u32[]{:S(2)}, u32[]{:S(2)}) collective-permute-start(bf16[64,128]{1,0:T(8,128)(2,1)S(1)} %bitcast.5), channel_id=1, source_target_pairs={{0,12},{4,8},{1,9},{5,13},{2,14},{6,10},{3,11},{7,15},{16,28},{20,... | collective-permute-start | bytes 49160 | tf_op jit(solution)/shard_map/ppermute | solution.py:343
  11.8 2.2 %collective-permute-start.3 = (bf16[192,640]{1,0:T(8,128)(2,1)S(1)}, bf16[192,640]{1,0:T(8,128)(2,1)S(1)}, u32[]{:S(2)}, u32[]{:S(2)}) collective-permute-start(bf16[192,640]{1,0:T(8,128)(2,1)S(1)} %mid.1.together), channel_id=1, source_target_pairs={{0,1},{1,0},{2,3},{3,2},{4,5},{5,4},{6,7},{7,6},{8,9},{9,8},{10,11... | collective-permute-start | bytes 737288 | tf_op jit(solution)/shard_map/ppermute | solution.py:408

commit v7 on v6

--- a/solution.py
+++ b/solution.py
@@ -205,26 +205,27 @@
         at = pl.ds(k * block, block)
         return pltpu.make_async_copy(out.at[:, at], out_hbm.at[:, at], sent.at[k])
 
-    def run(level):
+    def run(used):
         every = together.shape[0]
-        part = (0, sets, every)[level]
-        total = rows + part * (1 + len(swapped))
+        both = ((0, sets), (sets, every))
+        spans = [span for span, use in zip(both, used, strict=True) if use]
+        extent = slice(spans[0][0], spans[-1][1]) if spans else slice(0, 0)
+        total = rows + sum(end - begin for begin, end in spans) * (1 + len(swapped))
 
         def rows_of(own_part, direct_part, swapped_part):
             found = [own_part()]
-            for begin, end in ((0, sets), (sets, every)):
-                if begin < end <= part:
-                    found.append(direct_part(slice(begin, end)))
-                    for r in range(len(swapped)):
-                        found.append(swapped_part(r, slice(begin, end)))
+            for begin, end in spans:
+                found.append(direct_part(slice(begin, end)))
+                for r in range(len(swapped)):
+                    found.append(swapped_part(r, slice(begin, end)))
             return found[0] if len(found) == 1 else jnp.concatenate(found, 0)
 
         def grow(i):
             at = slice(2 * columns * i, 2 * columns * (i + 1))
             for r, ref in enumerate(swapped):
-                if part:
-                    grown[i % 4, r, :part] = jnp.dot(
-                        ref[:part, :width], weight[:, at], preferred_element_type=jnp.float32
+                if spans:
+                    grown[i % 4, r, extent] = jnp.dot(
+                        ref[extent, :width], weight[:, at], preferred_element_type=jnp.float32
                     ).astype(jnp.bfloat16)
 
         def column(h, begin, end):
@@ -286,11 +287,11 @@
                 if 0 <= t - 2 < steps:
                     mix(h, totals.pop(h))
 
-    for level, places in levels:
+    for used, places in levels:
 
         @pl.when(functools.reduce(jnp.logical_or, [ctx == c for c in places]))
         def _():
-            run(level)
+            run(used)
 
     for k in range(OUT_COPIES):
         leave(k).wait()
@@ -424,12 +425,12 @@
         ),
     )(together, up_weight)
 
-    needs = [0] * ctx_size
-    for level, groups in ((1, [e for by_core in sets for e in by_core]), (2, rest)):
-        for edges in groups:
-            for _, j in edges:
-                needs[j] = level
-    levels = [(k, [c for c in range(ctx_size) if needs[c] == k]) for k in sorted(set(needs))]
+    parts = [[e for by_core in sets for e in by_core], rest]
+    needs = [
+        tuple(any(j == c for edges in part for _, j in edges) for part in parts)
+        for c in range(ctx_size)
+    ]
+    levels = [(u, [c for c in range(ctx_size) if needs[c] == u]) for u in sorted(set(needs))]
     total = rows + sub_size * reach
     held = 2 * (up_weight.size + (reach + 2 * rows) * up_weight.shape[1] + total * wide)
     scratch = 8 * total * (NOPE + VDIM) * 2 + 24 * rows * total + 2 * rows * heads * VDIM

time: 17.8 us -> 17.8 us (level)
  no operation moved by 1% of the time
where the time goes in v7:
time: 17.8 us; the launch traced here: 17.6 us
  Pallas kernels  7.09 us (40%)
  starting transfers between devices  5.07 us (28%)
  waiting for transfers between devices  4.61 us (26%)
  between operations  0.78 us (4%)
    ppermute x3, waiting for transfers between devices, send(): return lax.ppermute(data, cores, pairs)  4.47 us
    ppermute x3, starting transfers between devices, send(): return lax.ppermute(data, cores, pairs)  4 us
    pallas_call x1, Pallas kernels, per_device(): pl.pallas_call(functools.partial(attend_kernel, heads, whole, levels), in...  3.6 us
    pallas_call x1, Pallas kernels, per_device(): pl.pallas_call(pack_kernel, in_specs=[HBM] * 4, out_specs=[VMEM] * 2, out...  1.25 us
    pallas_call x1, Pallas kernels, per_device(): pl.pallas_call(functools.partial(own_kernel, heads), in_specs=[VMEM] * 3...  1.1 us
    ppermute x1, starting transfers between devices, per_device(): swapped.append(lax.ppermute(together, 'sub', pairs))  1.07 us
    pallas_call x1, Pallas kernels, per_device(): pl.pallas_call(functools.partial(grow_kernel, 4 * (NOPE + VDIM)), in_spec...  1 us
  transfers between devices with their start and end apart: 4, of which 3 were waited for; matrix products, arithmetic and copies ran while one was open for 0% of the time, Pallas kernels for 19%

profile of v7, /device:TPU:25, one launch (start us, length us, event | category | flops | bytes accessed | tf_op | source)
XLA Modules:
  0.0 17.6 jit_solution(14318982608467137653)
XLA Ops:
  0.0 1.3 %collective-permute-start = (bf16[128,512]{1,0:T(8,128)(2,1)}, bf16[128,512]{1,0:T(8,128)(2,1)S(1)}, u32[]{:S(2)}, u32[]{:S(2)}) collective-permute-start(bf16[128,512]{1,0:T(8,128)(2,1)} %latent_hbm.1), channel_id=1, source_target_pairs={{0,12},{4,8},{1,9},{5,13},{2,14},{6,10},{3,11},{7,15},{16,28},{20,... | collective-permute-start | bytes 393224 | tf_op jit(solution)/shard_map/ppermute | solution.py:344
  1.3 0.0 copy-start.5
  1.3 0.0 copy-start
  1.3 0.0 copy-start.1
  1.3 0.0 copy-start.2
  1.3 1.2 %pack.1 = (bf16[128,640]{1,0:T(8,128)(2,1)S(1)}, bf16[64,640]{1,0:T(8,128)(2,1)S(1)}) custom-call(bf16[128,512]{1,0:T(8,128)(2,1)} %latent_hbm.1, bf16[64,128]{1,0:T(8,128)(2,1)} %bitcast.4, f32[1,512]{1,0:T(1,128)} %bitcast.2, f32[4,64,128]{2,1,0:T(8,128)} %constant.5.clone.tables_hbm.tables), custom_call_target="tpu_custom_call" | custom-call | flops 4000000000 | bytes 524288 | tf_op jit(solution)/shard_map/pack/pallas_call | solution.py:349
  2.6 0.0 copy-start.3
  2.6 0.0 copy-start.4
  2.6 1.4 %collective-permute-start.2 = (bf16[64,640]{1,0:T(8,128)(2,1)S(1)}, bf16[64,640]{1,0:T(8,128)(2,1)S(1)}, u32[]{:S(2)}, u32[]{:S(2)}) collective-permute-start(bf16[64,640]{1,0:T(8,128)(2,1)S(1)} %get-tuple-element.16), channel_id=1, source_target_pairs={{0,4},{8,12},{1,5},{9,13},{2,6},{10,14},{3,7},{11,15},{16,20},{24,... | collective-permute-start | bytes 245768 | tf_op jit(solution)/shard_map/ppermute | solution.py:344
  4.0 0.0 copy-done.5
  4.1 1.3 %collective-permute-start.1 = (bf16[64,128]{1,0:T(8,128)(2,1)S(1)}, bf16[64,128]{1,0:T(8,128)(2,1)S(1)}, u32[]{:S(2)}, u32[]{:S(2)}) collective-permute-start(bf16[64,128]{1,0:T(8,128)(2,1)S(1)} %bitcast.5), channel_id=1, source_target_pairs={{0,12},{4,8},{1,9},{5,13},{2,14},{6,10},{3,11},{7,15},{16,28},{20,... | collective-permute-start | bytes 49160 | tf_op jit(solution)/shard_map/ppermute | solution.py:344
  5.4 0.0 copy-done
  5.4 0.0 copy-done.1
  5.4 0.0 copy-done.2
  5.4 1.1 %own.1 = (bf16[128,4096]{1,0:T(8,128)(2,1)S(1)}, bf16[128,4096]{1,0:T(8,128)(2,1)S(1)}) custom-call(bf16[128,3072]{1,0:T(8,128)(2,1)S(1)} %copy-done.1, bf16[128,640]{1,0:T(8,128)(2,1)S(1)} %get-tuple-element.17.payload.own, bf16[512,4096]{1,0:T(8,128)(2,1)S(1)} %copy-done, f32[4,128,128]{2,1,0:T(8,128)S(1)} %copy-done.2), custom_call_target="tpu_custom_call" | custom-call | flops 536870912 | bytes 7077888 | tf_op jit(solution)/shard_map/own/pallas_call | solution.py:373
  7.1 3.9 %collective-permute-done.1.rest_1_ = bf16[64,128]{1,0:T(8,128)(2,1)S(1)} collective-permute-done((bf16[64,128]{1,0:T(8,128)(2,1)S(1)}, bf16[64,128]{1,0:T(8,128)(2,1)S(1)}, u32[]{:S(2)}, u32[]{:S(2)}) %collective-permute-start.1) | collective-permute-done | bytes 16416 | tf_op jit(solution)/shard_map/ppermute | solution.py:344
  11.1 0.5 %collective-permute-done.2.rest_2_ = bf16[64,640]{1,0:T(8,128)(2,1)S(1)} collective-permute-done((bf16[64,640]{1,0:T(8,128)(2,1)S(1)}, bf16[64,640]{1,0:T(8,128)(2,1)S(1)}, u32[]{:S(2)}, u32[]{:S(2)}) %collective-permute-start.2) | collective-permute-done | bytes 81952 | tf_op jit(solution)/shard_map/ppermute | solution.py:344
  11.6 0.0 collective-permute-done.rest_0_
  11.6 0.0 copy-done.3
  11.6 0.0 copy-done.4
  11.6 0.1 mid.1.together
  11.8 1.1 %collective-permute-start.3 = (bf16[192,640]{1,0:T(8,128)(2,1)S(1)}, bf16[192,640]{1,0:T(8,128)(2,1)S(1)}, u32[]{:S(2)}, u32[]{:S(2)}) collective-permute-start(bf16[192,640]{1,0:T(8,128)(2,1)S(1)} %mid.1.together), channel_id=1, source_target_pairs={{0,1},{1,0},{2,3},{3,2},{4,5},{5,4},{6,7},{7,6},{8,9},{9,8},{10,11... | collective-permute-start | bytes 737288 | tf_op jit(solution)/shard_map/ppermute | solution.py:409
  12.8 1.0 %grow.1.fetched = bf16[192,4096]{1,0:T(8,128)(2,1)S(1)} custom-call(bf16[192,640]{1,0:T(8,128)(2,1)S(1)} %mid.1.together, bf16[512,4096]{1,0:T(8,128)(2,1)S(1)} %copy-done), custom_call_target="tpu_custom_call" | custom-call | flops 805306368 | bytes 5767168 | tf_op jit(solution)/shard_map/grow/pallas_call | solution.py:411
  13.9 0.1 collective-permute-done.3.rest_0_
  14.0 3.6 %attend.1 = bf16[128,2048]{1,0:T(8,128)(2,1)} custom-call(bf16[128,4096]{1,0:T(8,128)(2,1)S(1)} %get-tuple-element.21.full, bf16[128,640]{1,0:T(8,128)(2,1)S(1)} %get-tuple-element.17.payload.own, bf16[128,4096]{1,0:T(8,128)(2,1)S(1)} %get-tuple-element.22.expanded, bf16[512,4096]{1,0:T(8,128)(2,1)S(1)} %copy-done, bf16[192,640]{1,0:T(8,128)(2,1)S(1)} %mid.1.together, ...), custom_call_target="tpu_custom_call" | custom-call | flops 3221225472 | bytes 7340032 | tf_op jit(solution)/shard_map/attend/pallas_call | solution.py:437
Async XLA Ops:
  0.0 11.6 %collective-permute-start = (bf16[128,512]{1,0:T(8,128)(2,1)}, bf16[128,512]{1,0:T(8,128)(2,1)S(1)}, u32[]{:S(2)}, u32[]{:S(2)}) collective-permute-start(bf16[128,512]{1,0:T(8,128)(2,1)} %latent_hbm.1), channel_id=1, source_target_pairs={{0,12},{4,8},{1,9},{5,13},{2,14},{6,10},{3,11},{7,15},{16,28},{20,... | collective-permute-start | bytes 393224 | tf_op jit(solution)/shard_map/ppermute | solution.py:344
  1.3 2.8 %copy-start.5 = (bf16[128,64]{0,1:T(8,128)(2,1)S(1)}, bf16[128,64]{0,1:T(8,128)(2,1)}, u32[]{:S(2)}) copy-start(bf16[128,64]{0,1:T(8,128)(2,1)} %param.10) | copy-start | bytes 49156
  1.3 4.1 %copy-start = (bf16[512,4096]{1,0:T(8,128)(2,1)S(1)}, bf16[512,4096]{1,0:T(8,128)(2,1)}, u32[]{:S(2)}) copy-start(bf16[512,4096]{1,0:T(8,128)(2,1)} %weight.5) | copy-start | bytes 12582916
  1.3 4.1 %copy-start.1 = (bf16[128,3072]{1,0:T(8,128)(2,1)S(1)}, bf16[128,3072]{1,0:T(8,128)(2,1)}, u32[]{:S(2)}) copy-start(bf16[128,3072]{1,0:T(8,128)(2,1)} %queries.1) | copy-start | bytes 2359300
  1.3 4.1 %copy-start.2 = (f32[4,128,128]{2,1,0:T(8,128)S(1)}, f32[4,128,128]{2,1,0:T(8,128)}, u32[]{:S(2)}) copy-start(f32[4,128,128]{2,1,0:T(8,128)} %constant.4.clone.tables_hbm) | copy-start | bytes 786436
  2.6 9.0 %copy-start.3 = (f32[4,64,128]{2,1,0:T(8,128)S(1)}, f32[4,64,128]{2,1,0:T(8,128)}, u32[]{:S(2)}) copy-start(f32[4,64,128]{2,1,0:T(8,128)} %constant.5.clone.tables_hbm.tables) | copy-start | bytes 393220
  2.6 9.0 %copy-start.4 = (f32[512]{0:T(512)S(1)}, f32[512]{0:T(512)}, u32[]{:S(2)}) copy-start(f32[512]{0:T(512)} %param.11) | copy-start | bytes 6148
  2.6 9.0 %collective-permute-start.2 = (bf16[64,640]{1,0:T(8,128)(2,1)S(1)}, bf16[64,640]{1,0:T(8,128)(2,1)S(1)}, u32[]{:S(2)}, u32[]{:S(2)}) collective-permute-start(bf16[64,640]{1,0:T(8,128)(2,1)S(1)} %get-tuple-element.16), channel_id=1, source_target_pairs={{0,4},{8,12},{1,5},{9,13},{2,6},{10,14},{3,7},{11,15},{16,20},{24,... | collective-permute-start | bytes 245768 | tf_op jit(solution)/shard_map/ppermute | solution.py:344
  4.1 7.0 %collective-permute-start.1 = (bf16[64,128]{1,0:T(8,128)(2,1)S(1)}, bf16[64,128]{1,0:T(8,128)(2,1)S(1)}, u32[]{:S(2)}, u32[]{:S(2)}) collective-permute-start(bf16[64,128]{1,0:T(8,128)(2,1)S(1)} %bitcast.5), channel_id=1, source_target_pairs={{0,12},{4,8},{1,9},{5,13},{2,14},{6,10},{3,11},{7,15},{16,28},{20,... | collective-permute-start | bytes 49160 | tf_op jit(solution)/shard_map/ppermute | solution.py:344
  11.8 2.2 %collective-permute-start.3 = (bf16[192,640]{1,0:T(8,128)(2,1)S(1)}, bf16[192,640]{1,0:T(8,128)(2,1)S(1)}, u32[]{:S(2)}, u32[]{:S(2)}) collective-permute-start(bf16[192,640]{1,0:T(8,128)(2,1)S(1)} %mid.1.together), channel_id=1, source_target_pairs={{0,1},{1,0},{2,3},{3,2},{4,5},{5,4},{6,7},{7,6},{8,9},{9,8},{10,11... | collective-permute-start | bytes 737288 | tf_op jit(solution)/shard_map/ppermute | solution.py:409

commit v8 on v7

--- a/solution.py
+++ b/solution.py
@@ -140,19 +140,30 @@
         at += size
 
 
-def grow_kernel(step, together, weight, grown):
+def grow_kernel(heads, together, weight, turned, straight, values):
     width = weight.shape[0]
 
     @pl.when(lax.axis_index("ctx") > 0)
     def _():
-        for k in range(weight.shape[1] // step):
-            at = slice(k * step, (k + 1) * step)
-            grown[:, at] = jnp.dot(
-                together[:, :width], weight[:, at], preferred_element_type=jnp.float32
-            ).astype(jnp.bfloat16)
-
-
-def own_kernel(heads, queries, payload, weight, tables_hbm, expanded, full, table, arrived):
+        for i in range(heads // 2):
+            project(together[:, :width], weight, i, turned, values, straight)
+
+
+def project(rows, weight, pair, turned, values, straight=None):
+    columns = NOPE + VDIM
+    at = slice(2 * columns * pair, 2 * columns * (pair + 1))
+    expanded = jnp.dot(rows, weight[:, at], preferred_element_type=jnp.float32).astype(jnp.bfloat16)
+    tokens = turned.shape[1]
+    for e in range(2):
+        h = 2 * pair + e
+        keys = expanded[:, columns * e : columns * e + NOPE]
+        turned[NOPE * h : NOPE * (h + 1)] = keys[:tokens].T
+        if straight is not None:
+            straight[:, NOPE * h : NOPE * (h + 1)] = keys[tokens:]
+        values[:, VDIM * h : VDIM * (h + 1)] = expanded[:, columns * e + NOPE : columns * (e + 1)]
+
+
+def own_kernel(heads, queries, payload, weight, tables_hbm, keys, values, full, table, arrived):
     copy = pltpu.make_async_copy(tables_hbm.at[lax.axis_index("ctx")], table, arrived)
     copy.start()
     copy.wait()
@@ -179,17 +190,27 @@
             full[:, at + NOPE : at + FULL] = jnp.concatenate(
                 [ropes[:, ROPE * e : ROPE * (e + 1)], tail], 1
             )
-    columns = NOPE + VDIM
     for i in range(heads // 2):
-        at = slice(2 * columns * i, 2 * columns * (i + 1))
-        expanded[:, at] = jnp.dot(
-            payload[:, :width], weight[:, at], preferred_element_type=jnp.float32
-        ).astype(jnp.bfloat16)
-
-
-def attend_kernel(heads, sets, levels, full, own, expanded, weight, together, fetched, *rest):
-    swapped = rest[:-8]
-    length, out_hbm, last_own, grown, scores, weights, out, sent = rest[-8:]
+        project(payload[:, :width], weight, i, keys, values)
+
+
+def attend_kernel(
+    heads,
+    sets,
+    levels,
+    full,
+    own,
+    own_keys,
+    own_values,
+    weight,
+    together,
+    turned,
+    straight,
+    fetched,
+    *rest,
+):
+    swapped = rest[:-9]
+    length, out_hbm, last_own, last_turned, grown, scores, weights, out, sent = rest[-9:]
     rows = full.shape[0]
     width = weight.shape[0]
     columns = NOPE + VDIM
@@ -228,24 +249,38 @@
                         ref[extent, :width], weight[:, at], preferred_element_type=jnp.float32
                     ).astype(jnp.bfloat16)
 
-        def column(h, begin, end):
+        last = rows_of(
+            lambda: last_own[...],
+            lambda piece: together[piece, width:],
+            lambda r, piece: swapped[r][piece, width:],
+        )
+        last_turned[:, :total] = last.T
+
+        def keys_of(h):
             i, e = divmod(h, 2)
+            at, head = slice(columns * e, columns * e + NOPE), slice(NOPE * h, NOPE * (h + 1))
+            found = [own_keys[head]]
+            if used[0]:
+                found.append(turned[head])
+                found += [grown[i % 4, r, :sets, at].T for r in range(len(swapped))]
+            if used[1]:
+                pieces = [grown[i % 4, r, sets:, at] for r in range(len(swapped))]
+                found.append(jnp.concatenate([straight[:, head], *pieces], 0).T)
+            return found[0] if len(found) == 1 else jnp.concatenate(found, 1)
+
+        def values_of(h):
+            i, e = divmod(h, 2)
+            at = slice(columns * e + NOPE, columns * (e + 1))
             return rows_of(
-                lambda: expanded[:, columns * h + begin : columns * h + end],
-                lambda piece: fetched[piece, columns * h + begin : columns * h + end],
-                lambda r, piece: grown[i % 4, r, piece, columns * e + begin : columns * e + end],
+                lambda: own_values[:, VDIM * h : VDIM * (h + 1)],
+                lambda piece: fetched[piece, VDIM * h : VDIM * (h + 1)],
+                lambda r, piece: grown[i % 4, r, piece, at],
             )
 
         def score(h):
-            last = rows_of(
-                lambda: last_own[...],
-                lambda piece: together[piece, width:],
-                lambda r, piece: swapped[r][piece, width:],
-            )
-            found = lax.dot_general(
+            found = jnp.dot(
                 full[:, FULL * h : FULL * (h + 1)],
-                jnp.concatenate([column(h, 0, NOPE), last], 1),
-                (((1,), (1,)), ((), ())),
+                jnp.concatenate([keys_of(h), last_turned[:, :total]], 0),
                 preferred_element_type=jnp.float32,
             )
             scores[h % buffers, :, :rows] = jnp.where(causal, found[:, :rows], MASKED)
@@ -262,7 +297,7 @@
         def mix(h, total_h):
             mixed = jnp.dot(
                 weights[h % buffers, :, :total],
-                column(h, NOPE, columns),
+                values_of(h),
                 preferred_element_type=jnp.float32,
             )
             out[:, VDIM * h : VDIM * (h + 1)] = jnp.where(live, mixed / total_h, 0.0).astype(
@@ -370,12 +405,13 @@
 
     pieces = [send(piece, [edges] * sub_size) for edges in rest]
 
-    expanded, full = pl.pallas_call(
+    own_keys, own_values, full = pl.pallas_call(
         functools.partial(own_kernel, heads),
         in_specs=[VMEM] * 3 + [ANY],
-        out_specs=[VMEM] * 2,
+        out_specs=[VMEM] * 3,
         out_shape=[
-            jax.ShapeDtypeStruct((rows, up_weight.shape[1]), bf16),
+            jax.ShapeDtypeStruct((heads * NOPE, rows), bf16),
+            jax.ShapeDtypeStruct((rows, heads * VDIM), bf16),
             jax.ShapeDtypeStruct((rows, heads * FULL), bf16),
         ],
         scratch_shapes=[pltpu.VMEM((rows, 2 * ROPE), jnp.float32), pltpu.SemaphoreType.DMA],
@@ -388,9 +424,9 @@
         ),
     )(queries, payload, up_weight, by_row)
 
-    expanded, prompt_length = lax.optimization_barrier((expanded, prompt_length))
-    latents, ropes, pieces, expanded, full = lax.optimization_barrier(
-        (latents, ropes, pieces, expanded, full)
+    own_keys, prompt_length = lax.optimization_barrier((own_keys, prompt_length))
+    latents, ropes, pieces, own_keys, own_values, full = lax.optimization_barrier(
+        (latents, ropes, pieces, own_keys, own_values, full)
     )
     reach = sum(x.shape[0] for x in (*latents, *pieces))
     whole = sum(x.shape[0] for x in latents)
@@ -409,10 +445,14 @@
         swapped.append(lax.ppermute(together, "sub", pairs))
 
     fetched = pl.pallas_call(
-        functools.partial(grow_kernel, 4 * (NOPE + VDIM)),
+        functools.partial(grow_kernel, heads),
         in_specs=[VMEM] * 2,
-        out_specs=VMEM,
-        out_shape=jax.ShapeDtypeStruct((reach, up_weight.shape[1]), bf16),
+        out_specs=[VMEM] * 3,
+        out_shape=[
+            jax.ShapeDtypeStruct((heads * NOPE, whole), bf16),
+            jax.ShapeDtypeStruct((reach - whole, heads * NOPE), bf16),
+            jax.ShapeDtypeStruct((reach, heads * VDIM), bf16),
+        ],
         compiler_params=pltpu.CompilerParams(
             vmem_limit_bytes=4 * MIB
             + 2 * (up_weight.size + reach * (wide + up_weight.shape[1]))
@@ -436,11 +476,12 @@
     scratch = 8 * total * (NOPE + VDIM) * 2 + 24 * rows * total + 2 * rows * heads * VDIM
     return pl.pallas_call(
         functools.partial(attend_kernel, heads, whole, levels),
-        in_specs=[VMEM] * (6 + len(swapped)) + [SMEM],
+        in_specs=[VMEM] * (9 + len(swapped)) + [SMEM],
         out_specs=ANY,
         out_shape=jax.ShapeDtypeStruct((rows, heads * VDIM), bf16),
         scratch_shapes=[
             pltpu.VMEM((rows, WIDE), bf16),
+            pltpu.VMEM((WIDE, total), bf16),
             pltpu.VMEM((4, len(swapped), reach, 2 * (NOPE + VDIM)), bf16),
             pltpu.VMEM((4, rows, total), jnp.float32),
             pltpu.VMEM((4, rows, total), bf16),
@@ -454,7 +495,7 @@
             bytes_accessed=2 * (up_weight.size + 3 * rows * up_weight.shape[1]),
             transcendentals=heads * rows * total,
         ),
-    )(full, payload, expanded, up_weight, together, fetched, *swapped, prompt_length)
+    )(full, payload, own_keys, own_values, up_weight, together, *fetched, *swapped, prompt_length)
 
 
 def solution(mesh):

time: 17.8 us -> 17.8 us (level)
  transfers between devices with their start and end apart: 4 -> 4, of which waited for: 3 -> 3; matrix products, arithmetic and copies ran while one was open for 0% -> 0% of each run, Pallas kernels for 19% -> 20%
where the time goes in v8:
time: 17.8 us; the launch traced here: 17.6 us
  Pallas kernels  7.23 us (41%)
  starting transfers between devices  5.07 us (28%)
  waiting for transfers between devices  4.45 us (25%)
  between operations  0.78 us (4%)
    ppermute x3, waiting for transfers between devices, send(): return lax.ppermute(data, cores, pairs)  4.35 us
    ppermute x3, starting transfers between devices, send(): return lax.ppermute(data, cores, pairs)  4 us
    pallas_call x1, Pallas kernels, per_device(): pl.pallas_call(functools.partial(attend_kernel, heads, whole, levels), in...  3.58 us
    pallas_call x1, Pallas kernels, per_device(): pl.pallas_call(pack_kernel, in_specs=[HBM] * 4, out_specs=[VMEM] * 2, out...  1.25 us
    pallas_call x1, Pallas kernels, per_device(): pl.pallas_call(functools.partial(own_kernel, heads), in_specs=[VMEM] * 3...  1.22 us
    ppermute x1, starting transfers between devices, per_device(): swapped.append(lax.ppermute(together, 'sub', pairs))  1.07 us
    pallas_call x1, Pallas kernels, per_device(): pl.pallas_call(functools.partial(grow_kernel, heads), in_specs=[VMEM] * 2...  1.03 us
  transfers between devices with their start and end apart: 4, of which 3 were waited for; matrix products, arithmetic and copies ran while one was open for 0% of the time, Pallas kernels for 20%

profile of v8, /device:TPU:25, one launch (start us, length us, event | category | flops | bytes accessed | tf_op | source)
XLA Modules:
  0.0 17.6 jit_solution(7210652816362187380)
XLA Ops:
  0.0 1.3 %collective-permute-start = (bf16[128,512]{1,0:T(8,128)(2,1)}, bf16[128,512]{1,0:T(8,128)(2,1)S(1)}, u32[]{:S(2)}, u32[]{:S(2)}) collective-permute-start(bf16[128,512]{1,0:T(8,128)(2,1)} %latent_hbm.1), channel_id=1, source_target_pairs={{0,12},{4,8},{1,9},{5,13},{2,14},{6,10},{3,11},{7,15},{16,28},{20,... | collective-permute-start | bytes 393224 | tf_op jit(solution)/shard_map/ppermute | solution.py:379
  1.3 0.0 copy-start.5
  1.3 0.0 copy-start
  1.3 0.0 copy-start.1
  1.3 0.0 copy-start.2
  1.3 1.2 %pack.1 = (bf16[128,640]{1,0:T(8,128)(2,1)S(1)}, bf16[64,640]{1,0:T(8,128)(2,1)S(1)}) custom-call(bf16[128,512]{1,0:T(8,128)(2,1)} %latent_hbm.1, bf16[64,128]{1,0:T(8,128)(2,1)} %bitcast.4, f32[1,512]{1,0:T(1,128)} %bitcast.2, f32[4,64,128]{2,1,0:T(8,128)} %constant.5.clone.tables_hbm.tables), custom_call_target="tpu_custom_call" | custom-call | flops 4000000000 | bytes 524288 | tf_op jit(solution)/shard_map/pack/pallas_call | solution.py:384
  2.6 0.0 copy-start.3
  2.6 0.0 copy-start.4
  2.6 1.4 %collective-permute-start.2 = (bf16[64,640]{1,0:T(8,128)(2,1)S(1)}, bf16[64,640]{1,0:T(8,128)(2,1)S(1)}, u32[]{:S(2)}, u32[]{:S(2)}) collective-permute-start(bf16[64,640]{1,0:T(8,128)(2,1)S(1)} %get-tuple-element.21), channel_id=1, source_target_pairs={{0,4},{8,12},{1,5},{9,13},{2,6},{10,14},{3,7},{11,15},{16,20},{24,... | collective-permute-start | bytes 245768 | tf_op jit(solution)/shard_map/ppermute | solution.py:379
  4.0 0.0 copy-done.5
  4.1 1.3 %collective-permute-start.1 = (bf16[64,128]{1,0:T(8,128)(2,1)S(1)}, bf16[64,128]{1,0:T(8,128)(2,1)S(1)}, u32[]{:S(2)}, u32[]{:S(2)}) collective-permute-start(bf16[64,128]{1,0:T(8,128)(2,1)S(1)} %bitcast.5), channel_id=1, source_target_pairs={{0,12},{4,8},{1,9},{5,13},{2,14},{6,10},{3,11},{7,15},{16,28},{20,... | collective-permute-start | bytes 49160 | tf_op jit(solution)/shard_map/ppermute | solution.py:379
  5.4 0.0 copy-done
  5.4 0.0 copy-done.1
  5.4 0.0 copy-done.2
  5.4 1.2 %own.1 = (bf16[2048,128]{1,0:T(8,128)(2,1)S(1)}, bf16[128,2048]{1,0:T(8,128)(2,1)S(1)}, bf16[128,4096]{1,0:T(8,128)(2,1)S(1)}) custom-call(bf16[128,3072]{1,0:T(8,128)(2,1)S(1)} %copy-done.1, bf16[128,640]{1,0:T(8,128)(2,1)S(1)} %get-tuple-element.22.payload.own, bf16[512,4096]{1,0:T(8,128)(2,1)S(1)} %copy-done, f32[4,128,128]{2,1,0:T(8,128)S(1)} %copy-done.2), custom_call_target="tpu_custom_call" | custom-call | flops 536870912 | bytes 7077888 | tf_op jit(solution)/shard_map/own/pallas_call | solution.py:408
  7.3 3.8 %collective-permute-done.1.rest_1_ = bf16[64,128]{1,0:T(8,128)(2,1)S(1)} collective-permute-done((bf16[64,128]{1,0:T(8,128)(2,1)S(1)}, bf16[64,128]{1,0:T(8,128)(2,1)S(1)}, u32[]{:S(2)}, u32[]{:S(2)}) %collective-permute-start.1) | collective-permute-done | bytes 16416 | tf_op jit(solution)/shard_map/ppermute | solution.py:379
  11.1 0.5 %collective-permute-done.2.rest_2_ = bf16[64,640]{1,0:T(8,128)(2,1)S(1)} collective-permute-done((bf16[64,640]{1,0:T(8,128)(2,1)S(1)}, bf16[64,640]{1,0:T(8,128)(2,1)S(1)}, u32[]{:S(2)}, u32[]{:S(2)}) %collective-permute-start.2) | collective-permute-done | bytes 81952 | tf_op jit(solution)/shard_map/ppermute | solution.py:379
  11.6 0.0 collective-permute-done.rest_0_
  11.6 0.0 copy-done.3
  11.6 0.0 copy-done.4
  11.6 0.1 mid.1.together
  11.8 1.1 %collective-permute-start.3 = (bf16[192,640]{1,0:T(8,128)(2,1)S(1)}, bf16[192,640]{1,0:T(8,128)(2,1)S(1)}, u32[]{:S(2)}, u32[]{:S(2)}) collective-permute-start(bf16[192,640]{1,0:T(8,128)(2,1)S(1)} %mid.1.together), channel_id=1, source_target_pairs={{0,1},{1,0},{2,3},{3,2},{4,5},{5,4},{6,7},{7,6},{8,9},{9,8},{10,11... | collective-permute-start | bytes 737288 | tf_op jit(solution)/shard_map/ppermute | solution.py:445
  12.8 1.0 %grow.1 = (bf16[2048,128]{1,0:T(8,128)(2,1)S(1)}, bf16[64,2048]{1,0:T(8,128)(2,1)S(1)}, bf16[192,2048]{1,0:T(8,128)(2,1)S(1)}) custom-call(bf16[192,640]{1,0:T(8,128)(2,1)S(1)} %mid.1.together, bf16[512,4096]{1,0:T(8,128)(2,1)S(1)} %copy-done), custom_call_target="tpu_custom_call" | custom-call | flops 805306368 | bytes 5767168 | tf_op jit(solution)/shard_map/grow/pallas_call | solution.py:447
  13.9 0.1 collective-permute-done.3.rest_0_
  14.0 3.6 %attend.1 = bf16[128,2048]{1,0:T(8,128)(2,1)} custom-call(bf16[128,4096]{1,0:T(8,128)(2,1)S(1)} %get-tuple-element.27.full, bf16[128,640]{1,0:T(8,128)(2,1)S(1)} %get-tuple-element.22.payload.own, bf16[2048,128]{1,0:T(8,128)(2,1)S(1)} %get-tuple-element.28.own_keys, bf16[128,2048]{1,0:T(8,128)(2,1)S(1)} %get-tuple-element.29.own_values, ...), custom_call_target="tpu_custom_call" | custom-call | flops 3221225472 | bytes 7340032 | tf_op jit(solution)/shard_map/attend/pallas_call | solution.py:477
Async XLA Ops:
  0.0 11.6 %collective-permute-start = (bf16[128,512]{1,0:T(8,128)(2,1)}, bf16[128,512]{1,0:T(8,128)(2,1)S(1)}, u32[]{:S(2)}, u32[]{:S(2)}) collective-permute-start(bf16[128,512]{1,0:T(8,128)(2,1)} %latent_hbm.1), channel_id=1, source_target_pairs={{0,12},{4,8},{1,9},{5,13},{2,14},{6,10},{3,11},{7,15},{16,28},{20,... | collective-permute-start | bytes 393224 | tf_op jit(solution)/shard_map/ppermute | solution.py:379
  1.3 2.8 %copy-start.5 = (bf16[128,64]{0,1:T(8,128)(2,1)S(1)}, bf16[128,64]{0,1:T(8,128)(2,1)}, u32[]{:S(2)}) copy-start(bf16[128,64]{0,1:T(8,128)(2,1)} %param.10) | copy-start | bytes 49156
  1.3 4.1 %copy-start = (bf16[512,4096]{1,0:T(8,128)(2,1)S(1)}, bf16[512,4096]{1,0:T(8,128)(2,1)}, u32[]{:S(2)}) copy-start(bf16[512,4096]{1,0:T(8,128)(2,1)} %weight.5) | copy-start | bytes 12582916
  1.3 4.1 %copy-start.1 = (bf16[128,3072]{1,0:T(8,128)(2,1)S(1)}, bf16[128,3072]{1,0:T(8,128)(2,1)}, u32[]{:S(2)}) copy-start(bf16[128,3072]{1,0:T(8,128)(2,1)} %queries.1) | copy-start | bytes 2359300
  1.3 4.1 %copy-start.2 = (f32[4,128,128]{2,1,0:T(8,128)S(1)}, f32[4,128,128]{2,1,0:T(8,128)}, u32[]{:S(2)}) copy-start(f32[4,128,128]{2,1,0:T(8,128)} %constant.4.clone.tables_hbm) | copy-start | bytes 786436
  2.6 9.0 %copy-start.3 = (f32[4,64,128]{2,1,0:T(8,128)S(1)}, f32[4,64,128]{2,1,0:T(8,128)}, u32[]{:S(2)}) copy-start(f32[4,64,128]{2,1,0:T(8,128)} %constant.5.clone.tables_hbm.tables) | copy-start | bytes 393220
  2.6 9.0 %copy-start.4 = (f32[512]{0:T(512)S(1)}, f32[512]{0:T(512)}, u32[]{:S(2)}) copy-start(f32[512]{0:T(512)} %param.11) | copy-start | bytes 6148
  2.6 9.0 %collective-permute-start.2 = (bf16[64,640]{1,0:T(8,128)(2,1)S(1)}, bf16[64,640]{1,0:T(8,128)(2,1)S(1)}, u32[]{:S(2)}, u32[]{:S(2)}) collective-permute-start(bf16[64,640]{1,0:T(8,128)(2,1)S(1)} %get-tuple-element.21), channel_id=1, source_target_pairs={{0,4},{8,12},{1,5},{9,13},{2,6},{10,14},{3,7},{11,15},{16,20},{24,... | collective-permute-start | bytes 245768 | tf_op jit(solution)/shard_map/ppermute | solution.py:379
  4.1 7.0 %collective-permute-start.1 = (bf16[64,128]{1,0:T(8,128)(2,1)S(1)}, bf16[64,128]{1,0:T(8,128)(2,1)S(1)}, u32[]{:S(2)}, u32[]{:S(2)}) collective-permute-start(bf16[64,128]{1,0:T(8,128)(2,1)S(1)} %bitcast.5), channel_id=1, source_target_pairs={{0,12},{4,8},{1,9},{5,13},{2,14},{6,10},{3,11},{7,15},{16,28},{20,... | collective-permute-start | bytes 49160 | tf_op jit(solution)/shard_map/ppermute | solution.py:379
  11.8 2.2 %collective-permute-start.3 = (bf16[192,640]{1,0:T(8,128)(2,1)S(1)}, bf16[192,640]{1,0:T(8,128)(2,1)S(1)}, u32[]{:S(2)}, u32[]{:S(2)}) collective-permute-start(bf16[192,640]{1,0:T(8,128)(2,1)S(1)} %mid.1.together), channel_id=1, source_target_pairs={{0,1},{1,0},{2,3},{3,2},{4,5},{5,4},{6,7},{7,6},{8,9},{9,8},{10,11... | collective-permute-start | bytes 737288 | tf_op jit(solution)/shard_map/ppermute | solution.py:445

commit v9 on v7

--- a/solution.py
+++ b/solution.py
@@ -140,16 +140,40 @@
         at += size
 
 
-def grow_kernel(step, together, weight, grown):
-    width = weight.shape[0]
-
-    @pl.when(lax.axis_index("ctx") > 0)
+def grow_kernel(heads, together, weight, full, own, expanded, length, grown, early):
+    rows, width = own.shape[0], weight.shape[0]
+    columns = NOPE + VDIM
+    ctx = lax.axis_index("ctx")
+
+    @pl.when(ctx > 0)
     def _():
-        for k in range(weight.shape[1] // step):
-            at = slice(k * step, (k + 1) * step)
+        row = lax.broadcasted_iota(jnp.int32, (rows, rows), 0)
+        causal = lax.broadcasted_iota(jnp.int32, (rows, rows), 1) <= row
+        last_own = masked_tile(own[:, width:], lambda token: ctx * rows + token < length[0])
+        last = jnp.concatenate([last_own, together[:rows, width:]], 0)
+        for i in range(heads // 2):
+            at = slice(2 * columns * i, 2 * columns * (i + 1))
             grown[:, at] = jnp.dot(
                 together[:, :width], weight[:, at], preferred_element_type=jnp.float32
             ).astype(jnp.bfloat16)
+            if i > 0:
+                score_early(i - 1, causal, last, full, expanded, grown, early)
+        score_early(heads // 2 - 1, causal, last, full, expanded, grown, early)
+
+
+def score_early(pair, causal, last, full, expanded, grown, early):
+    rows = full.shape[0]
+    for h in (2 * pair, 2 * pair + 1):
+        at = slice((NOPE + VDIM) * h, (NOPE + VDIM) * h + NOPE)
+        keys = jnp.concatenate([expanded[:, at], grown[:rows, at]], 0)
+        found = lax.dot_general(
+            full[:, FULL * h : FULL * (h + 1)],
+            jnp.concatenate([keys, last], 1),
+            (((1,), (1,)), ((), ())),
+            preferred_element_type=jnp.float32,
+        )
+        early[h, :, :rows] = jnp.where(causal, found[:, :rows], MASKED)
+        early[h, :, rows:] = found[:, rows:]
 
 
 def own_kernel(heads, queries, payload, weight, tables_hbm, expanded, full, table, arrived):
@@ -187,7 +211,7 @@
         ).astype(jnp.bfloat16)
 
 
-def attend_kernel(heads, sets, levels, full, own, expanded, weight, together, fetched, *rest):
+def attend_kernel(heads, sets, levels, full, own, expanded, weight, together, fetched, early, *rest):
     swapped = rest[:-8]
     length, out_hbm, last_own, grown, scores, weights, out, sent = rest[-8:]
     rows = full.shape[0]
@@ -205,7 +229,7 @@
         at = pl.ds(k * block, block)
         return pltpu.make_async_copy(out.at[:, at], out_hbm.at[:, at], sent.at[k])
 
-    def run(used):
+    def run(used, high):
         every = together.shape[0]
         both = ((0, sets), (sets, every))
         spans = [span for span, use in zip(both, used, strict=True) if use]
@@ -228,6 +252,8 @@
                         ref[extent, :width], weight[:, at], preferred_element_type=jnp.float32
                     ).astype(jnp.bfloat16)
 
+        known = 2 * rows if used[0] else 0
+
         def column(h, begin, end):
             i, e = divmod(h, 2)
             return rows_of(
@@ -243,31 +269,37 @@
                 lambda r, piece: swapped[r][piece, width:],
             )
             found = lax.dot_general(
-                full[:, FULL * h : FULL * (h + 1)],
-                jnp.concatenate([column(h, 0, NOPE), last], 1),
+                full[:high, FULL * h : FULL * (h + 1)],
+                jnp.concatenate([column(h, 0, NOPE)[known:], last[known:]], 1),
                 (((1,), (1,)), ((), ())),
                 preferred_element_type=jnp.float32,
             )
-            scores[h % buffers, :, :rows] = jnp.where(causal, found[:, :rows], MASKED)
+            if known:
+                scores[h % buffers, :high, known:total] = found
+                return
+            scores[h % buffers, :high, :rows] = jnp.where(causal[:high], found[:, :rows], MASKED)
             if total > rows:
-                scores[h % buffers, :, rows:total] = found[:, rows:]
+                scores[h % buffers, :high, rows:total] = found[:, rows:]
 
         def soften(h):
-            found = scores[h % buffers, :, :total]
+            found = scores[h % buffers, :high, known:total]
+            if known:
+                found = jnp.concatenate([early[h, :high], found], 1)
             top = jnp.max(found, 1, keepdims=True)
             raw = jnp.exp2(found * EXPONENT - top * EXPONENT)
-            weights[h % buffers, :, :total] = raw.astype(jnp.bfloat16)
+            weights[h % buffers, :high, :total] = raw.astype(jnp.bfloat16)
             return jnp.sum(raw, 1, keepdims=True)
 
         def mix(h, total_h):
             mixed = jnp.dot(
-                weights[h % buffers, :, :total],
+                weights[h % buffers, :high, :total],
                 column(h, NOPE, columns),
                 preferred_element_type=jnp.float32,
             )
-            out[:, VDIM * h : VDIM * (h + 1)] = jnp.where(live, mixed / total_h, 0.0).astype(
-                jnp.bfloat16
-            )
+            at = slice(VDIM * h, VDIM * (h + 1))
+            out[:high, at] = jnp.where(live[:high], mixed / total_h, 0.0).astype(jnp.bfloat16)
+            if high < rows:
+                out[high:, at] = jnp.zeros((rows - high, VDIM), jnp.bfloat16)
             if (h + 1) % (heads // OUT_COPIES) == 0:
                 leave(h // (heads // OUT_COPIES)).start()
 
@@ -287,11 +319,23 @@
                 if 0 <= t - 2 < steps:
                     mix(h, totals.pop(h))
 
+    left = length[0] - ctx * rows
+
+    @pl.when(left <= 0)
+    def _():
+        out[...] = jnp.zeros_like(out)
+        for k in range(OUT_COPIES):
+            leave(k).start()
+
     for used, places in levels:
-
-        @pl.when(functools.reduce(jnp.logical_or, [ctx == c for c in places]))
-        def _():
-            run(used)
+        here = functools.reduce(jnp.logical_or, [ctx == c for c in places])
+        bounds = [0, rows // 2, rows] if all(used) else [0, rows]
+        for low, high in zip(bounds[:-1], bounds[1:], strict=True):
+            fits = (left > low) if high == rows else (left > low) & (left <= high)
+
+            @pl.when(here & fits)
+            def _():
+                run(used, high)
 
     for k in range(OUT_COPIES):
         leave(k).wait()
@@ -408,14 +452,19 @@
         pairs = [(s, (s + r) % sub_size) for s in range(sub_size)]
         swapped.append(lax.ppermute(together, "sub", pairs))
 
-    fetched = pl.pallas_call(
-        functools.partial(grow_kernel, 4 * (NOPE + VDIM)),
-        in_specs=[VMEM] * 2,
-        out_specs=VMEM,
-        out_shape=jax.ShapeDtypeStruct((reach, up_weight.shape[1]), bf16),
+    fetched, early = pl.pallas_call(
+        functools.partial(grow_kernel, heads),
+        in_specs=[VMEM] * 5 + [SMEM],
+        out_specs=[VMEM] * 2,
+        out_shape=[
+            jax.ShapeDtypeStruct((reach, up_weight.shape[1]), bf16),
+            jax.ShapeDtypeStruct((heads, rows, 2 * rows), jnp.float32),
+        ],
         compiler_params=pltpu.CompilerParams(
             vmem_limit_bytes=4 * MIB
             + 2 * (up_weight.size + reach * (wide + up_weight.shape[1]))
+            + 2 * (full.size + expanded.size + payload.size)
+            + 8 * heads * rows * rows
         ),
         name="grow",
         cost_estimate=pl.CostEstimate(
@@ -423,7 +472,7 @@
             bytes_accessed=2 * (up_weight.size + reach * up_weight.shape[1]),
             transcendentals=0,
         ),
-    )(together, up_weight)
+    )(together, up_weight, full, payload, expanded, prompt_length)
 
     parts = [[e for by_core in sets for e in by_core], rest]
     needs = [
@@ -432,11 +481,11 @@
     ]
     levels = [(u, [c for c in range(ctx_size) if needs[c] == u]) for u in sorted(set(needs))]
     total = rows + sub_size * reach
-    held = 2 * (up_weight.size + (reach + 2 * rows) * up_weight.shape[1] + total * wide)
+    held = 8 * heads * rows * rows + 2 * (up_weight.size + (reach + 2 * rows) * up_weight.shape[1] + total * wide)
     scratch = 8 * total * (NOPE + VDIM) * 2 + 24 * rows * total + 2 * rows * heads * VDIM
     return pl.pallas_call(
         functools.partial(attend_kernel, heads, whole, levels),
-        in_specs=[VMEM] * (6 + len(swapped)) + [SMEM],
+        in_specs=[VMEM] * (7 + len(swapped)) + [SMEM],
         out_specs=ANY,
         out_shape=jax.ShapeDtypeStruct((rows, heads * VDIM), bf16),
         scratch_shapes=[
@@ -454,7 +503,7 @@
             bytes_accessed=2 * (up_weight.size + 3 * rows * up_weight.shape[1]),
             transcendentals=heads * rows * total,
         ),
-    )(full, payload, expanded, up_weight, together, fetched, *swapped, prompt_length)
+    )(full, payload, expanded, up_weight, together, fetched, early, *swapped, prompt_length)
 
 
 def solution(mesh):

time: 17.8 us -> 17.4 us (0.978)
  the two profiles are of different devices: /device:TPU:25 before, /device:TPU:9 now
where the time goes in v9:
time: 17.4 us; the launch traced here: 17.2 us
  starting transfers between devices  7.96 us (46%)
  Pallas kernels  6.9 us (40%)
  waiting for transfers between devices  1.54 us (9%)
  between operations  0.79 us (5%)
    ppermute x3, starting transfers between devices, send(): return lax.ppermute(data, cores, pairs)  6.92 us
    pallas_call x1, Pallas kernels, per_device(): pl.pallas_call(functools.partial(attend_kernel, heads, whole, levels), in...  2.76 us
    pallas_call x1, Pallas kernels, per_device(): pl.pallas_call(functools.partial(grow_kernel, heads), in_specs=[VMEM] * 5...  1.65 us
    ppermute x3, waiting for transfers between devices, send(): return lax.ppermute(data, cores, pairs)  1.54 us
    pallas_call x1, Pallas kernels, per_device(): pl.pallas_call(pack_kernel, in_specs=[HBM] * 4, out_specs=[VMEM] * 2, out...  1.25 us
    pallas_call x1, Pallas kernels, per_device(): pl.pallas_call(functools.partial(own_kernel, heads), in_specs=[VMEM] * 3...  1.1 us
    ppermute x1, starting transfers between devices, per_device(): swapped.append(lax.ppermute(together, 'sub', pairs))  1.04 us
  transfers between devices with their start and end apart: 4, of which 2 were waited for; matrix products, arithmetic and copies ran while one was open for 0% of the time, Pallas kernels for 23%

profile of v9, /device:TPU:9, one launch (start us, length us, event | category | flops | bytes accessed | tf_op | source)
XLA Modules:
  0.0 17.2 jit_solution(2146059229927730080)
XLA Ops:
  0.0 4.2 %collective-permute-start = (bf16[128,512]{1,0:T(8,128)(2,1)}, bf16[128,512]{1,0:T(8,128)(2,1)S(1)}, u32[]{:S(2)}, u32[]{:S(2)}) collective-permute-start(bf16[128,512]{1,0:T(8,128)(2,1)} %latent_hbm.1), channel_id=1, source_target_pairs={{0,12},{4,8},{1,9},{5,13},{2,14},{6,10},{3,11},{7,15},{16,28},{20,... | collective-permute-start | bytes 393224 | tf_op jit(solution)/shard_map/ppermute | solution.py:388
  4.2 0.0 copy-start.5
  4.2 0.0 copy-start
  4.2 0.0 copy-start.1
  4.2 0.0 copy-start.2
  4.3 1.2 %pack.1 = (bf16[128,640]{1,0:T(8,128)(2,1)S(1)}, bf16[64,640]{1,0:T(8,128)(2,1)S(1)}) custom-call(bf16[128,512]{1,0:T(8,128)(2,1)} %latent_hbm.1, bf16[64,128]{1,0:T(8,128)(2,1)} %bitcast.4, f32[1,512]{1,0:T(1,128)} %bitcast.2, f32[4,64,128]{2,1,0:T(8,128)} %constant.5.clone.tables_hbm.tables), custom_call_target="tpu_custom_call" | custom-call | flops 4000000000 | bytes 524288 | tf_op jit(solution)/shard_map/pack/pallas_call | solution.py:393
  5.5 1.4 %collective-permute-start.2 = (bf16[64,640]{1,0:T(8,128)(2,1)S(1)}, bf16[64,640]{1,0:T(8,128)(2,1)S(1)}, u32[]{:S(2)}, u32[]{:S(2)}) collective-permute-start(bf16[64,640]{1,0:T(8,128)(2,1)S(1)} %get-tuple-element.18), channel_id=1, source_target_pairs={{0,4},{8,12},{1,5},{9,13},{2,6},{10,14},{3,7},{11,15},{16,20},{24,... | collective-permute-start | bytes 245768 | tf_op jit(solution)/shard_map/ppermute | solution.py:388
  6.9 0.0 copy-done.5
  7.0 1.3 %collective-permute-start.1 = (bf16[64,128]{1,0:T(8,128)(2,1)S(1)}, bf16[64,128]{1,0:T(8,128)(2,1)S(1)}, u32[]{:S(2)}, u32[]{:S(2)}) collective-permute-start(bf16[64,128]{1,0:T(8,128)(2,1)S(1)} %bitcast.5), channel_id=1, source_target_pairs={{0,12},{4,8},{1,9},{5,13},{2,14},{6,10},{3,11},{7,15},{16,28},{20,... | collective-permute-start | bytes 49160 | tf_op jit(solution)/shard_map/ppermute | solution.py:388
  8.3 0.0 copy-done
  8.3 0.0 copy-done.1
  8.3 0.0 copy-done.2
  8.3 0.0 copy-start.3
  8.3 0.0 copy-start.4
  8.3 1.1 %own.1 = (bf16[128,4096]{1,0:T(8,128)(2,1)S(1)}, bf16[128,4096]{1,0:T(8,128)(2,1)S(1)}) custom-call(bf16[128,3072]{1,0:T(8,128)(2,1)S(1)} %copy-done.1, bf16[128,640]{1,0:T(8,128)(2,1)S(1)} %get-tuple-element.19.payload.own, bf16[512,4096]{1,0:T(8,128)(2,1)S(1)} %copy-done, f32[4,128,128]{2,1,0:T(8,128)S(1)} %copy-done.2), custom_call_target="tpu_custom_call" | custom-call | flops 536870912 | bytes 7077888 | tf_op jit(solution)/shard_map/own/pallas_call | solution.py:417
  10.1 0.5 %collective-permute-done.1.rest_1_ = bf16[64,128]{1,0:T(8,128)(2,1)S(1)} collective-permute-done((bf16[64,128]{1,0:T(8,128)(2,1)S(1)}, bf16[64,128]{1,0:T(8,128)(2,1)S(1)}, u32[]{:S(2)}, u32[]{:S(2)}) %collective-permute-start.1) | collective-permute-done | bytes 16416 | tf_op jit(solution)/shard_map/ppermute | solution.py:388
  10.6 1.0 %collective-permute-done.2.rest_2_ = bf16[64,640]{1,0:T(8,128)(2,1)S(1)} collective-permute-done((bf16[64,640]{1,0:T(8,128)(2,1)S(1)}, bf16[64,640]{1,0:T(8,128)(2,1)S(1)}, u32[]{:S(2)}, u32[]{:S(2)}) %collective-permute-start.2) | collective-permute-done | bytes 81952 | tf_op jit(solution)/shard_map/ppermute | solution.py:388
  11.6 0.0 collective-permute-done.rest_0_
  11.6 0.0 copy-done.3
  11.6 0.0 copy-done.4
  11.6 0.1 mid.1.together
  11.8 1.0 %collective-permute-start.3 = (bf16[192,640]{1,0:T(8,128)(2,1)S(1)}, bf16[192,640]{1,0:T(8,128)(2,1)S(1)}, u32[]{:S(2)}, u32[]{:S(2)}) collective-permute-start(bf16[192,640]{1,0:T(8,128)(2,1)S(1)} %mid.1.together), channel_id=1, source_target_pairs={{0,1},{1,0},{2,3},{3,2},{4,5},{5,4},{6,7},{7,6},{8,9},{9,8},{10,11... | collective-permute-start | bytes 737288 | tf_op jit(solution)/shard_map/ppermute | solution.py:453
  12.8 1.6 %grow.1 = (bf16[192,4096]{1,0:T(8,128)(2,1)S(1)}, f32[16,128,256]{2,1,0:T(8,128)S(1)}) custom-call(bf16[192,640]{1,0:T(8,128)(2,1)S(1)} %mid.1.together, bf16[512,4096]{1,0:T(8,128)(2,1)S(1)} %copy-done, bf16[128,4096]{1,0:T(8,128)(2,1)S(1)} %get-tuple-element.23.full, bf16[128,640]{1,0:T(8,128)(2,1)S(1)} %get-tuple-element.19.payload.own, ...), custom_call_target="tpu_custom_call" | custom-call | flops 805306368 | bytes 5767168 | tf_op jit(solution)/shard_map/grow/pallas_call | solution.py:455
  14.5 0.0 collective-permute-done.3.rest_0_
  14.5 2.8 %attend.1 = bf16[128,2048]{1,0:T(8,128)(2,1)} custom-call(bf16[128,4096]{1,0:T(8,128)(2,1)S(1)} %get-tuple-element.23.full, bf16[128,640]{1,0:T(8,128)(2,1)S(1)} %get-tuple-element.19.payload.own, bf16[128,4096]{1,0:T(8,128)(2,1)S(1)} %get-tuple-element.24.expanded, bf16[512,4096]{1,0:T(8,128)(2,1)S(1)} %copy-done, bf16[192,640]{1,0:T(8,128)(2,1)S(1)} %mid.1.together, ...), custom_call_target="tpu_custom_call" | custom-call | flops 3221225472 | bytes 7340032 | tf_op jit(solution)/shard_map/attend/pallas_call | solution.py:486
Async XLA Ops:
  0.0 11.6 %collective-permute-start = (bf16[128,512]{1,0:T(8,128)(2,1)}, bf16[128,512]{1,0:T(8,128)(2,1)S(1)}, u32[]{:S(2)}, u32[]{:S(2)}) collective-permute-start(bf16[128,512]{1,0:T(8,128)(2,1)} %latent_hbm.1), channel_id=1, source_target_pairs={{0,12},{4,8},{1,9},{5,13},{2,14},{6,10},{3,11},{7,15},{16,28},{20,... | collective-permute-start | bytes 393224 | tf_op jit(solution)/shard_map/ppermute | solution.py:388
  4.2 2.7 %copy-start.5 = (bf16[128,64]{0,1:T(8,128)(2,1)S(1)}, bf16[128,64]{0,1:T(8,128)(2,1)}, u32[]{:S(2)}) copy-start(bf16[128,64]{0,1:T(8,128)(2,1)} %param.10) | copy-start | bytes 49156
  4.2 4.0 %copy-start = (bf16[512,4096]{1,0:T(8,128)(2,1)S(1)}, bf16[512,4096]{1,0:T(8,128)(2,1)}, u32[]{:S(2)}) copy-start(bf16[512,4096]{1,0:T(8,128)(2,1)} %weight.5) | copy-start | bytes 12582916
  4.2 4.0 %copy-start.1 = (bf16[128,3072]{1,0:T(8,128)(2,1)S(1)}, bf16[128,3072]{1,0:T(8,128)(2,1)}, u32[]{:S(2)}) copy-start(bf16[128,3072]{1,0:T(8,128)(2,1)} %queries.1) | copy-start | bytes 2359300
  4.2 4.0 %copy-start.2 = (f32[4,128,128]{2,1,0:T(8,128)S(1)}, f32[4,128,128]{2,1,0:T(8,128)}, u32[]{:S(2)}) copy-start(f32[4,128,128]{2,1,0:T(8,128)} %constant.4.clone.tables_hbm) | copy-start | bytes 786436
  5.5 6.1 %collective-permute-start.2 = (bf16[64,640]{1,0:T(8,128)(2,1)S(1)}, bf16[64,640]{1,0:T(8,128)(2,1)S(1)}, u32[]{:S(2)}, u32[]{:S(2)}) collective-permute-start(bf16[64,640]{1,0:T(8,128)(2,1)S(1)} %get-tuple-element.18), channel_id=1, source_target_pairs={{0,4},{8,12},{1,5},{9,13},{2,6},{10,14},{3,7},{11,15},{16,20},{24,... | collective-permute-start | bytes 245768 | tf_op jit(solution)/shard_map/ppermute | solution.py:388
  7.0 3.6 %collective-permute-start.1 = (bf16[64,128]{1,0:T(8,128)(2,1)S(1)}, bf16[64,128]{1,0:T(8,128)(2,1)S(1)}, u32[]{:S(2)}, u32[]{:S(2)}) collective-permute-start(bf16[64,128]{1,0:T(8,128)(2,1)S(1)} %bitcast.5), channel_id=1, source_target_pairs={{0,12},{4,8},{1,9},{5,13},{2,14},{6,10},{3,11},{7,15},{16,28},{20,... | collective-permute-start | bytes 49160 | tf_op jit(solution)/shard_map/ppermute | solution.py:388
  8.3 3.3 %copy-start.3 = (f32[4,64,128]{2,1,0:T(8,128)S(1)}, f32[4,64,128]{2,1,0:T(8,128)}, u32[]{:S(2)}) copy-start(f32[4,64,128]{2,1,0:T(8,128)} %constant.5.clone.tables_hbm.tables) | copy-start | bytes 393220
  8.3 3.3 %copy-start.4 = (f32[512]{0:T(512)S(1)}, f32[512]{0:T(512)}, u32[]{:S(2)}) copy-start(f32[512]{0:T(512)} %param.11) | copy-start | bytes 6148
  11.8 2.7 %collective-permute-start.3 = (bf16[192,640]{1,0:T(8,128)(2,1)S(1)}, bf16[192,640]{1,0:T(8,128)(2,1)S(1)}, u32[]{:S(2)}, u32[]{:S(2)}) collective-permute-start(bf16[192,640]{1,0:T(8,128)(2,1)S(1)} %mid.1.together), channel_id=1, source_target_pairs={{0,1},{1,0},{2,3},{3,2},{4,5},{5,4},{6,7},{7,6},{8,9},{9,8},{10,11... | collective-permute-start | bytes 737288 | tf_op jit(solution)/shard_map/ppermute | solution.py:453

commit v10 on v9

--- a/solution.py
+++ b/solution.py
@@ -140,25 +140,33 @@
         at += size
 
 
-def grow_kernel(heads, together, weight, full, own, expanded, length, grown, early):
+def grow_kernel(heads, takers, together, weight, full, own, expanded, length, grown, early):
     rows, width = own.shape[0], weight.shape[0]
     columns = NOPE + VDIM
     ctx = lax.axis_index("ctx")
-
-    @pl.when(ctx > 0)
-    def _():
+    takes = functools.reduce(jnp.logical_or, [ctx == c for c in takers], ctx < 0)
+
+    def run(scored):
         row = lax.broadcasted_iota(jnp.int32, (rows, rows), 0)
         causal = lax.broadcasted_iota(jnp.int32, (rows, rows), 1) <= row
         last_own = masked_tile(own[:, width:], lambda token: ctx * rows + token < length[0])
         last = jnp.concatenate([last_own, together[:rows, width:]], 0)
-        for i in range(heads // 2):
-            at = slice(2 * columns * i, 2 * columns * (i + 1))
-            grown[:, at] = jnp.dot(
-                together[:, :width], weight[:, at], preferred_element_type=jnp.float32
-            ).astype(jnp.bfloat16)
-            if i > 0:
+        for i in range(heads // 2 + 1):
+            if i < heads // 2:
+                at = slice(2 * columns * i, 2 * columns * (i + 1))
+                grown[:, at] = jnp.dot(
+                    together[:, :width], weight[:, at], preferred_element_type=jnp.float32
+                ).astype(jnp.bfloat16)
+            if scored and i > 0:
                 score_early(i - 1, causal, last, full, expanded, grown, early)
-        score_early(heads // 2 - 1, causal, last, full, expanded, grown, early)
+
+    @pl.when(takes)
+    def _():
+        run(True)
+
+    @pl.when((ctx > 0) & ~takes)
+    def _():
+        run(False)
 
 
 def score_early(pair, causal, last, full, expanded, grown, early):
@@ -452,8 +460,15 @@
         pairs = [(s, (s + r) % sub_size) for s in range(sub_size)]
         swapped.append(lax.ppermute(together, "sub", pairs))
 
+    parts = [[e for by_core in sets for e in by_core], rest]
+    needs = [
+        tuple(any(j == c for edges in part for _, j in edges) for part in parts)
+        for c in range(ctx_size)
+    ]
+    levels = [(u, [c for c in range(ctx_size) if needs[c] == u]) for u in sorted(set(needs))]
+    takers = [c for c in range(ctx_size) if needs[c][0]]
     fetched, early = pl.pallas_call(
-        functools.partial(grow_kernel, heads),
+        functools.partial(grow_kernel, heads, takers),
         in_specs=[VMEM] * 5 + [SMEM],
         out_specs=[VMEM] * 2,
         out_shape=[
@@ -474,12 +489,6 @@
         ),
     )(together, up_weight, full, payload, expanded, prompt_length)
 
-    parts = [[e for by_core in sets for e in by_core], rest]
-    needs = [
-        tuple(any(j == c for edges in part for _, j in edges) for part in parts)
-        for c in range(ctx_size)
-    ]
-    levels = [(u, [c for c in range(ctx_size) if needs[c] == u]) for u in sorted(set(needs))]
     total = rows + sub_size * reach
     held = 8 * heads * rows * rows + 2 * (up_weight.size + (reach + 2 * rows) * up_weight.shape[1] + total * wide)
     scratch = 8 * total * (NOPE + VDIM) * 2 + 24 * rows * total + 2 * rows * heads * VDIM

time: 17.4 us -> 17.4 us (level)
  the two profiles are of different devices: /device:TPU:9 before, /device:TPU:23 now
where the time goes in v10:
time: 17.4 us; the launch traced here: 17.2 us
  starting transfers between devices  6.96 us (40%)
  Pallas kernels  6.89 us (40%)
  waiting for transfers between devices  2.51 us (14%)
  between operations  0.8 us (5%)
    ppermute x3, starting transfers between devices, send(): return lax.ppermute(data, cores, pairs)  5.91 us
    pallas_call x1, Pallas kernels, per_device(): pl.pallas_call(functools.partial(attend_kernel, heads, whole, levels), in...  2.75 us
    ppermute x3, waiting for transfers between devices, send(): return lax.ppermute(data, cores, pairs)  2.51 us
    pallas_call x1, Pallas kernels, per_device(): pl.pallas_call(functools.partial(grow_kernel, heads, takers), in_specs=[V...  1.65 us
    pallas_call x1, Pallas kernels, per_device(): pl.pallas_call(pack_kernel, in_specs=[HBM] * 4, out_specs=[VMEM] * 2, out...  1.25 us
    pallas_call x1, Pallas kernels, per_device(): pl.pallas_call(functools.partial(own_kernel, heads), in_specs=[VMEM] * 3...  1.09 us
    ppermute x1, starting transfers between devices, per_device(): swapped.append(lax.ppermute(together, 'sub', pairs))  1.05 us
  transfers between devices with their start and end apart: 4, of which 1 were waited for; matrix products, arithmetic and copies ran while one was open for 0% of the time, Pallas kernels for 23%

profile of v10, /device:TPU:23, one launch (start us, length us, event | category | flops | bytes accessed | tf_op | source)
XLA Modules:
  0.0 17.2 jit_solution(7088600756332002393)
XLA Ops:
  0.0 1.3 %collective-permute-start = (bf16[128,512]{1,0:T(8,128)(2,1)}, bf16[128,512]{1,0:T(8,128)(2,1)S(1)}, u32[]{:S(2)}, u32[]{:S(2)}) collective-permute-start(bf16[128,512]{1,0:T(8,128)(2,1)} %latent_hbm.1), channel_id=1, source_target_pairs={{0,12},{4,8},{1,9},{5,13},{2,14},{6,10},{3,11},{7,15},{16,28},{20,... | collective-permute-start | bytes 393224 | tf_op jit(solution)/shard_map/ppermute | solution.py:396
  1.3 0.0 copy-start.5
  1.3 0.0 copy-start
  1.3 0.0 copy-start.1
  1.3 0.0 copy-start.2
  1.3 1.2 %pack.1 = (bf16[128,640]{1,0:T(8,128)(2,1)S(1)}, bf16[64,640]{1,0:T(8,128)(2,1)S(1)}) custom-call(bf16[128,512]{1,0:T(8,128)(2,1)} %latent_hbm.1, bf16[64,128]{1,0:T(8,128)(2,1)} %bitcast.4, f32[1,512]{1,0:T(1,128)} %bitcast.2, f32[4,64,128]{2,1,0:T(8,128)} %constant.5.clone.tables_hbm.tables), custom_call_target="tpu_custom_call" | custom-call | flops 4000000000 | bytes 524288 | tf_op jit(solution)/shard_map/pack/pallas_call | solution.py:401
  2.6 3.3 %collective-permute-start.2 = (bf16[64,640]{1,0:T(8,128)(2,1)S(1)}, bf16[64,640]{1,0:T(8,128)(2,1)S(1)}, u32[]{:S(2)}, u32[]{:S(2)}) collective-permute-start(bf16[64,640]{1,0:T(8,128)(2,1)S(1)} %get-tuple-element.18), channel_id=1, source_target_pairs={{0,4},{8,12},{1,5},{9,13},{2,6},{10,14},{3,7},{11,15},{16,20},{24,... | collective-permute-start | bytes 245768 | tf_op jit(solution)/shard_map/ppermute | solution.py:396
  5.9 0.0 copy-done.5
  5.9 1.3 %collective-permute-start.1 = (bf16[64,128]{1,0:T(8,128)(2,1)S(1)}, bf16[64,128]{1,0:T(8,128)(2,1)S(1)}, u32[]{:S(2)}, u32[]{:S(2)}) collective-permute-start(bf16[64,128]{1,0:T(8,128)(2,1)S(1)} %bitcast.5), channel_id=1, source_target_pairs={{0,12},{4,8},{1,9},{5,13},{2,14},{6,10},{3,11},{7,15},{16,28},{20,... | collective-permute-start | bytes 49160 | tf_op jit(solution)/shard_map/ppermute | solution.py:396
  7.2 0.0 copy-done
  7.3 0.0 copy-done.1
  7.3 0.0 copy-done.2
  7.3 0.0 copy-start.3
  7.3 0.0 copy-start.4
  7.3 1.1 %own.1 = (bf16[128,4096]{1,0:T(8,128)(2,1)S(1)}, bf16[128,4096]{1,0:T(8,128)(2,1)S(1)}) custom-call(bf16[128,3072]{1,0:T(8,128)(2,1)S(1)} %copy-done.1, bf16[128,640]{1,0:T(8,128)(2,1)S(1)} %get-tuple-element.19.payload.own, bf16[512,4096]{1,0:T(8,128)(2,1)S(1)} %copy-done, f32[4,128,128]{2,1,0:T(8,128)S(1)} %copy-done.2), custom_call_target="tpu_custom_call" | custom-call | flops 536870912 | bytes 7077888 | tf_op jit(solution)/shard_map/own/pallas_call | solution.py:425
  9.0 2.5 %collective-permute-done.1.rest_1_ = bf16[64,128]{1,0:T(8,128)(2,1)S(1)} collective-permute-done((bf16[64,128]{1,0:T(8,128)(2,1)S(1)}, bf16[64,128]{1,0:T(8,128)(2,1)S(1)}, u32[]{:S(2)}, u32[]{:S(2)}) %collective-permute-start.1) | collective-permute-done | bytes 16416 | tf_op jit(solution)/shard_map/ppermute | solution.py:396
  11.5 0.0 collective-permute-done.2.rest_2_
  11.6 0.0 collective-permute-done.rest_0_
  11.6 0.0 copy-done.3
  11.6 0.0 copy-done.4
  11.6 0.1 mid.1.together
  11.7 1.1 %collective-permute-start.3 = (bf16[192,640]{1,0:T(8,128)(2,1)S(1)}, bf16[192,640]{1,0:T(8,128)(2,1)S(1)}, u32[]{:S(2)}, u32[]{:S(2)}) collective-permute-start(bf16[192,640]{1,0:T(8,128)(2,1)S(1)} %mid.1.together), channel_id=1, source_target_pairs={{0,1},{1,0},{2,3},{3,2},{4,5},{5,4},{6,7},{7,6},{8,9},{9,8},{10,11... | collective-permute-start | bytes 737288 | tf_op jit(solution)/shard_map/ppermute | solution.py:461
  12.8 1.6 %grow.1 = (bf16[192,4096]{1,0:T(8,128)(2,1)S(1)}, f32[16,128,256]{2,1,0:T(8,128)S(1)}) custom-call(bf16[192,640]{1,0:T(8,128)(2,1)S(1)} %mid.1.together, bf16[512,4096]{1,0:T(8,128)(2,1)S(1)} %copy-done, bf16[128,4096]{1,0:T(8,128)(2,1)S(1)} %get-tuple-element.23.full, bf16[128,640]{1,0:T(8,128)(2,1)S(1)} %get-tuple-element.19.payload.own, ...), custom_call_target="tpu_custom_call" | custom-call | flops 805306368 | bytes 5767168 | tf_op jit(solution)/shard_map/grow/pallas_call | solution.py:470
  14.4 0.0 collective-permute-done.3.rest_0_
  14.4 2.8 %attend.1 = bf16[128,2048]{1,0:T(8,128)(2,1)} custom-call(bf16[128,4096]{1,0:T(8,128)(2,1)S(1)} %get-tuple-element.23.full, bf16[128,640]{1,0:T(8,128)(2,1)S(1)} %get-tuple-element.19.payload.own, bf16[128,4096]{1,0:T(8,128)(2,1)S(1)} %get-tuple-element.24.expanded, bf16[512,4096]{1,0:T(8,128)(2,1)S(1)} %copy-done, bf16[192,640]{1,0:T(8,128)(2,1)S(1)} %mid.1.together, ...), custom_call_target="tpu_custom_call" | custom-call | flops 3221225472 | bytes 7340032 | tf_op jit(solution)/shard_map/attend/pallas_call | solution.py:495
Async XLA Ops:
  0.0 11.6 %collective-permute-start = (bf16[128,512]{1,0:T(8,128)(2,1)}, bf16[128,512]{1,0:T(8,128)(2,1)S(1)}, u32[]{:S(2)}, u32[]{:S(2)}) collective-permute-start(bf16[128,512]{1,0:T(8,128)(2,1)} %latent_hbm.1), channel_id=1, source_target_pairs={{0,12},{4,8},{1,9},{5,13},{2,14},{6,10},{3,11},{7,15},{16,28},{20,... | collective-permute-start | bytes 393224 | tf_op jit(solution)/shard_map/ppermute | solution.py:396
  1.3 4.6 %copy-start.5 = (bf16[128,64]{0,1:T(8,128)(2,1)S(1)}, bf16[128,64]{0,1:T(8,128)(2,1)}, u32[]{:S(2)}) copy-start(bf16[128,64]{0,1:T(8,128)(2,1)} %param.10) | copy-start | bytes 49156
  1.3 5.9 %copy-start = (bf16[512,4096]{1,0:T(8,128)(2,1)S(1)}, bf16[512,4096]{1,0:T(8,128)(2,1)}, u32[]{:S(2)}) copy-start(bf16[512,4096]{1,0:T(8,128)(2,1)} %weight.5) | copy-start | bytes 12582916
  1.3 5.9 %copy-start.1 = (bf16[128,3072]{1,0:T(8,128)(2,1)S(1)}, bf16[128,3072]{1,0:T(8,128)(2,1)}, u32[]{:S(2)}) copy-start(bf16[128,3072]{1,0:T(8,128)(2,1)} %queries.1) | copy-start | bytes 2359300
  1.3 5.9 %copy-start.2 = (f32[4,128,128]{2,1,0:T(8,128)S(1)}, f32[4,128,128]{2,1,0:T(8,128)}, u32[]{:S(2)}) copy-start(f32[4,128,128]{2,1,0:T(8,128)} %constant.4.clone.tables_hbm) | copy-start | bytes 786436
  2.6 9.0 %collective-permute-start.2 = (bf16[64,640]{1,0:T(8,128)(2,1)S(1)}, bf16[64,640]{1,0:T(8,128)(2,1)S(1)}, u32[]{:S(2)}, u32[]{:S(2)}) collective-permute-start(bf16[64,640]{1,0:T(8,128)(2,1)S(1)} %get-tuple-element.18), channel_id=1, source_target_pairs={{0,4},{8,12},{1,5},{9,13},{2,6},{10,14},{3,7},{11,15},{16,20},{24,... | collective-permute-start | bytes 245768 | tf_op jit(solution)/shard_map/ppermute | solution.py:396
  5.9 5.6 %collective-permute-start.1 = (bf16[64,128]{1,0:T(8,128)(2,1)S(1)}, bf16[64,128]{1,0:T(8,128)(2,1)S(1)}, u32[]{:S(2)}, u32[]{:S(2)}) collective-permute-start(bf16[64,128]{1,0:T(8,128)(2,1)S(1)} %bitcast.5), channel_id=1, source_target_pairs={{0,12},{4,8},{1,9},{5,13},{2,14},{6,10},{3,11},{7,15},{16,28},{20,... | collective-permute-start | bytes 49160 | tf_op jit(solution)/shard_map/ppermute | solution.py:396
  7.3 4.3 %copy-start.3 = (f32[4,64,128]{2,1,0:T(8,128)S(1)}, f32[4,64,128]{2,1,0:T(8,128)}, u32[]{:S(2)}) copy-start(f32[4,64,128]{2,1,0:T(8,128)} %constant.5.clone.tables_hbm.tables) | copy-start | bytes 393220
  7.3 4.3 %copy-start.4 = (f32[512]{0:T(512)S(1)}, f32[512]{0:T(512)}, u32[]{:S(2)}) copy-start(f32[512]{0:T(512)} %param.11) | copy-start | bytes 6148
  11.7 2.7 %collective-permute-start.3 = (bf16[192,640]{1,0:T(8,128)(2,1)S(1)}, bf16[192,640]{1,0:T(8,128)(2,1)S(1)}, u32[]{:S(2)}, u32[]{:S(2)}) collective-permute-start(bf16[192,640]{1,0:T(8,128)(2,1)S(1)} %mid.1.together), channel_id=1, source_target_pairs={{0,1},{1,0},{2,3},{3,2},{4,5},{5,4},{6,7},{7,6},{8,9},{9,8},{10,11... | collective-permute-start | bytes 737288 | tf_op jit(solution)/shard_map/ppermute | solution.py:461

commit v11 on v7

--- a/solution.py
+++ b/solution.py
@@ -205,7 +205,7 @@
         at = pl.ds(k * block, block)
         return pltpu.make_async_copy(out.at[:, at], out_hbm.at[:, at], sent.at[k])
 
-    def run(used):
+    def run(used, high):
         every = together.shape[0]
         both = ((0, sets), (sets, every))
         spans = [span for span, use in zip(both, used, strict=True) if use]
@@ -243,31 +243,32 @@
                 lambda r, piece: swapped[r][piece, width:],
             )
             found = lax.dot_general(
-                full[:, FULL * h : FULL * (h + 1)],
+                full[:high, FULL * h : FULL * (h + 1)],
                 jnp.concatenate([column(h, 0, NOPE), last], 1),
                 (((1,), (1,)), ((), ())),
                 preferred_element_type=jnp.float32,
             )
-            scores[h % buffers, :, :rows] = jnp.where(causal, found[:, :rows], MASKED)
+            scores[h % buffers, :high, :rows] = jnp.where(causal[:high], found[:, :rows], MASKED)
             if total > rows:
-                scores[h % buffers, :, rows:total] = found[:, rows:]
+                scores[h % buffers, :high, rows:total] = found[:, rows:]
 
         def soften(h):
-            found = scores[h % buffers, :, :total]
+            found = scores[h % buffers, :high, :total]
             top = jnp.max(found, 1, keepdims=True)
             raw = jnp.exp2(found * EXPONENT - top * EXPONENT)
-            weights[h % buffers, :, :total] = raw.astype(jnp.bfloat16)
+            weights[h % buffers, :high, :total] = raw.astype(jnp.bfloat16)
             return jnp.sum(raw, 1, keepdims=True)
 
         def mix(h, total_h):
             mixed = jnp.dot(
-                weights[h % buffers, :, :total],
+                weights[h % buffers, :high, :total],
                 column(h, NOPE, columns),
                 preferred_element_type=jnp.float32,
             )
-            out[:, VDIM * h : VDIM * (h + 1)] = jnp.where(live, mixed / total_h, 0.0).astype(
-                jnp.bfloat16
-            )
+            at = slice(VDIM * h, VDIM * (h + 1))
+            out[:high, at] = jnp.where(live[:high], mixed / total_h, 0.0).astype(jnp.bfloat16)
+            if high < rows:
+                out[high:, at] = jnp.zeros((rows - high, VDIM), jnp.bfloat16)
             if (h + 1) % (heads // OUT_COPIES) == 0:
                 leave(h // (heads // OUT_COPIES)).start()
 
@@ -287,11 +288,23 @@
                 if 0 <= t - 2 < steps:
                     mix(h, totals.pop(h))
 
+    left = length[0] - ctx * rows
+
+    @pl.when(left <= 0)
+    def _():
+        out[...] = jnp.zeros_like(out)
+        for k in range(OUT_COPIES):
+            leave(k).start()
+
     for used, places in levels:
-
-        @pl.when(functools.reduce(jnp.logical_or, [ctx == c for c in places]))
-        def _():
-            run(used)
+        here = functools.reduce(jnp.logical_or, [ctx == c for c in places])
+        bounds = [0, rows // 2, rows * 3 // 4, rows] if all(used) else [0, rows]
+        for low, high in zip(bounds[:-1], bounds[1:], strict=True):
+            fits = (left > low) if high == rows else (left > low) & (left <= high)
+
+            @pl.when(here & fits)
+            def _():
+                run(used, high)
 
     for k in range(OUT_COPIES):
         leave(k).wait()

time: 17.8 us -> 17.4 us (0.978)
  the two profiles are of different devices: /device:TPU:25 before, /device:TPU:21 now
where the time goes in v11:
time: 17.4 us; the launch traced here: 17.2 us
  starting transfers between devices  6.96 us (40%)
  Pallas kernels  6.62 us (38%)
  waiting for transfers between devices  2.65 us (15%)
  between operations  0.95 us (5%)
    ppermute x3, starting transfers between devices, send(): return lax.ppermute(data, cores, pairs)  5.91 us
    pallas_call x1, Pallas kernels, per_device(): pl.pallas_call(functools.partial(attend_kernel, heads, whole, levels), in...  3.12 us
    ppermute x3, waiting for transfers between devices, send(): return lax.ppermute(data, cores, pairs)  2.52 us
    pallas_call x1, Pallas kernels, per_device(): pl.pallas_call(pack_kernel, in_specs=[HBM] * 4, out_specs=[VMEM] * 2, out...  1.25 us
    pallas_call x1, Pallas kernels, per_device(): pl.pallas_call(functools.partial(own_kernel, heads), in_specs=[VMEM] * 3...  1.11 us
    ppermute x1, starting transfers between devices, per_device(): swapped.append(lax.ppermute(together, 'sub', pairs))  1.05 us
    pallas_call x1, Pallas kernels, per_device(): pl.pallas_call(functools.partial(grow_kernel, 4 * (NOPE + VDIM)), in_spec...  1 us
  transfers between devices with their start and end apart: 4, of which 2 were waited for; matrix products, arithmetic and copies ran while one was open for 0% of the time, Pallas kernels for 19%

profile of v11, /device:TPU:21, one launch (start us, length us, event | category | flops | bytes accessed | tf_op | source)
XLA Modules:
  0.0 17.2 jit_solution(18081199390005351765)
XLA Ops:
  0.0 1.3 %collective-permute-start = (bf16[128,512]{1,0:T(8,128)(2,1)}, bf16[128,512]{1,0:T(8,128)(2,1)S(1)}, u32[]{:S(2)}, u32[]{:S(2)}) collective-permute-start(bf16[128,512]{1,0:T(8,128)(2,1)} %latent_hbm.1), channel_id=1, source_target_pairs={{0,12},{4,8},{1,9},{5,13},{2,14},{6,10},{3,11},{7,15},{16,28},{20,... | collective-permute-start | bytes 393224 | tf_op jit(solution)/shard_map/ppermute | solution.py:357
  1.3 0.0 copy-start.5
  1.3 0.0 copy-start
  1.3 0.0 copy-start.1
  1.3 0.0 copy-start.2
  1.3 1.2 %pack.1 = (bf16[128,640]{1,0:T(8,128)(2,1)S(1)}, bf16[64,640]{1,0:T(8,128)(2,1)S(1)}) custom-call(bf16[128,512]{1,0:T(8,128)(2,1)} %latent_hbm.1, bf16[64,128]{1,0:T(8,128)(2,1)} %bitcast.4, f32[1,512]{1,0:T(1,128)} %bitcast.2, f32[4,64,128]{2,1,0:T(8,128)} %constant.5.clone.tables_hbm.tables), custom_call_target="tpu_custom_call" | custom-call | flops 4000000000 | bytes 524288 | tf_op jit(solution)/shard_map/pack/pallas_call | solution.py:362
  2.6 0.0 copy-start.3
  2.6 0.0 copy-start.4
  2.6 3.3 %collective-permute-start.2 = (bf16[64,640]{1,0:T(8,128)(2,1)S(1)}, bf16[64,640]{1,0:T(8,128)(2,1)S(1)}, u32[]{:S(2)}, u32[]{:S(2)}) collective-permute-start(bf16[64,640]{1,0:T(8,128)(2,1)S(1)} %get-tuple-element.16), channel_id=1, source_target_pairs={{0,4},{8,12},{1,5},{9,13},{2,6},{10,14},{3,7},{11,15},{16,20},{24,... | collective-permute-start | bytes 245768 | tf_op jit(solution)/shard_map/ppermute | solution.py:357
  6.0 0.0 copy-done.5
  6.0 1.3 %collective-permute-start.1 = (bf16[64,128]{1,0:T(8,128)(2,1)S(1)}, bf16[64,128]{1,0:T(8,128)(2,1)S(1)}, u32[]{:S(2)}, u32[]{:S(2)}) collective-permute-start(bf16[64,128]{1,0:T(8,128)(2,1)S(1)} %bitcast.5), channel_id=1, source_target_pairs={{0,12},{4,8},{1,9},{5,13},{2,14},{6,10},{3,11},{7,15},{16,28},{20,... | collective-permute-start | bytes 49160 | tf_op jit(solution)/shard_map/ppermute | solution.py:357
  7.3 0.0 copy-done
  7.3 0.0 copy-done.1
  7.3 0.0 copy-done.2
  7.3 1.1 %own.1 = (bf16[128,4096]{1,0:T(8,128)(2,1)S(1)}, bf16[128,4096]{1,0:T(8,128)(2,1)S(1)}) custom-call(bf16[128,3072]{1,0:T(8,128)(2,1)S(1)} %copy-done.1, bf16[128,640]{1,0:T(8,128)(2,1)S(1)} %get-tuple-element.17.payload.own, bf16[512,4096]{1,0:T(8,128)(2,1)S(1)} %copy-done, f32[4,128,128]{2,1,0:T(8,128)S(1)} %copy-done.2), custom_call_target="tpu_custom_call" | custom-call | flops 536870912 | bytes 7077888 | tf_op jit(solution)/shard_map/own/pallas_call | solution.py:386
  9.1 2.5 %collective-permute-done.1.rest_1_ = bf16[64,128]{1,0:T(8,128)(2,1)S(1)} collective-permute-done((bf16[64,128]{1,0:T(8,128)(2,1)S(1)}, bf16[64,128]{1,0:T(8,128)(2,1)S(1)}, u32[]{:S(2)}, u32[]{:S(2)}) %collective-permute-start.1) | collective-permute-done | bytes 16416 | tf_op jit(solution)/shard_map/ppermute | solution.py:357
  11.6 0.0 collective-permute-done.2.rest_2_
  11.6 0.0 collective-permute-done.rest_0_
  11.6 0.0 copy-done.3
  11.6 0.0 copy-done.4
  11.6 0.1 mid.1.together
  11.7 1.1 %collective-permute-start.3 = (bf16[192,640]{1,0:T(8,128)(2,1)S(1)}, bf16[192,640]{1,0:T(8,128)(2,1)S(1)}, u32[]{:S(2)}, u32[]{:S(2)}) collective-permute-start(bf16[192,640]{1,0:T(8,128)(2,1)S(1)} %mid.1.together), channel_id=1, source_target_pairs={{0,1},{1,0},{2,3},{3,2},{4,5},{5,4},{6,7},{7,6},{8,9},{9,8},{10,11... | collective-permute-start | bytes 737288 | tf_op jit(solution)/shard_map/ppermute | solution.py:422
  12.8 1.0 %grow.1.fetched = bf16[192,4096]{1,0:T(8,128)(2,1)S(1)} custom-call(bf16[192,640]{1,0:T(8,128)(2,1)S(1)} %mid.1.together, bf16[512,4096]{1,0:T(8,128)(2,1)S(1)} %copy-done), custom_call_target="tpu_custom_call" | custom-call | flops 805306368 | bytes 5767168 | tf_op jit(solution)/shard_map/grow/pallas_call | solution.py:424
  13.8 0.1 collective-permute-done.3.rest_0_
  13.9 3.1 %attend.1 = bf16[128,2048]{1,0:T(8,128)(2,1)} custom-call(bf16[128,4096]{1,0:T(8,128)(2,1)S(1)} %get-tuple-element.21.full, bf16[128,640]{1,0:T(8,128)(2,1)S(1)} %get-tuple-element.17.payload.own, bf16[128,4096]{1,0:T(8,128)(2,1)S(1)} %get-tuple-element.22.expanded, bf16[512,4096]{1,0:T(8,128)(2,1)S(1)} %copy-done, bf16[192,640]{1,0:T(8,128)(2,1)S(1)} %mid.1.together, ...), custom_call_target="tpu_custom_call" | custom-call | flops 3221225472 | bytes 7340032 | tf_op jit(solution)/shard_map/attend/pallas_call | solution.py:450
Async XLA Ops:
  0.0 11.6 %collective-permute-start = (bf16[128,512]{1,0:T(8,128)(2,1)}, bf16[128,512]{1,0:T(8,128)(2,1)S(1)}, u32[]{:S(2)}, u32[]{:S(2)}) collective-permute-start(bf16[128,512]{1,0:T(8,128)(2,1)} %latent_hbm.1), channel_id=1, source_target_pairs={{0,12},{4,8},{1,9},{5,13},{2,14},{6,10},{3,11},{7,15},{16,28},{20,... | collective-permute-start | bytes 393224 | tf_op jit(solution)/shard_map/ppermute | solution.py:357
  1.3 4.7 %copy-start.5 = (bf16[128,64]{0,1:T(8,128)(2,1)S(1)}, bf16[128,64]{0,1:T(8,128)(2,1)}, u32[]{:S(2)}) copy-start(bf16[128,64]{0,1:T(8,128)(2,1)} %param.10) | copy-start | bytes 49156
  1.3 6.0 %copy-start = (bf16[512,4096]{1,0:T(8,128)(2,1)S(1)}, bf16[512,4096]{1,0:T(8,128)(2,1)}, u32[]{:S(2)}) copy-start(bf16[512,4096]{1,0:T(8,128)(2,1)} %weight.5) | copy-start | bytes 12582916
  1.3 6.0 %copy-start.1 = (bf16[128,3072]{1,0:T(8,128)(2,1)S(1)}, bf16[128,3072]{1,0:T(8,128)(2,1)}, u32[]{:S(2)}) copy-start(bf16[128,3072]{1,0:T(8,128)(2,1)} %queries.1) | copy-start | bytes 2359300
  1.3 6.0 %copy-start.2 = (f32[4,128,128]{2,1,0:T(8,128)S(1)}, f32[4,128,128]{2,1,0:T(8,128)}, u32[]{:S(2)}) copy-start(f32[4,128,128]{2,1,0:T(8,128)} %constant.4.clone.tables_hbm) | copy-start | bytes 786436
  2.6 9.0 %copy-start.3 = (f32[4,64,128]{2,1,0:T(8,128)S(1)}, f32[4,64,128]{2,1,0:T(8,128)}, u32[]{:S(2)}) copy-start(f32[4,64,128]{2,1,0:T(8,128)} %constant.5.clone.tables_hbm.tables) | copy-start | bytes 393220
  2.6 9.0 %copy-start.4 = (f32[512]{0:T(512)S(1)}, f32[512]{0:T(512)}, u32[]{:S(2)}) copy-start(f32[512]{0:T(512)} %param.11) | copy-start | bytes 6148
  2.6 9.0 %collective-permute-start.2 = (bf16[64,640]{1,0:T(8,128)(2,1)S(1)}, bf16[64,640]{1,0:T(8,128)(2,1)S(1)}, u32[]{:S(2)}, u32[]{:S(2)}) collective-permute-start(bf16[64,640]{1,0:T(8,128)(2,1)S(1)} %get-tuple-element.16), channel_id=1, source_target_pairs={{0,4},{8,12},{1,5},{9,13},{2,6},{10,14},{3,7},{11,15},{16,20},{24,... | collective-permute-start | bytes 245768 | tf_op jit(solution)/shard_map/ppermute | solution.py:357
  6.0 5.6 %collective-permute-start.1 = (bf16[64,128]{1,0:T(8,128)(2,1)S(1)}, bf16[64,128]{1,0:T(8,128)(2,1)S(1)}, u32[]{:S(2)}, u32[]{:S(2)}) collective-permute-start(bf16[64,128]{1,0:T(8,128)(2,1)S(1)} %bitcast.5), channel_id=1, source_target_pairs={{0,12},{4,8},{1,9},{5,13},{2,14},{6,10},{3,11},{7,15},{16,28},{20,... | collective-permute-start | bytes 49160 | tf_op jit(solution)/shard_map/ppermute | solution.py:357
  11.7 2.2 %collective-permute-start.3 = (bf16[192,640]{1,0:T(8,128)(2,1)S(1)}, bf16[192,640]{1,0:T(8,128)(2,1)S(1)}, u32[]{:S(2)}, u32[]{:S(2)}) collective-permute-start(bf16[192,640]{1,0:T(8,128)(2,1)S(1)} %mid.1.together), channel_id=1, source_target_pairs={{0,1},{1,0},{2,3},{3,2},{4,5},{5,4},{6,7},{7,6},{8,9},{9,8},{10,11... | collective-permute-start | bytes 737288 | tf_op jit(solution)/shard_map/ppermute | solution.py:422
